TPU v7x, 512 devices: a whole 4x8x8 slice. The times are simulated.
512 devices in a mesh: tm: 32 (over x, z), frame: 16 (over y, core).
Axes of the slice: x: 4, y: 8, z: 8, core: 2. Of those that a mesh axis runs over, the one named last changes fastest.
Arguments:
- start_state: float32 [16, 32, 32, 128], P('frame'), may hold values from -6 to 6
- initial_guess: float32 [32, 16, 32, 32, 128], P('tm', 'frame'), may hold values from -6 to 6
- noise_draws: float32 [32, 16, 32, 32, 128], P('tm', 'frame'), may hold values from -6 to 6
- timesteps: int32 [32], P('tm'), may hold values from 0 to 999
- gain_space: float32 [128], replicated, may hold values from 0.1 to 1.9
- gain_attention: float32 [128], replicated, may hold values from 0.1 to 1.9
- time_weight: float32 [128, 256], replicated, may hold values from -0.5 to 0.5
- space_weight: bfloat16 [1152, 128], replicated, may hold values from -0.1875 to 0.1875
- attention_weight: bfloat16 [128, 384], replicated, may hold values from -4 to 4
- output_weight: bfloat16 [128, 128], replicated, may hold values from -0.5 to 0.5
Outputs:
- advanced: float32 [32, 16, 32, 32, 128], P('tm', 'frame')
All inputs are finite; a program needn't handle non-finite values.
Results may differ from a plain program's by a relative error of at most 0.0025.
Values may be sent and summed in bfloat16 or wider, within the bound.
No kernel may reach another device: no remote copies, remote signals or barrier semaphores. Data moves between devices by JAX's collectives and lax.ppermute only.
A program may use at most 64 MiB of HBM per device.

v0:
```python
import math

import jax
import jax.numpy as jnp
from jax import lax
from jax.sharding import Mesh
from jax.sharding import PartitionSpec as P

C = 128
HEAD_DIM = 64
ITERS = 2
TM = ("tm_0", "tm_1")


def nothing_yet(shard, identity):
    return jnp.zeros_like(shard) + jnp.asarray(identity, shard.dtype)


def carried_in(shard, axes, combine, identity):
    before = start = nothing_yet(shard, identity)
    subtotal = shard
    for axis in reversed(axes):
        size, position = (lax.axis_size(axis), lax.axis_index(axis))
        pieces = lax.all_gather(subtotal, axis)
        inside, subtotal = (start, start)
        for k in range(size):
            passed = k < position
            subtotal = combine(subtotal, pieces[k])
            inside = jnp.where(passed, subtotal, inside)
        before = combine(inside, before)
    return before


def embed_time(step_value):
    half_width = C // 2
    frequency = jnp.exp(-math.log(10000.0) * jnp.arange(half_width, dtype=jnp.float32) / half_width)
    angles = step_value.astype(jnp.float32) * frequency
    return jnp.concatenate([jnp.cos(angles), jnp.sin(angles)])


def modulation(step_value, time_weight):
    encoded = embed_time(step_value)[None, :]
    shifted = jnp.dot(
        encoded, time_weight, precision=lax.Precision.HIGHEST, preferred_element_type=jnp.float32
    )[0]
    return (1.0 + shifted[:C], shifted[C:])


def normalize(field, gain):
    return field * lax.rsqrt(jnp.mean(field * field, axis=-1, keepdims=True) + 1e-06) * gain


def conv_taps(padded, space_weight):
    frames_here = padded.shape[0]
    rows_here = padded.shape[1] - 2
    cols_here = padded.shape[2] - 2
    shifted = [
        padded[:, row_shift : row_shift + rows_here, col_shift : col_shift + cols_here, :]
        for row_shift in range(3)
        for col_shift in range(3)
    ]
    stacked = jnp.concatenate(shifted, axis=-1).reshape(-1, 9 * padded.shape[3])
    result = jnp.dot(stacked, space_weight, preferred_element_type=jnp.float32)
    return result.reshape(frames_here, rows_here, cols_here, space_weight.shape[1])


def attend(normed_in, attention_weight):
    frames_all, rows_here, cols_here, channels = normed_in.shape
    head_count = channels // HEAD_DIM
    projected = jnp.dot(
        normed_in.reshape(-1, channels), attention_weight, preferred_element_type=jnp.float32
    ).astype(jnp.bfloat16)
    projected = projected.reshape(frames_all, rows_here, cols_here, 3, head_count, HEAD_DIM)
    scores = jnp.einsum(
        "fxyhd,gxyhd->xyhfg",
        projected[:, :, :, 0],
        projected[:, :, :, 1],
        preferred_element_type=jnp.float32,
    ) / math.sqrt(HEAD_DIM)
    weights = jax.nn.softmax(scores, axis=-1).astype(jnp.bfloat16)
    attended = jnp.einsum(
        "xyhfg,gxyhd->fxyhd", weights, projected[:, :, :, 2], preferred_element_type=jnp.float32
    )
    return attended.reshape(frames_all, rows_here, cols_here, channels).astype(jnp.bfloat16)


def add_terms(earlier, later):
    return earlier + later


def prefix_before(term):
    return carried_in(term, TM, add_terms, jnp.zeros_like(term))


def shards(
    start_state,
    initial_guess,
    noise_draws,
    timesteps,
    gain_space,
    gain_attention,
    time_weight,
    space_weight,
    attention_weight,
    output_weight,
):
    step_value = timesteps[0]
    time_value = step_value.astype(jnp.float32) / 1000.0
    coefficient = (0.5 + time_value) / math.sqrt(lax.axis_size(TM))
    scaling, offset = modulation(step_value, time_weight)
    guess_here = initial_guess[0]
    noise_here = noise_draws[0]
    state = guess_here
    term = jnp.zeros_like(guess_here)
    before = jnp.zeros_like(guess_here)
    for picard_turn in range(ITERS):
        evaluate_normed = (normalize(state, gain_space) * scaling + offset).astype(jnp.bfloat16)
        mixed_state = state + jax.nn.silu(
            conv_taps(jnp.pad(evaluate_normed, ((0, 0), (1, 1), (1, 1), (0, 0))), space_weight)
        )
        attended = attend(
            lax.all_to_all(
                normalize(mixed_state, gain_attention).astype(jnp.bfloat16),
                "frame",
                split_axis=1,
                concat_axis=0,
                tiled=True,
            ),
            attention_weight,
        )
        evaluate_attended = lax.all_to_all(
            attended, "frame", split_axis=0, concat_axis=1, tiled=True
        )
        projected = jnp.dot(
            evaluate_attended.reshape(-1, evaluate_attended.shape[-1]),
            output_weight,
            preferred_element_type=jnp.float32,
        )
        evaluated = mixed_state + projected.reshape(mixed_state.shape)
        term = coefficient * (evaluated + time_value * noise_here)
        before = prefix_before(term)
        state = start_state + before
    advanced = start_state + (before + term)
    return advanced[None]


def solution(mesh):
    finer = Mesh(mesh.devices.reshape(4, 8, mesh.shape["frame"]), ("tm_0", "tm_1", "frame"))
    placed = (
        P("frame", None, None, None),
        P(TM, "frame", None, None, None),
        P(TM, "frame", None, None, None),
        P(TM),
        P(),
        P(),
        P(),
        P(),
        P(),
        P(),
    )
    return jax.shard_map(
        shards,
        mesh=finer,
        in_specs=placed,
        out_specs=P(TM, "frame", None, None, None),
        check_vma=False,
    )
```

profile of v0, /device:TPU:1, one launch (start us, length us, event | category | flops | bytes accessed | tf_op | source)
XLA Modules:
  0.0 310.9 jit_solution(7780189712590760370)
XLA Ops:
  7.3 1.1 fusion.48
  8.4 1.2 fusion.29
  9.8 1.2 fusion.33
  12.7 0.8 fusion.63
  13.9 21.0 %all_to_all.16 = bf16[1,32,32,128]{3,2,0,1:T(8,128)(2,1)S(1)} all-to-all(bf16[1,32,32,128]{3,2,0,1:T(8,128)(2,1)S(1)} %fusion.44), channel_id=1, replica_groups=mesh['tm_0'=4,'tm_1'=8,'frame'=16] {'frame'}, dimensions={1} | all-to-all | bytes 524288 | tf_op jit(solution)/shard_map/all_to_all | solution.py:122
  34.9 1.2 convolution_convert_fusion.1
  36.2 3.3 %reshape.801 = bf16[16,2,32,3,2,64]{5,4,3,2,1,0:T(2,128)(2,1)S(1)} reshape(bf16[1024,384]{1,0:T(8,128)(2,1)} %convolution_convert_fusion.1) | data formatting | bytes 1572864 | tf_op jit(solution)/shard_map/reshape | solution.py:73
  39.5 2.7 fusion.60
  42.2 3.2 %fusion.61 = (f32[2,32,2,16]{3,2,1,0:T(2,128)S(1)}, f32[2,32,2,16,16]{3,4,2,1,0:T(8,128)}) fusion(bf16[16,2,32,1,2,64]{5,4,3,2,1,0:T(2,128)(2,1)} %get-tuple-element.18, bf16[16,2,32,1,2,64]{5,4,3,2,1,0:T(2,128)(2,1)} %get-tuple-element.17), kind=kOutput, calls=%fused_computation.143 | convolution fusion | flops 4292623 | bytes 663552 | tf_op jit(solution)/shard_map/sub | solution.py:80
  45.5 1.8 fusion.6
  47.2 0.6 copy.34
  47.8 1.0 convert_element_type.80
  48.8 3.4 %all-to-all-start.1 = ((bf16[16,2,32,128]{3,2,1,0:T(8,128)(2,1)}), bf16[16,2,32,128]{3,2,1,0:T(8,128)(2,1)S(1)}, u32[]{:S(2)}, u32[]{:S(2)}) async-start(bf16[16,2,32,128]{3,2,1,0:T(8,128)(2,1)} %convert_element_type.80), calls=%async_computation.1 | async-start | bytes 524288 | tf_op jit(solution)/shard_map/all_to_all | solution.py:131
  52.2 10.9 %all-to-all-done.1 = bf16[16,2,32,128]{3,2,1,0:T(8,128)(2,1)S(1)} async-done(((bf16[16,2,32,128]{3,2,1,0:T(8,128)(2,1)}), bf16[16,2,32,128]{3,2,1,0:T(8,128)(2,1)S(1)}, u32[]{:S(2)}, u32[]{:S(2)}) %all-to-all-start.1) | async-done | bytes 262176 | tf_op jit(solution)/shard_map/all_to_all | solution.py:131
  63.1 1.1 fusion.9
  64.3 57.2 %all-gather.11.cloned.1.call-done = f32[256,32,128]{2,1,0:T(8,128)} async-done(((f32[32,32,128]{2,1,0:T(8,128)}), f32[256,32,128]{2,1,0:T(8,128)}) %all-gather.11.cloned.1.call-update) | async-done | bytes 4194320 | tf_op jit(solution)/shard_map/all_gather | solution.py:24
  121.5 3.4 %fusion.24 = (f32[1,1,32,32,128]{4,3,2,1,0:T(8,128)}, f32[32,32,128]{2,1,0:T(8,128)S(1)}) fusion(f32[256,32,128]{2,1,0:T(8,128)} %all-gather.11.cloned.1.call-done), kind=kLoop, calls=%fused_computation.48 | loop fusion | flops 917504 | bytes 5242880 | tf_op jit(solution)/shard_map/add | solution.py:88
  125.0 34.2 %all-gather.7.cloned.1.call-done = f32[4,1,32,32,128]{4,3,2,1,0:T(8,128)} async-done(((f32[1,1,32,32,128]{4,3,2,1,0:T(8,128)}), f32[4,1,32,32,128]{4,3,2,1,0:T(8,128)}) %all-gather.7.cloned.1.call-update) | async-done | bytes 2097168 | tf_op jit(solution)/shard_map/all_gather | solution.py:24
  159.2 3.0 multiply_reduce_fusion.1
  163.6 0.8 fusion.64
  164.8 19.0 %all_to_all.17 = bf16[1,32,32,128]{3,2,0,1:T(8,128)(2,1)S(1)} all-to-all(bf16[1,32,32,128]{3,2,0,1:T(8,128)(2,1)S(1)} %fusion.45), channel_id=1, replica_groups=mesh['tm_0'=4,'tm_1'=8,'frame'=16] {'frame'}, dimensions={1} | all-to-all | bytes 524288 | tf_op jit(solution)/shard_map/all_to_all | solution.py:122
  184.1 0.8 reshape.805
  185.0 2.5 fusion.59
  187.5 3.0 fusion.62
  190.6 1.8 fusion.7
  192.3 0.6 copy.40
  193.1 14.4 %all_to_all.18 = bf16[16,2,32,128]{3,2,1,0:T(8,128)(2,1)S(1)} all-to-all(bf16[16,2,32,128]{3,2,1,0:T(8,128)(2,1)S(1)} %convert_element_type.87), channel_id=1, replica_groups=mesh['tm_0'=4,'tm_1'=8,'frame'=16] {'frame'}, dimensions={0} | all-to-all | bytes 524288 | tf_op jit(solution)/shard_map/all_to_all | solution.py:131
  207.5 1.0 fusion.12
  208.6 53.7 %all-gather.13.cloned.1.call-done = f32[8,32,32,128]{3,2,1,0:T(8,128)} async-done(((f32[1,32,32,128]{3,2,1,0:T(8,128)}), f32[8,32,32,128]{3,2,1,0:T(8,128)}) %all-gather.13.cloned.1.call-update) | async-done | bytes 4194320 | tf_op jit(solution)/shard_map/all_gather | solution.py:24
  262.4 3.4 %fusion.19 = (f32[1,1,32,32,128]{4,3,2,1,0:T(8,128)}, f32[1,32,32,128]{3,2,1,0:T(8,128)S(1)}) fusion(f32[8,32,32,128]{3,2,1,0:T(8,128)} %all-gather.13.cloned.1.call-done), kind=kLoop, calls=%fused_computation.33 | loop fusion | flops 917504 | bytes 5242880 | tf_op jit(solution)/shard_map/add | solution.py:88
  265.8 34.3 %all-gather.9.cloned.1.call-done = f32[4,1,32,32,128]{4,3,2,1,0:T(8,128)} async-done(((f32[1,1,32,32,128]{4,3,2,1,0:T(8,128)}), f32[4,1,32,32,128]{4,3,2,1,0:T(8,128)}) %all-gather.9.cloned.1.call-update) | async-done | bytes 2097168 | tf_op jit(solution)/shard_map/all_gather | solution.py:24
  300.1 4.2 %fusion.18 = f32[1,1,32,32,128]{4,3,2,1,0:T(8,128)} fusion(f32[1,32,32,128]{3,2,1,0:T(8,128)S(1)} %copy-done.4, f32[1,32,32,128]{3,2,1,0:T(8,128)S(1)} %copy-done.2, f32[4,1,32,32,128]{4,3,2,1,0:T(8,128)} %all-gather.9.cloned.1.call-done, f32[1,1,32,32,128]{4,3,2,1,0:T(8,128)} %get-tuple-element.5, f32[1,32,32,128]{3,2,1,0:T(8,128)S(1)} %get-tuple-element.6, ...), kind=kLoop, calls=%fused_computation.29 | loop fusion | flops 3014656 | bytes 7864332 | tf_op jit(solution)/shard_map/broadcast_in_dim | solution.py:144
  (65 shorter events, 4.7 us)
Async XLA Ops:
  6.5 6.1 %copy-start = (bf16[1152,128]{1,0:T(8,128)(2,1)S(1)}, bf16[1152,128]{1,0:T(8,128)(2,1)}, u32[]{:S(2)}) copy-start(bf16[1152,128]{1,0:T(8,128)(2,1)} %param.17) | copy-start | bytes 884740
  11.0 1.0 copy-start.1
  11.0 1.0 copy-start.10
  12.6 1.1 copy-start.11
  13.4 21.5 %copy-start.7 = (bf16[128,384]{1,0:T(8,128)(2,1)S(1)}, bf16[128,384]{1,0:T(8,128)(2,1)}, u32[]{:S(2)}) copy-start(bf16[128,384]{1,0:T(8,128)(2,1)} %param.18) | copy-start | bytes 294916
  45.4 17.7 %copy-start.5 = (f32[1,1,32,32,128]{4,3,2,1,0:T(8,128)S(1)}, f32[1,1,32,32,128]{4,3,2,1,0:T(8,128)}, u32[]{:S(2)}) copy-start(f32[1,1,32,32,128]{4,3,2,1,0:T(8,128)} %param.12) | copy-start | bytes 1572868
  45.5 17.7 %copy-start.8 = (bf16[128,128]{1,0:T(8,128)(2,1)S(1)}, bf16[128,128]{1,0:T(8,128)(2,1)}, u32[]{:S(2)}) copy-start(bf16[128,128]{1,0:T(8,128)(2,1)} %param.19) | copy-start | bytes 98308
  48.8 14.4 %all-to-all-start.1 = ((bf16[16,2,32,128]{3,2,1,0:T(8,128)(2,1)}), bf16[16,2,32,128]{3,2,1,0:T(8,128)(2,1)S(1)}, u32[]{:S(2)}, u32[]{:S(2)}) async-start(bf16[16,2,32,128]{3,2,1,0:T(8,128)(2,1)} %convert_element_type.80), calls=%async_computation.1 | async-start | bytes 524288 | tf_op jit(solution)/shard_map/all_to_all | solution.py:131
  52.2 69.3 %all-gather.11.cloned.1.call-start = ((), (), s32[]{:S(2)}) async-start(), calls=%async_computation.6 | async-start | bytes 4718592 | tf_op jit(solution)/shard_map/all_gather | solution.py:24
  64.2 95.0 %copy-start.3 = (f32[1,32,32,128]{3,2,1,0:T(8,128)S(1)}, f32[1,32,32,128]{3,2,1,0:T(8,128)}, u32[]{:S(2)}) copy-start(f32[1,32,32,128]{3,2,1,0:T(8,128)} %param.10) | copy-start | bytes 1572868
  64.2 95.0 %all-gather.7.cloned.1.call-start = ((), (), s32[]{:S(2)}) async-start(), calls=%async_computation.4 | async-start | bytes 2621440 | tf_op jit(solution)/shard_map/all_gather | solution.py:24
  124.9 137.5 %all-gather.13.cloned.1.call-start = ((), (), s32[]{:S(2)}) async-start(), calls=%async_computation.7 | async-start | bytes 4718592 | tf_op jit(solution)/shard_map/all_gather | solution.py:24
  190.5 17.0 %copy-start.6 = (f32[1,1,32,32,128]{4,3,2,1,0:T(8,128)S(1)}, f32[1,1,32,32,128]{4,3,2,1,0:T(8,128)}, u32[]{:S(2)}) copy-start(f32[1,1,32,32,128]{4,3,2,1,0:T(8,128)} %param.12) | copy-start | bytes 1572868
  190.5 17.0 %copy-start.9 = (bf16[128,128]{1,0:T(8,128)(2,1)S(1)}, bf16[128,128]{1,0:T(8,128)(2,1)}, u32[]{:S(2)}) copy-start(bf16[128,128]{1,0:T(8,128)(2,1)} %param.19) | copy-start | bytes 98308
  208.6 91.6 %copy-start.2 = (f32[1,32,32,128]{3,2,1,0:T(8,128)S(1)}, f32[1,32,32,128]{3,2,1,0:T(8,128)}, u32[]{:S(2)}) copy-start(f32[1,32,32,128]{3,2,1,0:T(8,128)} %fusion.12) | copy-start | bytes 1572868
  208.6 91.6 %copy-start.4 = (f32[1,32,32,128]{3,2,1,0:T(8,128)S(1)}, f32[1,32,32,128]{3,2,1,0:T(8,128)}, u32[]{:S(2)}) copy-start(f32[1,32,32,128]{3,2,1,0:T(8,128)} %param.10) | copy-start | bytes 1572868
  208.6 91.6 %all-gather.9.cloned.1.call-start = ((), (), s32[]{:S(2)}) async-start(), calls=%async_computation.5 | async-start | bytes 2621440 | tf_op jit(solution)/shard_map/all_gather | solution.py:24
Sparse Core Ops, SparseCore 0:
  64.3 57.0 all-gather.10
  125.0 34.1 all-gather.6
  208.7 53.6 all-gather.12
  265.9 34.1 all-gather.8
where the time goes:
time: 311 us
  waiting for transfers between devices  190 us (61%)
  blocking collectives  54.3 us (17%)
  other arithmetic  18.3 us (6%)
  matrix products  16.1 us (5%)
  between operations  14.3 us (5%)
  local copies, waits for them, and re-layouts  13.9 us (4%)
  starting transfers between devices  3.6 us (1%)
    all_gather x4, waiting for transfers between devices, carried_in(): pieces = lax.all_gather(subtotal, axis)  179 us
    all_to_all x2, blocking collectives, shards(): lax.all_to_all(normalize(mixed_state, gain_attention).astype(jnp.bfloat16...  40 us
    all_to_all x1, blocking collectives, shards(): lax.all_to_all(attended, 'frame', split_axis=0, concat_axis=1, tiled=True)  14.4 us
    all_to_all x1, waiting for transfers between devices, shards(): lax.all_to_all(attended, 'frame', split_axis=0, concat_axis=1, tiled=True)  10.9 us
    add x2, other arithmetic, add_terms(): return earlier + later  6.84 us
    sub x2, matrix products, attend(): weights = jax.nn.softmax(scores, axis=-1).astype(jnp.bfloat16)  6.23 us
  transfers between devices with their start and end apart: 5, of which 5 were waited for; matrix products, arithmetic and copies ran while one was open for 0% of the time, Pallas kernels for 0%

commit v1 on v0

v1 whole, which is shorter than its diff:
```python
import math

import jax
import jax.numpy as jnp
from jax import lax
from jax.experimental import pallas as pl
from jax.experimental.pallas import tpu as pltpu
from jax.sharding import Mesh
from jax.sharding import PartitionSpec as P

C = 128
HEAD_DIM = 64
FRAMES = 16
STEPS = 32
SIDE = 32
CELLS = SIDE * SIDE
TM = ("tm_0", "tm_1")
ALL = ("tm_0", "tm_1", "frame")
F32 = jnp.float32
BF16 = jnp.bfloat16
VMEM = pl.BlockSpec(memory_space=pltpu.VMEM)
SMEM = pl.BlockSpec(memory_space=pltpu.SMEM)


def dot(left, right):
    return jnp.dot(left, right, preferred_element_type=F32)


def unit(field, gain):
    return field * lax.rsqrt(jnp.mean(field * field, axis=-1, keepdims=True) + 1e-06) * gain


def attention_masks():
    row = lax.broadcasted_iota(jnp.int32, (128, 128), 0)
    lane = lax.broadcasted_iota(jnp.int32, (128, 128), 1)
    return row // FRAMES == lane // FRAMES, lane < HEAD_DIM


def attend_block(mixed, gain, attention_weight, output_weight, masks):
    same_cell, first_head = masks
    projected = dot(unit(mixed, gain).astype(BF16), attention_weight).astype(BF16)
    queries, keys, values = (projected[:, i * C : (i + 1) * C] for i in range(3))
    zero = jnp.zeros((), BF16)
    attended = None
    for head in range(2):
        lanes = first_head if head == 0 else jnp.logical_not(first_head)
        scores = lax.dot_general(
            jnp.where(lanes, queries, zero), keys, (((1,), (1,)), ((), ())), preferred_element_type=F32
        ) * (1.0 / math.sqrt(HEAD_DIM))
        scores = jnp.where(same_cell, scores, -1e30)
        grown = jnp.exp(scores - jnp.max(scores, axis=-1, keepdims=True))
        weights = (grown * (1.0 / jnp.sum(grown, axis=-1, keepdims=True))).astype(BF16)
        part = dot(weights, jnp.where(lanes, values, zero))
        attended = part if attended is None else attended + part
    return dot(attended.astype(BF16), output_weight)


def first_kernel(
    scalars, guess, noise, start, gain, scaling, offset, space_weight, out, padded, plain, packed
):
    col = lax.broadcasted_iota(jnp.int32, (8, SIDE, C), 1)
    padded[0] = jnp.zeros((SIDE, 3 * C), BF16)
    padded[SIDE + 1] = jnp.zeros((SIDE, 3 * C), BF16)
    for block in range(4):
        rows = pl.ds(block * 8, 8)
        state = guess[rows]
        normed = unit(state, gain[...]) * scaling[...] + offset[...]
        left = jnp.where(col == 0, 0.0, pltpu.roll(normed, 1, 1))
        right = jnp.where(col == SIDE - 1, 0.0, pltpu.roll(normed, SIDE - 1, 1))
        at = pl.ds(block * 8 + 1, 8)
        padded[at, :, 0:C] = left.astype(BF16)
        padded[at, :, C : 2 * C] = normed.astype(BF16)
        padded[at, :, 2 * C : 3 * C] = right.astype(BF16)
    total = None
    for shift in range(3):
        part = dot(
            padded[shift : shift + SIDE].reshape(CELLS, 3 * C),
            space_weight[shift * 3 * C : (shift + 1) * 3 * C, :],
        )
        total = part if total is None else total + part
    plain[...] = total
    scale = scalars[0]
    last = scalars[1] > 0.5
    for block in range(8):
        rows = pl.ds(block * 128, 128)
        conv = plain[rows, :]
        mixed = guess[pl.ds(block * 4, 4)].reshape(128, C) + conv * jax.nn.sigmoid(conv)
        begun = start[pl.ds(block * 4, 4)].reshape(128, C)
        begun_high = begun.astype(BF16).astype(F32)
        plain[rows, :] = jnp.where(last, begun - begun_high, mixed)
        drawn = noise[pl.ds(block * 4, 4)].reshape(128, C) * scale
        packed[pl.ds(CELLS + block * 128, 128), :] = jnp.where(last, begun_high, drawn)
    for block in range(8):
        half = CELLS // 16
        for slot in range(4):
            if slot < 2:
                piece = plain[pl.ds(block * 128 + slot, half, 2), :]
            else:
                piece = packed[pl.ds(CELLS + block * 128 + slot - 2, half, 2), :]
            packed[pl.ds(2 * CELLS + slot, half, 4), :] = piece
        out[pl.ds(block * 256, 256), :] = packed[pl.ds(2 * CELLS, 256), :].astype(BF16)


def owner_kernel(coefficients, received, gain, attention_weight, output_weight, states, noise_before, wide, drifts):
    masks = attention_masks()
    wide[...] = received[...].astype(F32)
    for cell in range(2):
        for block in range(4):
            mixed = wide[pl.ds(block * 512 + cell, 128, 4), :]
            drifts[pl.ds(cell * 512 + block * 128, 128), :] = mixed + attend_block(
                mixed, gain[...], attention_weight[...], output_weight[...], masks
            )
    for cell in range(2):
        tail = (STEPS - 1) * FRAMES * 4 + cell
        state = wide[pl.ds(tail + 2, FRAMES, 4), :] + wide[pl.ds(tail, FRAMES, 4), :]
        noises = jnp.zeros((FRAMES, C), F32)
        for step in range(STEPS):
            rows = pl.ds(step * 32 + cell * FRAMES, FRAMES)
            states[rows, :] = state.astype(BF16)
            noise_before[rows, :] = noises
            if step < STEPS - 1:
                drawn = wide[pl.ds(step * FRAMES * 4 + 2 + cell, FRAMES, 4), :]
                drift = drifts[pl.ds(cell * 512 + step * FRAMES, FRAMES), :]
                state = state + (coefficients[step] * drift + drawn)
                noises = noises + drawn


def norm_kernel(state, gain, scaling, offset, first, second):
    for cell, out in ((0, first), (1, second)):
        for block in range(4):
            rows = state[pl.ds(block * 8, 8), cell].astype(F32)
            normed = unit(rows, gain[...]) * scaling[...] + offset[...]
            out[pl.ds(block * 8, 8)] = normed.astype(BF16)


def second_kernel(
    scalars, state, left, first, second, right, space_weight, gain, attention_weight, output_weight, out, padded, conv
):
    for col, piece in enumerate((left, first, second, right)):
        padded[col, 0] = jnp.zeros((FRAMES, C), BF16)
        padded[col, SIDE + 1] = jnp.zeros((FRAMES, C), BF16)
        padded[col, 1 : SIDE + 1] = piece[...]
    for cell in range(2):
        taps = [
            padded[cell + across, down : down + SIDE].reshape(SIDE * FRAMES, C)
            for down in range(3)
            for across in range(3)
        ]
        conv[cell] = dot(jnp.concatenate(taps, axis=-1), space_weight[...])
    masks = attention_masks()
    coefficient = scalars[2]
    for cell in range(2):
        for block in range(4):
            found = conv[cell, pl.ds(block * 128, 128), :]
            here = state[pl.ds(block * 8, 8), cell].reshape(128, C).astype(F32)
            mixed = here + found * jax.nn.sigmoid(found)
            drift = mixed + attend_block(
                mixed, gain[...], attention_weight[...], output_weight[...], masks
            )
            out[pl.ds(block * 8, 8), cell] = (coefficient * drift).reshape(8, FRAMES, C).astype(BF16)


def sum_kernel(received, noise_before, out):
    for cell in range(2):
        total = jnp.zeros((FRAMES, C), F32)
        for step in range(STEPS):
            rows = pl.ds(step * 32 + cell * FRAMES, FRAMES)
            total = total + received[rows, :].astype(F32)
            out[pl.ds(step * 32 + cell, FRAMES, 2), :] = total + noise_before[rows, :]


def call(kernel, outs, operands, scratch, scalar_first, flops):
    specs = [SMEM if scalar_first and i == 0 else VMEM for i in range(len(operands))]
    moved = sum(x.size * x.dtype.itemsize for x in (*operands, *outs))
    return pl.pallas_call(
        kernel,
        out_shape=outs,
        in_specs=specs,
        out_specs=[VMEM] * len(outs),
        scratch_shapes=scratch,
        cost_estimate=pl.CostEstimate(flops=flops, bytes_accessed=moved, transcendentals=0),
    )(*operands)


def struct(shape, dtype):
    return jax.ShapeDtypeStruct(shape, dtype)


def embed_time(step_value):
    half_width = C // 2
    frequency = jnp.exp(-math.log(10000.0) * jnp.arange(half_width, dtype=F32) / half_width)
    angles = step_value.astype(F32) * frequency
    return jnp.concatenate([jnp.cos(angles), jnp.sin(angles)])


def modulation(step_value, time_weight):
    encoded = embed_time(step_value)[None, :]
    shifted = jnp.dot(encoded, time_weight, precision=lax.Precision.HIGHEST, preferred_element_type=F32)
    return (1.0 + shifted[:, :C], shifted[:, C:])


def exchange(array, axes):
    return lax.all_to_all(array, axes, 0, 0, tiled=True)


def shards(
    start_state,
    initial_guess,
    noise_draws,
    timesteps,
    gain_space,
    gain_attention,
    time_weight,
    space_weight,
    attention_weight,
    output_weight,
):
    steps_total = lax.axis_size(TM)
    step_value = timesteps[0]
    time_value = step_value.astype(F32) / 1000.0
    coefficient = (0.5 + time_value) / math.sqrt(steps_total)
    scaling, offset = modulation(step_value, time_weight)
    guess, noise, start = initial_guess[0, 0], noise_draws[0, 0], start_state[0]
    gain_s, gain_a = gain_space[None, :], gain_attention[None, :]
    is_last = (lax.axis_index(TM) == steps_total - 1).astype(F32)
    scalars = jnp.stack([coefficient * time_value, is_last, coefficient])

    (sent,) = call(
        first_kernel,
        [struct((2 * CELLS, C), BF16)],
        (scalars, guess, noise, start, gain_s, scaling, offset, space_weight),
        [
            pltpu.VMEM((SIDE + 2, SIDE, 3 * C), BF16),
            pltpu.VMEM((CELLS, C), F32),
            pltpu.VMEM((2 * CELLS + 256, C), F32),
        ],
        True,
        2 * CELLS * 9 * C * C,
    )
    received = exchange(sent.reshape(512, 4, C), ALL).reshape(2 * CELLS, C)
    all_steps = lax.all_gather(timesteps, TM, tiled=True)
    coefficients = (0.5 + all_steps.astype(F32) / 1000.0) / math.sqrt(steps_total)
    states, noise_before = call(
        owner_kernel,
        [struct((CELLS, C), BF16), struct((CELLS, C), F32)],
        (coefficients, received, gain_a, attention_weight, output_weight),
        [pltpu.VMEM((2 * CELLS, C), F32), pltpu.VMEM((CELLS, C), F32)],
        True,
        2 * CELLS * 8 * C * C,
    )
    state = exchange(states.reshape(32, 32, C), TM).reshape(SIDE, 2, FRAMES, C)
    first, second = call(
        norm_kernel,
        [struct((SIDE, FRAMES, C), BF16)] * 2,
        (state, gain_s, scaling, offset),
        [],
        False,
        10 * CELLS * C,
    )
    count = lax.axis_size("frame")
    left = lax.ppermute(second, "frame", [(k, k + 1) for k in range(count - 1)])
    right = lax.ppermute(first, "frame", [(k + 1, k) for k in range(count - 1)])
    (drifts,) = call(
        second_kernel,
        [struct((SIDE, 2, FRAMES, C), BF16)],
        (scalars, state, left, first, second, right, space_weight, gain_a, attention_weight, output_weight),
        [pltpu.VMEM((4, SIDE + 2, FRAMES, C), BF16), pltpu.VMEM((2, CELLS // 2, C), F32)],
        True,
        2 * CELLS * 17 * C * C,
    )
    drifts = exchange(drifts.reshape(32, 32, C), TM).reshape(CELLS, C)
    (sums,) = call(
        sum_kernel, [struct((CELLS, C), F32)], (drifts, noise_before), [], False, 2 * CELLS * C
    )
    sums = exchange(sums.reshape(512, 2, C), ALL).reshape(SIDE, SIDE, C)
    advanced = start + (sums + coefficient * time_value * noise)
    return advanced[None, None]


def solution(mesh):
    finer = Mesh(mesh.devices.reshape(4, 8, mesh.shape["frame"]), ALL)
    placed = (
        P("frame", None, None, None),
        P(TM, "frame", None, None, None),
        P(TM, "frame", None, None, None),
        P(TM),
        P(),
        P(),
        P(),
        P(),
        P(),
        P(),
    )
    return jax.shard_map(
        shards,
        mesh=finer,
        in_specs=placed,
        out_specs=P(TM, "frame", None, None, None),
        check_vma=False,
    )
```

time: 311 us -> 153 us (0.49)
  waiting for transfers between devices: 190 us -> 4.57 us
  blocking collectives: 54.3 us -> 88.3 us
  starting transfers between devices: 3.6 us -> 31.2 us
  Pallas kernels: 0 us -> 21.7 us
  matrix products: 16.1 us -> 0.21 us
  other arithmetic: 18.3 us -> 2.73 us
  between operations: 14.3 us -> 0.75 us
  local copies, waits for them, and re-layouts: 13.9 us -> 3.57 us
    all_gather x4 -> x0, waiting for transfers between devices: 179 us -> none  [carried_in(): pieces = lax.all_gather(subtotal, axis)]
    unnamed x0 -> x1, blocking collectives: none -> 21.9 us
    pallas_call x0 -> x5, Pallas kernels: none -> 21.7 us  [call(): pl.pallas_call(kernel, out_shape=outs, in_specs=specs, out_specs=[VMEM] *...]
    all_to_all x1, starting transfers between devices: 3.43 us -> 22.1 us  [exchange(): return lax.all_to_all(array, axes, 0, 0, tiled=True)]
    all_to_all x3, blocking collectives: 54.3 us -> 66.4 us  [exchange(): return lax.all_to_all(array, axes, 0, 0, tiled=True)]
    all_to_all x1, waiting for transfers between devices: 10.9 us -> 0.01 us  [exchange(): return lax.all_to_all(array, axes, 0, 0, tiled=True)]
    ppermute x0 -> x2, starting transfers between devices: none -> 9.03 us  [the longest x1 7.11 us: shards(): left = lax.ppermute(second, 'frame', [(k, k + 1) for k in range(count - 1)])]
    dot_general x8 -> x0, matrix products: 8.75 us -> none  [the longest x2 3.52 us: attend(): jnp.einsum('xyhfg,gxyhd->fxyhd', weights, projected[:, :, :, 2], preferre...]
  transfers between devices with their start and end apart: 5 -> 3, of which waited for: 5 -> 2; matrix products, arithmetic and copies ran while one was open for 0% -> 2% of each run, Pallas kernels for 0% -> 0%
where the time goes in v1:
time: 153 us
  blocking collectives  88.3 us (58%)
  starting transfers between devices  31.2 us (20%)
  Pallas kernels  21.7 us (14%)
  waiting for transfers between devices  4.57 us (3%)
  local copies, waits for them, and re-layouts  3.57 us (2%)
  other arithmetic  2.73 us (2%)
    all_to_all x3, blocking collectives, exchange(): return lax.all_to_all(array, axes, 0, 0, tiled=True)  66.4 us
    all_to_all x1, starting transfers between devices, exchange(): return lax.all_to_all(array, axes, 0, 0, tiled=True)  22.1 us
    unnamed x1, blocking collectives  21.9 us
    pallas_call x5, Pallas kernels, call(): pl.pallas_call(kernel, out_shape=outs, in_specs=specs, out_specs=[VMEM] *...  21.7 us
    ppermute x1, starting transfers between devices, shards(): left = lax.ppermute(second, 'frame', [(k, k + 1) for k in range(count - 1)])  7.11 us
    ppermute x1, waiting for transfers between devices, shards(): right = lax.ppermute(first, 'frame', [(k + 1, k) for k in range(count - 1)])  4.25 us
    unnamed x15, local copies, waits for them, and re-layouts  3.57 us
  transfers between devices with their start and end apart: 3, of which 2 were waited for; matrix products, arithmetic and copies ran while one was open for 2% of the time, Pallas kernels for 0%

profile of v1, /device:TPU:1, one launch (start us, length us, event | category | flops | bytes accessed | tf_op | source)
XLA Modules:
  0.0 152.9 jit_solution(7121516528160103506)
XLA Ops:
  0.0 0.0 copy-start
  0.8 0.2 copy-done
  0.9 0.2 fusion
  1.1 0.6 fusion.6
  1.7 0.6 pad_maximum_fusion.scalars
  2.4 3.5 %shard_map.100 = bf16[2048,128]{1,0:T(8,128)(2,1)} custom-call(f32[3]{0:T(128)} %pad_maximum_fusion.scalars, f32[32,32,128]{2,1,0:T(8,128)} %bitcast.34, f32[32,32,128]{2,1,0:T(8,128)} %bitcast.27, f32[32,32,128]{2,1,0:T(8,128)} %bitcast.26, f32[1,128]{1,0:T(1,128)} %bitcast.37, f32[1,128]{1,0:T(1,128)} %get-tuple-element.14.scaling, ...), custom_call_target="tpu_custom_call" | custom-call | flops 301989888 | bytes 2393612 | tf_op jit(solution)/shard_map/pallas_call | solution.py:175
  5.8 22.1 %all-to-all-start = ((bf16[512,4,128]{2,1,0:T(4,128)(2,1)}), bf16[512,4,128]{2,1,0:T(4,128)(2,1)S(1)}, u32[]{:S(2)}, u32[]{:S(2)}) async-start(bf16[512,4,128]{2,1,0:T(4,128)(2,1)} %bitcast.29), calls=%async_computation | async-start | bytes 1048576 | tf_op jit(solution)/shard_map/all_to_all | solution.py:203
  28.0 1.3 dynamic-slice
  29.3 0.7 dynamic-update-slice
  29.9 21.9 %all-reduce = s32[32]{0:T(128)S(1)} all-reduce(s32[32]{0:T(128)S(1)} %dynamic-update-slice), channel_id=1, replica_groups=mesh['tm_0'=4,'tm_1'=8,'frame'=16] {'tm_0','tm_1'}, use_global_device_ids=true, to_apply=%add | all-reduce | flops 32 | bytes 256
  51.8 0.5 add_multiply_fusion.coefficients
  52.4 0.0 all-to-all-done
  52.4 0.0 copy-start.3
  52.4 0.8 copy-done.3
  53.2 6.8 %shard_map.101 = (bf16[1024,128]{1,0:T(8,128)(2,1)}, f32[1024,128]{1,0:T(8,128)}) custom-call(f32[32]{0:T(128)} %add_multiply_fusion.coefficients, bf16[2048,128]{1,0:T(8,128)(2,1)} %bitcast.33, f32[1,128]{1,0:T(1,128)} %bitcast.39, bf16[128,384]{1,0:T(8,128)(2,1)} %attention_weight.3, bf16[128,128]{1,0:T(8,128)(2,1)} %output_weight.3), custom_call_target="tpu_custom_call" | custom-call | flops 268435456 | bytes 1442432 | tf_op jit(solution)/shard_map/pallas_call | solution.py:175
  60.0 14.3 %all_to_all.20 = bf16[32,32,128]{2,1,0:T(8,128)(2,1)} all-to-all(bf16[32,32,128]{2,1,0:T(8,128)(2,1)} %bitcast.36), channel_id=1, replica_groups=mesh['tm_0'=4,'tm_1'=8,'frame'=16] {'tm_0','tm_1'}, dimensions={0} | all-to-all | bytes 524288 | tf_op jit(solution)/shard_map/all_to_all | solution.py:203
  74.2 1.8 %shard_map.102 = (bf16[32,16,128]{2,1,0:T(8,128)(2,1)}, bf16[32,16,128]{2,1,0:T(8,128)(2,1)}) custom-call(bf16[32,2,16,128]{3,2,1,0:T(8,128)(2,1)} %bitcast.31, f32[1,128]{1,0:T(1,128)} %bitcast.38, f32[1,128]{1,0:T(1,128)} %get-tuple-element.14.scaling, f32[1,128]{1,0:T(1,128)} %get-tuple-element.13.offset), custom_call_target="tpu_custom_call" | custom-call | flops 1310720 | bytes 525824 | tf_op jit(solution)/shard_map/pallas_call | solution.py:175
  76.1 7.1 %collective-permute-start = (bf16[32,16,128]{2,1,0:T(8,128)(2,1)}, bf16[32,16,128]{2,1,0:T(8,128)(2,1)S(1)}, u32[]{:S(2)}, u32[]{:S(2)}) collective-permute-start(bf16[32,16,128]{2,1,0:T(8,128)(2,1)} %get-tuple-element.10.second), channel_id=1, source_target_pairs={{0,1},{1,2},{2,3},{3,4},{4,5},{5,6},{6,7},{7,8},{8,9},{9,10},{10,1... | collective-permute-start | bytes 393224 | tf_op jit(solution)/shard_map/ppermute | solution.py:261
  83.2 1.9 %collective-permute-start.1 = (bf16[32,16,128]{2,1,0:T(8,128)(2,1)}, bf16[32,16,128]{2,1,0:T(8,128)(2,1)S(1)}, u32[]{:S(2)}, u32[]{:S(2)}) collective-permute-start(bf16[32,16,128]{2,1,0:T(8,128)(2,1)} %get-tuple-element.11.first), channel_id=1, source_target_pairs={{1,0},{2,1},{3,2},{4,3},{5,4},{6,5},{7,6},{8,7},{9,8},{10,9},{11,1... | collective-permute-start | bytes 393224 | tf_op jit(solution)/shard_map/ppermute | solution.py:262
  85.1 0.3 collective-permute-done.left
  85.5 0.0 copy-start.4
  85.5 4.3 %collective-permute-done.1.right = bf16[32,16,128]{2,1,0:T(8,128)(2,1)S(1)} collective-permute-done((bf16[32,16,128]{2,1,0:T(8,128)(2,1)}, bf16[32,16,128]{2,1,0:T(8,128)(2,1)S(1)}, u32[]{:S(2)}, u32[]{:S(2)}) %collective-permute-start.1) | collective-permute-done | bytes 131104 | tf_op jit(solution)/shard_map/ppermute | solution.py:262
  89.7 0.0 copy-done.4
  89.7 0.0 copy-start.5
  89.7 0.7 copy-done.5
  90.4 7.6 %shard_map.103 = bf16[32,2,16,128]{3,2,1,0:T(8,128)(2,1)} custom-call(f32[3]{0:T(128)} %pad_maximum_fusion.scalars, bf16[32,2,16,128]{3,2,1,0:T(8,128)(2,1)} %bitcast.32, bf16[32,16,128]{2,1,0:T(8,128)(2,1)} %copy-done.4, bf16[32,16,128]{2,1,0:T(8,128)(2,1)} %get-tuple-element.11.first, bf16[32,16,128]{2,1,0:T(8,128)(2,1)} %get-tuple-element.10.second, ...), custom_call_target="tpu_custom_call" | custom-call | flops 570425344 | bytes 1475084 | tf_op jit(solution)/shard_map/pallas_call | solution.py:175
  97.9 14.7 %all_to_all.21 = bf16[32,32,128]{2,1,0:T(8,128)(2,1)} all-to-all(bf16[32,32,128]{2,1,0:T(8,128)(2,1)} %bitcast.35), channel_id=1, replica_groups=mesh['tm_0'=4,'tm_1'=8,'frame'=16] {'tm_0','tm_1'}, dimensions={0} | all-to-all | bytes 524288 | tf_op jit(solution)/shard_map/all_to_all | solution.py:203
  112.6 2.0 %shard_map.104 = f32[1024,128]{1,0:T(8,128)} custom-call(bf16[1024,128]{1,0:T(8,128)(2,1)} %bitcast.30, f32[1024,128]{1,0:T(8,128)} %get-tuple-element.12.noise_before), custom_call_target="tpu_custom_call" | custom-call | flops 262144 | bytes 1310720 | tf_op jit(solution)/shard_map/pallas_call | solution.py:175
  114.6 37.4 %all_to_all.22 = f32[512,2,128]{2,1,0:T(2,128)S(1)} all-to-all(f32[512,2,128]{2,1,0:T(2,128)} %bitcast.28), channel_id=1, replica_groups=mesh['tm_0'=4,'tm_1'=8,'frame'=16] {'tm_0','tm_1','frame'}, dimensions={0} | all-to-all | bytes 1048576 | tf_op jit(solution)/shard_map/all_to_all | solution.py:203
  152.0 0.0 copy-done.1
  152.0 0.0 copy-done.2
  152.0 0.9 bitcast_add_fusion
  (4 shorter events, 0.1 us)
Async XLA Ops:
  0.0 0.9 copy-start
  5.8 46.5 %all-to-all-start = ((bf16[512,4,128]{2,1,0:T(4,128)(2,1)}), bf16[512,4,128]{2,1,0:T(4,128)(2,1)S(1)}, u32[]{:S(2)}, u32[]{:S(2)}) async-start(bf16[512,4,128]{2,1,0:T(4,128)(2,1)} %bitcast.29), calls=%async_computation | async-start | bytes 1048576 | tf_op jit(solution)/shard_map/all_to_all | solution.py:203
  52.4 0.8 copy-start.3
  76.1 9.4 %collective-permute-start = (bf16[32,16,128]{2,1,0:T(8,128)(2,1)}, bf16[32,16,128]{2,1,0:T(8,128)(2,1)S(1)}, u32[]{:S(2)}, u32[]{:S(2)}) collective-permute-start(bf16[32,16,128]{2,1,0:T(8,128)(2,1)} %get-tuple-element.10.second), channel_id=1, source_target_pairs={{0,1},{1,2},{2,3},{3,4},{4,5},{5,6},{6,7},{7,8},{8,9},{9,10},{10,1... | collective-permute-start | bytes 393224 | tf_op jit(solution)/shard_map/ppermute | solution.py:261
  83.2 6.5 %collective-permute-start.1 = (bf16[32,16,128]{2,1,0:T(8,128)(2,1)}, bf16[32,16,128]{2,1,0:T(8,128)(2,1)S(1)}, u32[]{:S(2)}, u32[]{:S(2)}) collective-permute-start(bf16[32,16,128]{2,1,0:T(8,128)(2,1)} %get-tuple-element.11.first), channel_id=1, source_target_pairs={{1,0},{2,1},{3,2},{4,3},{5,4},{6,5},{7,6},{8,7},{9,8},{10,9},{11,1... | collective-permute-start | bytes 393224 | tf_op jit(solution)/shard_map/ppermute | solution.py:262
  85.5 4.3 %copy-start.4 = (bf16[32,16,128]{2,1,0:T(8,128)(2,1)}, bf16[32,16,128]{2,1,0:T(8,128)(2,1)S(1)}, u32[]{:S(2)}) copy-start(bf16[32,16,128]{2,1,0:T(8,128)(2,1)S(1)} %collective-permute-done.left) | copy-start | bytes 393220
  89.7 0.7 copy-start.5
  114.6 37.4 %copy-start.1 = (f32[1,32,32,128]{3,2,1,0:T(8,128)S(1)}, f32[1,32,32,128]{3,2,1,0:T(8,128)}, u32[]{:S(2)}) copy-start(f32[1,32,32,128]{3,2,1,0:T(8,128)} %param.10) | copy-start | bytes 1572868
  114.6 37.4 %copy-start.2 = (f32[1,1,32,32,128]{4,3,2,1,0:T(8,128)S(1)}, f32[1,1,32,32,128]{4,3,2,1,0:T(8,128)}, u32[]{:S(2)}) copy-start(f32[1,1,32,32,128]{4,3,2,1,0:T(8,128)} %param.12) | copy-start | bytes 1572868

commit v2 on v1

--- a/solution.py
+++ b/solution.py
@@ -121,7 +121,7 @@
             if step < STEPS - 1:
                 drawn = wide[pl.ds(step * FRAMES * 4 + 2 + cell, FRAMES, 4), :]
                 drift = drifts[pl.ds(cell * 512 + step * FRAMES, FRAMES), :]
-                state = state + (coefficients[step] * drift + drawn)
+                state = state + (coefficients[step : step + 1, :] * drift + drawn)
                 noises = noises + drawn
 
 
@@ -178,6 +178,7 @@
         in_specs=specs,
         out_specs=[VMEM] * len(outs),
         scratch_shapes=scratch,
+        compiler_params=pltpu.CompilerParams(vmem_limit_bytes=16 << 20),
         cost_estimate=pl.CostEstimate(flops=flops, bytes_accessed=moved, transcendentals=0),
     )(*operands)
 
@@ -238,14 +239,13 @@
         2 * CELLS * 9 * C * C,
     )
     received = exchange(sent.reshape(512, 4, C), ALL).reshape(2 * CELLS, C)
-    all_steps = lax.all_gather(timesteps, TM, tiled=True)
-    coefficients = (0.5 + all_steps.astype(F32) / 1000.0) / math.sqrt(steps_total)
+    coefficients = exchange(jnp.broadcast_to(coefficient, (steps_total, 1, C)), TM).reshape(steps_total, C)
     states, noise_before = call(
         owner_kernel,
         [struct((CELLS, C), BF16), struct((CELLS, C), F32)],
         (coefficients, received, gain_a, attention_weight, output_weight),
         [pltpu.VMEM((2 * CELLS, C), F32), pltpu.VMEM((CELLS, C), F32)],
-        True,
+        False,
         2 * CELLS * 8 * C * C,
     )
     state = exchange(states.reshape(32, 32, C), TM).reshape(SIDE, 2, FRAMES, C)

time: 153 us -> 149 us (0.974)
  blocking collectives: 88.3 us -> 100 us
  starting transfers between devices: 31.2 us -> 20.8 us
  Pallas kernels: 21.7 us -> 13.2 us
  local copies, waits for them, and re-layouts: 3.57 us -> 6.05 us
  other arithmetic: 2.73 us -> 1.08 us
    all_to_all x3 -> x4, blocking collectives: 66.4 us -> 100 us  [exchange(): return lax.all_to_all(array, axes, 0, 0, tiled=True)]
    unnamed x1 -> x0, blocking collectives: 21.9 us -> none
    pallas_call x5, Pallas kernels: 21.7 us -> 13.2 us  [call(): pl.pallas_call(kernel, out_shape=outs, in_specs=specs, out_specs=[VMEM] *...]
    all_to_all x1, starting transfers between devices: 22.1 us -> 13.7 us  [exchange(): return lax.all_to_all(array, axes, 0, 0, tiled=True)]
    ppermute x1, starting transfers between devices: 7.11 us -> 5.19 us  [shards(): left = lax.ppermute(second, 'frame', [(k, k + 1) for k in range(count - 1)])]
    unnamed x15 -> x24, local copies, waits for them, and re-layouts: 3.57 us -> 5.43 us
    all_to_all x1, waiting for transfers between devices: 0.01 us -> 1.67 us  [exchange(): return lax.all_to_all(array, axes, 0, 0, tiled=True)]
  transfers between devices with their start and end apart: 3 -> 3, of which waited for: 2 -> 2; matrix products, arithmetic and copies ran while one was open for 2% -> 0% of each run, Pallas kernels for 0% -> 1%
where the time goes in v2:
time: 149 us; the launch traced here: 148 us
  blocking collectives  100 us (67%)
  starting transfers between devices  20.8 us (14%)
  Pallas kernels  13.2 us (9%)
  local copies, waits for them, and re-layouts  6.05 us (4%)
  waiting for transfers between devices  6.02 us (4%)
    all_to_all x4, blocking collectives, exchange(): return lax.all_to_all(array, axes, 0, 0, tiled=True)  100 us
    all_to_all x1, starting transfers between devices, exchange(): return lax.all_to_all(array, axes, 0, 0, tiled=True)  13.7 us
    pallas_call x5, Pallas kernels, call(): pl.pallas_call(kernel, out_shape=outs, in_specs=specs, out_specs=[VMEM] *...  13.2 us
    unnamed x24, local copies, waits for them, and re-layouts  5.43 us
    ppermute x1, starting transfers between devices, shards(): left = lax.ppermute(second, 'frame', [(k, k + 1) for k in range(count - 1)])  5.19 us
    ppermute x1, waiting for transfers between devices, shards(): right = lax.ppermute(first, 'frame', [(k + 1, k) for k in range(count - 1)])  4.35 us
  transfers between devices with their start and end apart: 3, of which 2 were waited for; matrix products, arithmetic and copies ran while one was open for 0% of the time, Pallas kernels for 1%

profile of v2, /device:TPU:1, one launch (start us, length us, event | category | flops | bytes accessed | tf_op | source)
XLA Modules:
  0.0 148.5 jit_solution(18067159168807559309)
XLA Ops:
  0.0 0.0 copy-start
  0.7 0.6 broadcast_in_dim.11
  1.3 13.7 %all-to-all-start = ((f32[32,1,128]{2,1,0:T(1,128)}), f32[32,1,128]{2,1,0:T(1,128)S(1)}, u32[]{:S(2)}, u32[]{:S(2)}) async-start(f32[32,1,128]{2,1,0:T(1,128)} %broadcast_in_dim.11), calls=%async_computation | async-start | bytes 32768 | tf_op jit(solution)/shard_map/all_to_all | solution.py:204
  15.1 0.0 copy-done
  15.1 0.2 fusion
  15.3 0.1 pad_maximum_fusion.scalars
  15.4 0.7 copy-done.8
  16.1 1.0 copy-done.1
  17.1 1.0 copy-done.3
  18.2 1.0 copy-done.5
  19.2 1.0 copy-done.6
  20.2 1.8 %shard_map.100 = bf16[2048,128]{1,0:T(8,128)(2,1)S(1)} custom-call(f32[3]{0:T(128)S(1)} %pad_maximum_fusion.scalars, f32[32,32,128]{2,1,0:T(8,128)S(1)} %bitcast.33, f32[32,32,128]{2,1,0:T(8,128)S(1)} %bitcast.26, f32[32,32,128]{2,1,0:T(8,128)S(1)} %bitcast.25, f32[1,128]{1,0:T(1,128)S(1)} %bitcast.37, f32[1,128]{1,0:T(1,128)S(1)} %get-tuple-element.14.scaling, ...), custom_call_target="tpu_custom_call" | custom-call | flops 301989888 | bytes 2393612 | tf_op jit(solution)/shard_map/pallas_call | solution.py:175
  21.9 1.7 %all-to-all-done = f32[32,1,128]{2,1,0:T(1,128)S(1)} async-done(((f32[32,1,128]{2,1,0:T(1,128)}), f32[32,1,128]{2,1,0:T(1,128)S(1)}, u32[]{:S(2)}, u32[]{:S(2)}) %all-to-all-start) | async-done | bytes 16416 | tf_op jit(solution)/shard_map/all_to_all | solution.py:204
  23.6 38.3 %all_to_all.25 = bf16[512,4,128]{2,1,0:T(4,128)(2,1)S(1)} all-to-all(bf16[512,4,128]{2,1,0:T(4,128)(2,1)S(1)} %bitcast.28), channel_id=1, replica_groups=mesh['tm_0'=4,'tm_1'=8,'frame'=16] {'tm_0','tm_1','frame'}, dimensions={0} | all-to-all | bytes 1048576 | tf_op jit(solution)/shard_map/all_to_all | solution.py:204
  61.9 0.0 copy-done.9
  62.0 0.6 copy-done.11
  62.6 5.0 %shard_map.101 = (bf16[1024,128]{1,0:T(8,128)(2,1)S(1)}, f32[1024,128]{1,0:T(8,128)S(1)}) custom-call(f32[32,128]{1,0:T(8,128)S(1)} %bitcast.36, bf16[2048,128]{1,0:T(8,128)(2,1)S(1)} %bitcast.32, f32[1,128]{1,0:T(1,128)S(1)} %bitcast.39, bf16[128,384]{1,0:T(8,128)(2,1)S(1)} %copy-done.9, bf16[128,128]{1,0:T(8,128)(2,1)S(1)} %copy-done.10), custom_call_target="tpu_custom_call" | custom-call | flops 268435456 | bytes 1458688 | tf_op jit(solution)/shard_map/pallas_call | solution.py:175
  67.6 0.0 copy-start.7
  67.6 15.3 %all_to_all.26 = bf16[32,32,128]{2,1,0:T(8,128)(2,1)S(1)} all-to-all(bf16[32,32,128]{2,1,0:T(8,128)(2,1)S(1)} %bitcast.35), channel_id=1, replica_groups=mesh['tm_0'=4,'tm_1'=8,'frame'=16] {'tm_0','tm_1'}, dimensions={0} | all-to-all | bytes 524288 | tf_op jit(solution)/shard_map/all_to_all | solution.py:204
  83.0 0.2 shard_map.102
  83.2 5.2 %collective-permute-start = (bf16[32,16,128]{2,1,0:T(8,128)(2,1)S(1)}, bf16[32,16,128]{2,1,0:T(8,128)(2,1)S(1)}, u32[]{:S(2)}, u32[]{:S(2)}) collective-permute-start(bf16[32,16,128]{2,1,0:T(8,128)(2,1)S(1)} %get-tuple-element.10.second), channel_id=1, source_target_pairs={{0,1},{1,2},{2,3},{3,4},{4,5},{5,6},{6,7},{7,8},{8,9},{9,10},{10,1... | collective-permute-start | bytes 393224 | tf_op jit(solution)/shard_map/ppermute | solution.py:261
  88.4 1.9 %collective-permute-start.1 = (bf16[32,16,128]{2,1,0:T(8,128)(2,1)S(1)}, bf16[32,16,128]{2,1,0:T(8,128)(2,1)S(1)}, u32[]{:S(2)}, u32[]{:S(2)}) collective-permute-start(bf16[32,16,128]{2,1,0:T(8,128)(2,1)S(1)} %get-tuple-element.11.first), channel_id=1, source_target_pairs={{1,0},{2,1},{3,2},{4,3},{5,4},{6,5},{7,6},{8,7},{9,8},{10,9},{11,1... | collective-permute-start | bytes 393224 | tf_op jit(solution)/shard_map/ppermute | solution.py:262
  90.3 0.0 collective-permute-done.left
  90.3 4.3 %collective-permute-done.1.right = bf16[32,16,128]{2,1,0:T(8,128)(2,1)S(1)} collective-permute-done((bf16[32,16,128]{2,1,0:T(8,128)(2,1)S(1)}, bf16[32,16,128]{2,1,0:T(8,128)(2,1)S(1)}, u32[]{:S(2)}, u32[]{:S(2)}) %collective-permute-start.1) | collective-permute-done | bytes 131104 | tf_op jit(solution)/shard_map/ppermute | solution.py:262
  94.7 0.0 copy-done.7
  94.7 6.1 %shard_map.103 = bf16[32,2,16,128]{3,2,1,0:T(8,128)(2,1)S(1)} custom-call(f32[3]{0:T(128)S(1)} %pad_maximum_fusion.scalars, bf16[32,2,16,128]{3,2,1,0:T(8,128)(2,1)S(1)} %bitcast.31, bf16[32,16,128]{2,1,0:T(8,128)(2,1)S(1)} %collective-permute-done.left, bf16[32,16,128]{2,1,0:T(8,128)(2,1)S(1)} %get-tuple-element.11.first, ...), custom_call_target="tpu_custom_call" | custom-call | flops 570425344 | bytes 1475084 | tf_op jit(solution)/shard_map/pallas_call | solution.py:175
  100.8 14.5 %all_to_all.27 = bf16[32,32,128]{2,1,0:T(8,128)(2,1)S(1)} all-to-all(bf16[32,32,128]{2,1,0:T(8,128)(2,1)S(1)} %bitcast.34), channel_id=1, replica_groups=mesh['tm_0'=4,'tm_1'=8,'frame'=16] {'tm_0','tm_1'}, dimensions={0} | all-to-all | bytes 524288 | tf_op jit(solution)/shard_map/all_to_all | solution.py:204
  115.3 0.1 shard_map.104
  115.4 0.0 copy-start.2
  115.4 0.0 copy-start.4
  115.4 32.1 %all_to_all.28 = f32[512,2,128]{2,1,0:T(2,128)S(1)} all-to-all(f32[512,2,128]{2,1,0:T(2,128)S(1)} %bitcast.27), channel_id=1, replica_groups=mesh['tm_0'=4,'tm_1'=8,'frame'=16] {'tm_0','tm_1','frame'}, dimensions={0} | all-to-all | bytes 1048576 | tf_op jit(solution)/shard_map/all_to_all | solution.py:204
  147.5 0.9 bitcast_add_fusion
  (13 shorter events, 0.1 us)
Async XLA Ops:
  0.0 15.1 %copy-start = (f32[128,256]{1,0:T(8,128)S(1)}, f32[128,256]{1,0:T(8,128)}, u32[]{:S(2)}) copy-start(f32[128,256]{1,0:T(8,128)} %param.16) | copy-start | bytes 393220
  1.3 22.3 %all-to-all-start = ((f32[32,1,128]{2,1,0:T(1,128)}), f32[32,1,128]{2,1,0:T(1,128)S(1)}, u32[]{:S(2)}, u32[]{:S(2)}) async-start(f32[32,1,128]{2,1,0:T(1,128)} %broadcast_in_dim.11), calls=%async_computation | async-start | bytes 32768 | tf_op jit(solution)/shard_map/all_to_all | solution.py:204
  15.4 0.7 copy-start.8
  16.1 1.0 copy-start.1
  17.1 1.0 copy-start.3
  18.2 1.0 copy-start.5
  19.2 1.0 copy-start.6
  23.6 38.3 %copy-start.9 = (bf16[128,384]{1,0:T(8,128)(2,1)S(1)}, bf16[128,384]{1,0:T(8,128)(2,1)}, u32[]{:S(2)}) copy-start(bf16[128,384]{1,0:T(8,128)(2,1)} %attention_weight.3) | copy-start | bytes 294916
  23.6 38.3 %copy-start.10 = (bf16[128,128]{1,0:T(8,128)(2,1)S(1)}, bf16[128,128]{1,0:T(8,128)(2,1)}, u32[]{:S(2)}) copy-start(bf16[128,128]{1,0:T(8,128)(2,1)} %output_weight.3) | copy-start | bytes 98308
  61.9 0.7 copy-start.11
  67.6 27.1 %copy-start.7 = (bf16[1152,128]{1,0:T(8,128)(2,1)S(1)}, bf16[1152,128]{1,0:T(8,128)(2,1)}, u32[]{:S(2)}) copy-start(bf16[1152,128]{1,0:T(8,128)(2,1)} %space_weight.3) | copy-start | bytes 884740
  83.2 7.1 %collective-permute-start = (bf16[32,16,128]{2,1,0:T(8,128)(2,1)S(1)}, bf16[32,16,128]{2,1,0:T(8,128)(2,1)S(1)}, u32[]{:S(2)}, u32[]{:S(2)}) collective-permute-start(bf16[32,16,128]{2,1,0:T(8,128)(2,1)S(1)} %get-tuple-element.10.second), channel_id=1, source_target_pairs={{0,1},{1,2},{2,3},{3,4},{4,5},{5,6},{6,7},{7,8},{8,9},{9,10},{10,1... | collective-permute-start | bytes 393224 | tf_op jit(solution)/shard_map/ppermute | solution.py:261
  88.4 6.3 %collective-permute-start.1 = (bf16[32,16,128]{2,1,0:T(8,128)(2,1)S(1)}, bf16[32,16,128]{2,1,0:T(8,128)(2,1)S(1)}, u32[]{:S(2)}, u32[]{:S(2)}) collective-permute-start(bf16[32,16,128]{2,1,0:T(8,128)(2,1)S(1)} %get-tuple-element.11.first), channel_id=1, source_target_pairs={{1,0},{2,1},{3,2},{4,3},{5,4},{6,5},{7,6},{8,7},{9,8},{10,9},{11,1... | collective-permute-start | bytes 393224 | tf_op jit(solution)/shard_map/ppermute | solution.py:262
  115.4 32.1 %copy-start.2 = (f32[1,32,32,128]{3,2,1,0:T(8,128)S(1)}, f32[1,32,32,128]{3,2,1,0:T(8,128)}, u32[]{:S(2)}) copy-start(f32[1,32,32,128]{3,2,1,0:T(8,128)} %param.10) | copy-start | bytes 1572868
  115.4 32.1 %copy-start.4 = (f32[1,1,32,32,128]{4,3,2,1,0:T(8,128)S(1)}, f32[1,1,32,32,128]{4,3,2,1,0:T(8,128)}, u32[]{:S(2)}) copy-start(f32[1,1,32,32,128]{4,3,2,1,0:T(8,128)} %param.12) | copy-start | bytes 1572868

commit v3 on v2

v3 whole, which is shorter than its diff:
```python
import math

import jax
import jax.numpy as jnp
from jax import lax
from jax.experimental import pallas as pl
from jax.experimental.pallas import tpu as pltpu
from jax.sharding import Mesh
from jax.sharding import PartitionSpec as P

C = 128
HEAD_DIM = 64
FRAMES = 16
STEPS = 32
SIDE = 32
CELLS = SIDE * SIDE
TM = ("tm_0", "tm_1")
ALL = ("tm_0", "tm_1", "frame")
F32 = jnp.float32
BF16 = jnp.bfloat16
VMEM = pl.BlockSpec(memory_space=pltpu.VMEM)
SMEM = pl.BlockSpec(memory_space=pltpu.SMEM)
FAR = pl.BlockSpec(memory_space=pltpu.HBM)


def dot(left, right):
    return jnp.dot(left, right, preferred_element_type=F32)


def unit(field, gain):
    return field * lax.rsqrt(jnp.mean(field * field, axis=-1, keepdims=True) + 1e-06) * gain


def attention_masks(cell_major):
    row = lax.broadcasted_iota(jnp.int32, (128, 128), 0)
    lane = lax.broadcasted_iota(jnp.int32, (128, 128), 1)
    same_cell = row // FRAMES == lane // FRAMES if cell_major else row % 8 == lane % 8
    return same_cell, lane < HEAD_DIM


def attend_block(mixed, gain, attention_weight, output_weight, masks):
    same_cell, first_head = masks
    projected = dot(unit(mixed, gain).astype(BF16), attention_weight).astype(BF16)
    queries, keys, values = (projected[:, i * C : (i + 1) * C] for i in range(3))
    zero = jnp.zeros((), BF16)
    attended = None
    for head in range(2):
        lanes = first_head if head == 0 else jnp.logical_not(first_head)
        scores = lax.dot_general(
            jnp.where(lanes, queries, zero), keys, (((1,), (1,)), ((), ())), preferred_element_type=F32
        ) * (1.0 / math.sqrt(HEAD_DIM))
        scores = jnp.where(same_cell, scores, -1e30)
        grown = jnp.exp(scores - jnp.max(scores, axis=-1, keepdims=True))
        weights = (grown * (1.0 / jnp.sum(grown, axis=-1, keepdims=True))).astype(BF16)
        part = dot(weights, jnp.where(lanes, values, zero))
        attended = part if attended is None else attended + part
    return dot(attended.astype(BF16), output_weight)


def first_kernel(
    scalars, guess_far, noise_far, start_far, weight_far, gain, scaling, offset, out,
    guess, noise, start, space_weight, padded, mixed, drawn, sems,
):
    copies = [
        pltpu.make_async_copy(far, near, sems.at[i])
        for i, (far, near) in enumerate(
            ((guess_far, guess), (weight_far, space_weight), (noise_far, noise), (start_far, start))
        )
    ]
    for copy in copies:
        copy.start()
    col = lax.broadcasted_iota(jnp.int32, (8, SIDE, C), 1)
    padded[0] = jnp.zeros((SIDE, 3 * C), BF16)
    padded[SIDE + 1] = jnp.zeros((SIDE, 3 * C), BF16)
    copies[0].wait()
    for block in range(4):
        rows = pl.ds(block * 8, 8)
        state = guess[rows]
        normed = unit(state, gain[...]) * scaling[...] + offset[...]
        left = jnp.where(col == 0, 0.0, pltpu.roll(normed, 1, 1))
        right = jnp.where(col == SIDE - 1, 0.0, pltpu.roll(normed, SIDE - 1, 1))
        at = pl.ds(block * 8 + 1, 8)
        padded[at, :, 0:C] = left.astype(BF16)
        padded[at, :, C : 2 * C] = normed.astype(BF16)
        padded[at, :, 2 * C : 3 * C] = right.astype(BF16)
    copies[1].wait()
    total = None
    for shift in range(3):
        part = dot(
            padded[shift : shift + SIDE].reshape(CELLS, 3 * C),
            space_weight[shift * 3 * C : (shift + 1) * 3 * C, :],
        )
        total = part if total is None else total + part
    mixed[...] = total
    copies[2].wait()
    copies[3].wait()
    scale = scalars[0]
    last = scalars[1] > 0.5
    for block in range(8):
        rows = pl.ds(block * 128, 128)
        band = pl.ds(block * 4, 4)
        conv = mixed[rows, :]
        here = guess[band].reshape(128, C) + conv * jax.nn.sigmoid(conv)
        begun = start[band].reshape(128, C)
        begun_high = begun.astype(BF16).astype(F32)
        mixed[rows, :] = jnp.where(last, begun - begun_high, here)
        drawn[rows, :] = jnp.where(last, begun_high, noise[band].reshape(128, C) * scale)
    for holder in range(FRAMES):
        for slot, source in enumerate((mixed, drawn)):
            for side in range(2):
                piece = source[pl.ds(2 * holder + side, SIDE, SIDE), :]
                out[holder, pl.ds(slot * 64 + side * SIDE, SIDE), :] = piece.astype(BF16)


def holder_kernel(scalars, received, gain, attention_weight, output_weight, terms, noises, wide, turned, turned_noise):
    masks = attention_masks(False)
    wide[...] = received[...].astype(F32)
    last = scalars[1] > 0.5
    coefficient = scalars[2]
    for side in range(2):
        for block in range(4):
            first = side * SIDE + block * 8
            mixed = wide[:, first : first + 8, :].reshape(128, C)
            drawn = wide[:, 64 + first : 64 + first + 8, :].reshape(128, C)
            drift = mixed + attend_block(
                mixed, gain[...], attention_weight[...], output_weight[...], masks
            )
            turned[...] = jnp.where(last, mixed + drawn, coefficient * drift + drawn)
            turned_noise[...] = jnp.where(last, 0.0, drawn)
            for j in range(8):
                rows = pl.ds(((block * 8 + j) * 2 + side) * FRAMES, FRAMES)
                terms[rows, :] = turned[pl.ds(j, FRAMES, 8), :]
                noises[rows, :] = turned_noise[pl.ds(j, FRAMES, 8), :]


def before_kernel(received, states):
    for half in range(2):
        state = received[pl.ds((STEPS - 1) * 32 + half * 16, 16), :]
        for step in range(STEPS):
            rows = pl.ds(step * 32 + half * 16, 16)
            states[rows, :] = state.astype(BF16)
            state = state + received[rows, :]


def norm_kernel(state, gain, scaling, offset, first, second):
    for cell, out in ((0, first), (1, second)):
        for block in range(4):
            rows = state[pl.ds(block * 8, 8), cell].astype(F32)
            normed = unit(rows, gain[...]) * scaling[...] + offset[...]
            out[pl.ds(block * 8, 8)] = normed.astype(BF16)


def second_kernel(
    scalars, state, left, first, second, right, noises, space_weight, gain, attention_weight, output_weight, out, padded, conv
):
    for col, piece in enumerate((left, first, second, right)):
        padded[col, 0] = jnp.zeros((FRAMES, C), BF16)
        padded[col, SIDE + 1] = jnp.zeros((FRAMES, C), BF16)
        padded[col, 1 : SIDE + 1] = piece[...]
    for cell in range(2):
        taps = [
            padded[cell + across, down : down + SIDE].reshape(SIDE * FRAMES, C)
            for down in range(3)
            for across in range(3)
        ]
        conv[cell] = dot(jnp.concatenate(taps, axis=-1), space_weight[...])
    masks = attention_masks(True)
    coefficient = scalars[2]
    for cell in range(2):
        for block in range(4):
            found = conv[cell, pl.ds(block * 128, 128), :]
            here = state[pl.ds(block * 8, 8), cell].reshape(128, C).astype(F32)
            mixed = here + found * jax.nn.sigmoid(found)
            drift = mixed + attend_block(
                mixed, gain[...], attention_weight[...], output_weight[...], masks
            )
            term = coefficient * drift + noises[pl.ds(block * 8, 8), cell].reshape(128, C)
            out[pl.ds(block * 8, 8), cell] = term.reshape(8, FRAMES, C).astype(BF16)


def sum_kernel(received, out):
    for cell in range(2):
        total = jnp.zeros((FRAMES, C), F32)
        for step in range(STEPS):
            rows = pl.ds(step * 32 + cell * FRAMES, FRAMES)
            total = total + received[rows, :].astype(F32)
            out[pl.ds(step * 32 + cell, FRAMES, 2), :] = total


def call(kernel, outs, operands, scratch, flops, spaces=(), grant=16):
    specs = [*spaces, *[VMEM] * (len(operands) - len(spaces))]
    moved = sum(x.size * x.dtype.itemsize for x in (*operands, *outs))
    return pl.pallas_call(
        kernel,
        out_shape=outs,
        in_specs=specs,
        out_specs=[VMEM] * len(outs),
        scratch_shapes=scratch,
        compiler_params=pltpu.CompilerParams(vmem_limit_bytes=grant << 20),
        cost_estimate=pl.CostEstimate(flops=flops, bytes_accessed=moved, transcendentals=0),
    )(*operands)


def struct(shape, dtype):
    return jax.ShapeDtypeStruct(shape, dtype)


def embed_time(step_value):
    half_width = C // 2
    frequency = jnp.exp(-math.log(10000.0) * jnp.arange(half_width, dtype=F32) / half_width)
    angles = step_value.astype(F32) * frequency
    return jnp.concatenate([jnp.cos(angles), jnp.sin(angles)])


def modulation(step_value, time_weight):
    encoded = embed_time(step_value)[None, :]
    shifted = jnp.dot(encoded, time_weight, precision=lax.Precision.HIGHEST, preferred_element_type=F32)
    return (1.0 + shifted[:, :C], shifted[:, C:])


def exchange(array, axes):
    return lax.all_to_all(array, axes, 0, 0, tiled=True)


def shards(
    start_state,
    initial_guess,
    noise_draws,
    timesteps,
    gain_space,
    gain_attention,
    time_weight,
    space_weight,
    attention_weight,
    output_weight,
):
    steps_total = lax.axis_size(TM)
    step_value = timesteps[0]
    time_value = step_value.astype(F32) / 1000.0
    coefficient = (0.5 + time_value) / math.sqrt(steps_total)
    scaling, offset = modulation(step_value, time_weight)
    guess, noise, start = initial_guess[0, 0], noise_draws[0, 0], start_state[0]
    gain_s, gain_a = gain_space[None, :], gain_attention[None, :]
    is_last = (lax.axis_index(TM) == steps_total - 1).astype(F32)
    noise_scale = coefficient * time_value
    scalars = jnp.stack([noise_scale, is_last, coefficient])
    scalars, own_scale = lax.optimization_barrier((scalars, is_last * noise_scale))

    (sent,) = call(
        first_kernel,
        [struct((FRAMES, 128, C), BF16)],
        (scalars, guess, noise, start, space_weight, gain_s, scaling, offset),
        [
            pltpu.VMEM((SIDE, SIDE, C), F32),
            pltpu.VMEM((SIDE, SIDE, C), F32),
            pltpu.VMEM((SIDE, SIDE, C), F32),
            pltpu.VMEM((9 * C, C), BF16),
            pltpu.VMEM((SIDE + 2, SIDE, 3 * C), BF16),
            pltpu.VMEM((CELLS, C), F32),
            pltpu.VMEM((CELLS, C), F32),
            pltpu.SemaphoreType.DMA((4,)),
        ],
        2 * CELLS * 9 * C * C,
        (SMEM, FAR, FAR, FAR, FAR),
        62,
    )
    terms, noises = call(
        holder_kernel,
        [struct((CELLS, C), F32), struct((CELLS, C), F32)],
        (scalars, exchange(sent, "frame"), gain_a, attention_weight, output_weight),
        [pltpu.VMEM((FRAMES, 128, C), F32), pltpu.VMEM((128, C), F32), pltpu.VMEM((128, C), F32)],
        2 * CELLS * 8 * C * C,
        (SMEM,),
    )
    terms = exchange(terms.reshape(32, 32, C), TM).reshape(CELLS, C)
    (states,) = call(before_kernel, [struct((CELLS, C), BF16)], (terms,), [], 2 * CELLS * C)
    state = exchange(states.reshape(32, 32, C), TM).reshape(SIDE, 2, FRAMES, C)
    first, second = call(
        norm_kernel,
        [struct((SIDE, FRAMES, C), BF16)] * 2,
        (state, gain_s, scaling, offset),
        [],
        10 * CELLS * C,
    )
    count = lax.axis_size("frame")
    left = lax.ppermute(second, "frame", [(k, k + 1) for k in range(count - 1)])
    right = lax.ppermute(first, "frame", [(k + 1, k) for k in range(count - 1)])
    noises = noises.reshape(SIDE, 2, FRAMES, C)
    (terms,) = call(
        second_kernel,
        [struct((SIDE, 2, FRAMES, C), BF16)],
        (scalars, state, left, first, second, right, noises, space_weight, gain_a, attention_weight, output_weight),
        [pltpu.VMEM((4, SIDE + 2, FRAMES, C), BF16), pltpu.VMEM((2, CELLS // 2, C), F32)],
        2 * CELLS * 17 * C * C,
        (SMEM,),
    )
    terms = exchange(terms.reshape(32, 32, C), TM).reshape(CELLS, C)
    (sums,) = call(sum_kernel, [struct((CELLS, C), F32)], (terms,), [], 2 * CELLS * C)
    sums = exchange(sums.reshape(512, 2, C), ALL).reshape(SIDE, SIDE, C)
    advanced = start + (sums + own_scale * noise)
    return advanced[None, None]


def solution(mesh):
    finer = Mesh(mesh.devices.reshape(4, 8, mesh.shape["frame"]), ALL)
    placed = (
        P("frame", None, None, None),
        P(TM, "frame", None, None, None),
        P(TM, "frame", None, None, None),
        P(TM),
        P(),
        P(),
        P(),
        P(),
        P(),
        P(),
    )
    return jax.shard_map(
        shards,
        mesh=finer,
        in_specs=placed,
        out_specs=P(TM, "frame", None, None, None),
        check_vma=False,
    )
```

time: 149 us -> 151 us (1.013)
  blocking collectives: 100 us -> 118 us
  starting transfers between devices: 20.8 us -> 6.92 us
  local copies, waits for them, and re-layouts: 6.05 us -> 1.37 us
  Pallas kernels: 13.2 us -> 16.6 us
  waiting for transfers between devices: 6.02 us -> 3.75 us
    all_to_all x4 -> x5, blocking collectives: 100 us -> 118 us  [exchange(): return lax.all_to_all(array, axes, 0, 0, tiled=True)]
    all_to_all x1 -> x0, starting transfers between devices: 13.7 us -> none  [exchange(): return lax.all_to_all(array, axes, 0, 0, tiled=True)]
    unnamed x24 -> x22, local copies, waits for them, and re-layouts: 5.43 us -> 1.37 us
    pallas_call x5 -> x6, Pallas kernels: 13.2 us -> 16.6 us  [call(): pl.pallas_call(kernel, out_shape=outs, in_specs=specs, out_specs=[VMEM] *...]
    all_to_all x1 -> x0, waiting for transfers between devices: 1.67 us -> none  [exchange(): return lax.all_to_all(array, axes, 0, 0, tiled=True)]
  transfers between devices with their start and end apart: 3 -> 2, of which waited for: 2 -> 1; matrix products, arithmetic and copies ran while one was open for 0% -> 0% of each run, Pallas kernels for 1% -> 0%
where the time goes in v3:
time: 151 us; the launch traced here: 150 us
  blocking collectives  118 us (78%)
  Pallas kernels  16.6 us (11%)
  starting transfers between devices  6.92 us (5%)
  waiting for transfers between devices  3.75 us (2%)
  other arithmetic  2.22 us (1%)
    all_to_all x5, blocking collectives, exchange(): return lax.all_to_all(array, axes, 0, 0, tiled=True)  118 us
    pallas_call x6, Pallas kernels, call(): pl.pallas_call(kernel, out_shape=outs, in_specs=specs, out_specs=[VMEM] *...  16.6 us
    ppermute x1, starting transfers between devices, shards(): left = lax.ppermute(second, 'frame', [(k, k + 1) for k in range(count - 1)])  4.4 us
    ppermute x1, waiting for transfers between devices, shards(): right = lax.ppermute(first, 'frame', [(k + 1, k) for k in range(count - 1)])  3.75 us
  transfers between devices with their start and end apart: 2, of which 1 were waited for; matrix products, arithmetic and copies ran while one was open for 0% of the time, Pallas kernels for 0%

profile of v3, /device:TPU:1, one launch (start us, length us, event | category | flops | bytes accessed | tf_op | source)
XLA Modules:
  0.0 150.2 jit_solution(9238984207213180729)
XLA Ops:
  0.0 0.0 copy-start
  0.8 0.6 pad_maximum_fusion.scalars
  1.4 0.0 copy-done
  1.4 0.2 fusion
  1.6 0.6 fusion.6
  2.2 4.5 %shard_map.100 = bf16[16,128,128]{2,1,0:T(8,128)(2,1)} custom-call(f32[3]{0:T(128)} %pad_maximum_fusion.scalars, f32[32,32,128]{2,1,0:T(8,128)} %bitcast.41, f32[32,32,128]{2,1,0:T(8,128)} %bitcast.40, f32[32,32,128]{2,1,0:T(8,128)} %bitcast.39, bf16[1152,128]{1,0:T(8,128)(2,1)} %space_weight.1, f32[1,128]{1,0:T(1,128)} %bitcast.33, ...), custom_call_target="tpu_custom_call" | custom-call | flops 301989888 | bytes 2393612 | tf_op jit(solution)/shard_map/pallas_call | solution.py:193
  6.7 0.0 copy-start.6
  6.8 0.0 copy-start.7
  6.8 27.6 %all_to_all.25.received = bf16[16,128,128]{2,1,0:T(8,128)(2,1)S(1)} all-to-all(bf16[16,128,128]{2,1,0:T(8,128)(2,1)} %shard_map.100), channel_id=1, replica_groups=mesh['tm_0'=4,'tm_1'=8,'frame'=16] {'frame'}, dimensions={0} | all-to-all | bytes 1048576 | tf_op jit(solution)/shard_map/all_to_all | solution.py:222
  34.4 0.0 copy-done.7
  34.4 0.6 copy-done.5
  35.0 0.0 copy-done.8
  35.1 5.6 %shard_map.101 = (f32[1024,128]{1,0:T(8,128)S(1)}, f32[1024,128]{1,0:T(8,128)S(1)}) custom-call(f32[3]{0:T(128)S(1)} %copy-done.5, bf16[16,128,128]{2,1,0:T(8,128)(2,1)S(1)} %all_to_all.25.received, f32[1,128]{1,0:T(1,128)S(1)} %bitcast.35, bf16[128,384]{1,0:T(8,128)(2,1)S(1)} %copy-done.6, bf16[128,128]{1,0:T(8,128)(2,1)S(1)} %copy-done.7), custom_call_target="tpu_custom_call" | custom-call | flops 268435456 | bytes 1704460 | tf_op jit(solution)/shard_map/pallas_call | solution.py:193
  40.7 27.6 %all_to_all.26 = f32[32,32,128]{2,1,0:T(8,128)S(1)} all-to-all(f32[32,32,128]{2,1,0:T(8,128)S(1)} %bitcast.31), channel_id=1, replica_groups=mesh['tm_0'=4,'tm_1'=8,'frame'=16] {'tm_0','tm_1'}, dimensions={0} | all-to-all | bytes 1048576 | tf_op jit(solution)/shard_map/all_to_all | solution.py:222
  68.3 0.0 copy-start.1
  68.3 15.0 %all_to_all.27 = bf16[32,32,128]{2,1,0:T(8,128)(2,1)S(1)} all-to-all(bf16[32,32,128]{2,1,0:T(8,128)(2,1)S(1)} %bitcast.27), channel_id=1, replica_groups=mesh['tm_0'=4,'tm_1'=8,'frame'=16] {'tm_0','tm_1'}, dimensions={0} | all-to-all | bytes 524288 | tf_op jit(solution)/shard_map/all_to_all | solution.py:222
  83.4 0.6 copy-done.2
  83.9 0.1 copy-done.3
  84.0 0.0 copy-done.4
  84.0 0.2 shard_map.103
  84.3 4.4 %collective-permute-start = (bf16[32,16,128]{2,1,0:T(8,128)(2,1)S(1)}, bf16[32,16,128]{2,1,0:T(8,128)(2,1)S(1)}, u32[]{:S(2)}, u32[]{:S(2)}) collective-permute-start(bf16[32,16,128]{2,1,0:T(8,128)(2,1)S(1)} %get-tuple-element.13.second), channel_id=1, source_target_pairs={{0,1},{1,2},{2,3},{3,4},{4,5},{5,6},{6,7},{7,8},{8,9},{9,10},{10,1... | collective-permute-start | bytes 393224 | tf_op jit(solution)/shard_map/ppermute | solution.py:286
  88.7 2.5 %collective-permute-start.1 = (bf16[32,16,128]{2,1,0:T(8,128)(2,1)S(1)}, bf16[32,16,128]{2,1,0:T(8,128)(2,1)S(1)}, u32[]{:S(2)}, u32[]{:S(2)}) collective-permute-start(bf16[32,16,128]{2,1,0:T(8,128)(2,1)S(1)} %get-tuple-element.14.first), channel_id=1, source_target_pairs={{1,0},{2,1},{3,2},{4,3},{5,4},{6,5},{7,6},{8,7},{9,8},{10,9},{11,1... | collective-permute-start | bytes 393224 | tf_op jit(solution)/shard_map/ppermute | solution.py:287
  91.2 0.0 collective-permute-done.left
  91.2 3.7 %collective-permute-done.1.right = bf16[32,16,128]{2,1,0:T(8,128)(2,1)S(1)} collective-permute-done((bf16[32,16,128]{2,1,0:T(8,128)(2,1)S(1)}, bf16[32,16,128]{2,1,0:T(8,128)(2,1)S(1)}, u32[]{:S(2)}, u32[]{:S(2)}) %collective-permute-start.1) | collective-permute-done | bytes 131104 | tf_op jit(solution)/shard_map/ppermute | solution.py:287
  95.0 0.0 copy-done.1
  95.0 6.1 %shard_map.104 = bf16[32,2,16,128]{3,2,1,0:T(8,128)(2,1)S(1)} custom-call(f32[3]{0:T(128)S(1)} %copy-done.5, bf16[32,2,16,128]{3,2,1,0:T(8,128)(2,1)S(1)} %bitcast.30, bf16[32,16,128]{2,1,0:T(8,128)(2,1)S(1)} %collective-permute-done.left, bf16[32,16,128]{2,1,0:T(8,128)(2,1)S(1)} %get-tuple-element.14.first, ...), custom_call_target="tpu_custom_call" | custom-call | flops 570425344 | bytes 1999372 | tf_op jit(solution)/shard_map/pallas_call | solution.py:193
  101.1 14.9 %all_to_all.28 = bf16[32,32,128]{2,1,0:T(8,128)(2,1)S(1)} all-to-all(bf16[32,32,128]{2,1,0:T(8,128)(2,1)S(1)} %bitcast.32), channel_id=1, replica_groups=mesh['tm_0'=4,'tm_1'=8,'frame'=16] {'tm_0','tm_1'}, dimensions={0} | all-to-all | bytes 524288 | tf_op jit(solution)/shard_map/all_to_all | solution.py:222
  116.0 0.0 copy-start.9
  116.0 0.0 copy-start.10
  116.1 33.2 %all_to_all.29 = f32[512,2,128]{2,1,0:T(2,128)S(1)} all-to-all(f32[512,2,128]{2,1,0:T(2,128)S(1)} %bitcast.26), channel_id=1, replica_groups=mesh['tm_0'=4,'tm_1'=8,'frame'=16] {'tm_0','tm_1','frame'}, dimensions={0} | all-to-all | bytes 1048576 | tf_op jit(solution)/shard_map/all_to_all | solution.py:222
  149.3 0.0 copy-done.10
  149.3 0.9 bitcast_add_fusion
  (10 shorter events, 0.1 us)
Async XLA Ops:
  0.0 1.4 copy-start
  6.7 27.7 %copy-start.6 = (bf16[128,384]{1,0:T(8,128)(2,1)S(1)}, bf16[128,384]{1,0:T(8,128)(2,1)}, u32[]{:S(2)}) copy-start(bf16[128,384]{1,0:T(8,128)(2,1)} %attention_weight.3) | copy-start | bytes 294916
  6.8 27.7 %copy-start.7 = (bf16[128,128]{1,0:T(8,128)(2,1)S(1)}, bf16[128,128]{1,0:T(8,128)(2,1)}, u32[]{:S(2)}) copy-start(bf16[128,128]{1,0:T(8,128)(2,1)} %output_weight.3) | copy-start | bytes 98308
  34.4 0.6 copy-start.5
  34.4 0.7 copy-start.8
  68.3 26.6 %copy-start.1 = (bf16[1152,128]{1,0:T(8,128)(2,1)S(1)}, bf16[1152,128]{1,0:T(8,128)(2,1)}, u32[]{:S(2)}) copy-start(bf16[1152,128]{1,0:T(8,128)(2,1)} %space_weight.1) | copy-start | bytes 884740
  83.4 0.6 copy-start.2
  83.4 0.7 copy-start.3
  83.4 0.7 copy-start.4
  84.3 6.9 %collective-permute-start = (bf16[32,16,128]{2,1,0:T(8,128)(2,1)S(1)}, bf16[32,16,128]{2,1,0:T(8,128)(2,1)S(1)}, u32[]{:S(2)}, u32[]{:S(2)}) collective-permute-start(bf16[32,16,128]{2,1,0:T(8,128)(2,1)S(1)} %get-tuple-element.13.second), channel_id=1, source_target_pairs={{0,1},{1,2},{2,3},{3,4},{4,5},{5,6},{6,7},{7,8},{8,9},{9,10},{10,1... | collective-permute-start | bytes 393224 | tf_op jit(solution)/shard_map/ppermute | solution.py:286
  88.7 6.3 %collective-permute-start.1 = (bf16[32,16,128]{2,1,0:T(8,128)(2,1)S(1)}, bf16[32,16,128]{2,1,0:T(8,128)(2,1)S(1)}, u32[]{:S(2)}, u32[]{:S(2)}) collective-permute-start(bf16[32,16,128]{2,1,0:T(8,128)(2,1)S(1)} %get-tuple-element.14.first), channel_id=1, source_target_pairs={{1,0},{2,1},{3,2},{4,3},{5,4},{6,5},{7,6},{8,7},{9,8},{10,9},{11,1... | collective-permute-start | bytes 393224 | tf_op jit(solution)/shard_map/ppermute | solution.py:287
  116.0 33.3 %copy-start.9 = (f32[1,32,32,128]{3,2,1,0:T(8,128)S(1)}, f32[1,32,32,128]{3,2,1,0:T(8,128)}, u32[]{:S(2)}) copy-start(f32[1,32,32,128]{3,2,1,0:T(8,128)} %param.10) | copy-start | bytes 1572868
  116.0 33.2 %copy-start.10 = (f32[1,1,32,32,128]{4,3,2,1,0:T(8,128)S(1)}, f32[1,1,32,32,128]{4,3,2,1,0:T(8,128)}, u32[]{:S(2)}) copy-start(f32[1,1,32,32,128]{4,3,2,1,0:T(8,128)} %param.12) | copy-start | bytes 1572868

commit v4 on v3

--- a/solution.py
+++ b/solution.py
@@ -59,7 +59,7 @@
 
 def first_kernel(
     scalars, guess_far, noise_far, start_far, weight_far, gain, scaling, offset, out,
-    guess, noise, start, space_weight, padded, mixed, drawn, sems,
+    guess, noise, start, space_weight, padded, mixed, drawn, packed, sems,
 ):
     copies = [
         pltpu.make_async_copy(far, near, sems.at[i])
@@ -105,41 +105,33 @@
         begun_high = begun.astype(BF16).astype(F32)
         mixed[rows, :] = jnp.where(last, begun - begun_high, here)
         drawn[rows, :] = jnp.where(last, begun_high, noise[band].reshape(128, C) * scale)
-    for holder in range(FRAMES):
-        for slot, source in enumerate((mixed, drawn)):
-            for side in range(2):
-                piece = source[pl.ds(2 * holder + side, SIDE, SIDE), :]
-                out[holder, pl.ds(slot * 64 + side * SIDE, SIDE), :] = piece.astype(BF16)
-
-
-def holder_kernel(scalars, received, gain, attention_weight, output_weight, terms, noises, wide, turned, turned_noise):
-    masks = attention_masks(False)
+    for block in range(8):
+        half = CELLS // 16
+        for slot, source in enumerate((mixed, mixed, drawn, drawn)):
+            packed[pl.ds(block * 256 + slot, half, 4), :] = source[pl.ds(block * 128 + slot % 2, half, 2), :]
+        rows = pl.ds(block * 256, 256)
+        out[rows, :] = packed[rows, :].astype(BF16)
+
+
+def owner_kernel(all_steps, received, gain, attention_weight, output_weight, states, wide, drifts):
+    masks = attention_masks(True)
     wide[...] = received[...].astype(F32)
-    last = scalars[1] > 0.5
-    coefficient = scalars[2]
-    for side in range(2):
+    for cell in range(2):
         for block in range(4):
-            first = side * SIDE + block * 8
-            mixed = wide[:, first : first + 8, :].reshape(128, C)
-            drawn = wide[:, 64 + first : 64 + first + 8, :].reshape(128, C)
-            drift = mixed + attend_block(
+            mixed = wide[pl.ds(block * 512 + cell, 128, 4), :]
+            drifts[pl.ds(cell * 512 + block * 128, 128), :] = mixed + attend_block(
                 mixed, gain[...], attention_weight[...], output_weight[...], masks
             )
-            turned[...] = jnp.where(last, mixed + drawn, coefficient * drift + drawn)
-            turned_noise[...] = jnp.where(last, 0.0, drawn)
-            for j in range(8):
-                rows = pl.ds(((block * 8 + j) * 2 + side) * FRAMES, FRAMES)
-                terms[rows, :] = turned[pl.ds(j, FRAMES, 8), :]
-                noises[rows, :] = turned_noise[pl.ds(j, FRAMES, 8), :]
-
-
-def before_kernel(received, states):
-    for half in range(2):
-        state = received[pl.ds((STEPS - 1) * 32 + half * 16, 16), :]
+    for cell in range(2):
+        tail = (STEPS - 1) * FRAMES * 4 + cell
+        state = wide[pl.ds(tail + 2, FRAMES, 4), :] + wide[pl.ds(tail, FRAMES, 4), :]
         for step in range(STEPS):
-            rows = pl.ds(step * 32 + half * 16, 16)
-            states[rows, :] = state.astype(BF16)
-            state = state + received[rows, :]
+            states[pl.ds(step * 32 + cell * FRAMES, FRAMES), :] = state.astype(BF16)
+            if step < STEPS - 1:
+                drawn = wide[pl.ds(step * FRAMES * 4 + 2 + cell, FRAMES, 4), :]
+                drift = drifts[pl.ds(cell * 512 + step * FRAMES, FRAMES), :]
+                coefficient = (0.5 + all_steps[step].astype(F32) / 1000.0) / math.sqrt(STEPS)
+                state = state + (coefficient * drift + drawn)
 
 
 def norm_kernel(state, gain, scaling, offset, first, second):
@@ -151,7 +143,7 @@
 
 
 def second_kernel(
-    scalars, state, left, first, second, right, noises, space_weight, gain, attention_weight, output_weight, out, padded, conv
+    scalars, state, left, first, second, right, space_weight, gain, attention_weight, output_weight, out, padded, conv, block_out, turned
 ):
     for col, piece in enumerate((left, first, second, right)):
         padded[col, 0] = jnp.zeros((FRAMES, C), BF16)
@@ -174,17 +166,27 @@
             drift = mixed + attend_block(
                 mixed, gain[...], attention_weight[...], output_weight[...], masks
             )
-            term = coefficient * drift + noises[pl.ds(block * 8, 8), cell].reshape(128, C)
-            out[pl.ds(block * 8, 8), cell] = term.reshape(8, FRAMES, C).astype(BF16)
+            block_out[...] = coefficient * drift
+            for frame in range(FRAMES):
+                turned[frame, pl.ds(cell * SIDE + block * 8, 8), :] = block_out[pl.ds(frame, 8, FRAMES), :]
+    out[...] = turned[...].astype(BF16)
+
+
+def frame_kernel(scalars, received, noise, out, natural):
+    for holder in range(FRAMES):
+        for side in range(2):
+            piece = received[holder, pl.ds(side * SIDE, SIDE), :].astype(F32)
+            natural[pl.ds(2 * holder + side, SIDE, SIDE), :] = piece
+    out[...] = (natural[...] + scalars[0] * noise[...]).astype(BF16)
 
 
 def sum_kernel(received, out):
-    for cell in range(2):
+    for half in range(2):
         total = jnp.zeros((FRAMES, C), F32)
         for step in range(STEPS):
-            rows = pl.ds(step * 32 + cell * FRAMES, FRAMES)
+            rows = pl.ds(step * 32 + half * FRAMES, FRAMES)
             total = total + received[rows, :].astype(F32)
-            out[pl.ds(step * 32 + cell, FRAMES, 2), :] = total
+            out[rows, :] = total
 
 
 def call(kernel, outs, operands, scratch, flops, spaces=(), grant=16):
@@ -242,13 +244,11 @@
     guess, noise, start = initial_guess[0, 0], noise_draws[0, 0], start_state[0]
     gain_s, gain_a = gain_space[None, :], gain_attention[None, :]
     is_last = (lax.axis_index(TM) == steps_total - 1).astype(F32)
-    noise_scale = coefficient * time_value
-    scalars = jnp.stack([noise_scale, is_last, coefficient])
-    scalars, own_scale = lax.optimization_barrier((scalars, is_last * noise_scale))
+    scalars = jnp.stack([coefficient * time_value, is_last, coefficient])
 
     (sent,) = call(
         first_kernel,
-        [struct((FRAMES, 128, C), BF16)],
+        [struct((2 * CELLS, C), BF16)],
         (scalars, guess, noise, start, space_weight, gain_s, scaling, offset),
         [
             pltpu.VMEM((SIDE, SIDE, C), F32),
@@ -258,22 +258,23 @@
             pltpu.VMEM((SIDE + 2, SIDE, 3 * C), BF16),
             pltpu.VMEM((CELLS, C), F32),
             pltpu.VMEM((CELLS, C), F32),
+            pltpu.VMEM((2 * CELLS, C), F32),
             pltpu.SemaphoreType.DMA((4,)),
         ],
         2 * CELLS * 9 * C * C,
         (SMEM, FAR, FAR, FAR, FAR),
         62,
     )
-    terms, noises = call(
-        holder_kernel,
-        [struct((CELLS, C), F32), struct((CELLS, C), F32)],
-        (scalars, exchange(sent, "frame"), gain_a, attention_weight, output_weight),
-        [pltpu.VMEM((FRAMES, 128, C), F32), pltpu.VMEM((128, C), F32), pltpu.VMEM((128, C), F32)],
+    received = exchange(sent.reshape(512, 4, C), ALL).reshape(2 * CELLS, C)
+    all_steps = lax.all_gather(timesteps, TM, tiled=True)
+    (states,) = call(
+        owner_kernel,
+        [struct((CELLS, C), BF16)],
+        (all_steps, received, gain_a, attention_weight, output_weight),
+        [pltpu.VMEM((2 * CELLS, C), F32), pltpu.VMEM((CELLS, C), F32)],
         2 * CELLS * 8 * C * C,
         (SMEM,),
     )
-    terms = exchange(terms.reshape(32, 32, C), TM).reshape(CELLS, C)
-    (states,) = call(before_kernel, [struct((CELLS, C), BF16)], (terms,), [], 2 * CELLS * C)
     state = exchange(states.reshape(32, 32, C), TM).reshape(SIDE, 2, FRAMES, C)
     first, second = call(
         norm_kernel,
@@ -285,20 +286,31 @@
     count = lax.axis_size("frame")
     left = lax.ppermute(second, "frame", [(k, k + 1) for k in range(count - 1)])
     right = lax.ppermute(first, "frame", [(k + 1, k) for k in range(count - 1)])
-    noises = noises.reshape(SIDE, 2, FRAMES, C)
     (terms,) = call(
         second_kernel,
-        [struct((SIDE, 2, FRAMES, C), BF16)],
-        (scalars, state, left, first, second, right, noises, space_weight, gain_a, attention_weight, output_weight),
-        [pltpu.VMEM((4, SIDE + 2, FRAMES, C), BF16), pltpu.VMEM((2, CELLS // 2, C), F32)],
+        [struct((FRAMES, 64, C), BF16)],
+        (scalars, state, left, first, second, right, space_weight, gain_a, attention_weight, output_weight),
+        [
+            pltpu.VMEM((4, SIDE + 2, FRAMES, C), BF16),
+            pltpu.VMEM((2, CELLS // 2, C), F32),
+            pltpu.VMEM((128, C), F32),
+            pltpu.VMEM((FRAMES, 64, C), F32),
+        ],
         2 * CELLS * 17 * C * C,
         (SMEM,),
     )
+    (terms,) = call(
+        frame_kernel,
+        [struct((CELLS, C), BF16)],
+        (scalars, exchange(terms, "frame"), noise.reshape(CELLS, C)),
+        [pltpu.VMEM((CELLS, C), F32)],
+        2 * CELLS * C,
+        (SMEM,),
+    )
     terms = exchange(terms.reshape(32, 32, C), TM).reshape(CELLS, C)
     (sums,) = call(sum_kernel, [struct((CELLS, C), F32)], (terms,), [], 2 * CELLS * C)
-    sums = exchange(sums.reshape(512, 2, C), ALL).reshape(SIDE, SIDE, C)
-    advanced = start + (sums + own_scale * noise)
-    return advanced[None, None]
+    sums = exchange(sums.reshape(32, 32, C), TM).reshape(SIDE, SIDE, C)
+    return (start + sums)[None, None]
 
 
 def solution(mesh):

time: 151 us -> 154 us (1.020); the launches traced: 150 us -> 151 us
  blocking collectives: 118 us -> 91.1 us
  starting transfers between devices: 6.92 us -> 32 us
  local copies, waits for them, and re-layouts: 1.37 us -> 3.65 us
    all_to_all x5 -> x4, blocking collectives: 118 us -> 69.4 us  [exchange(): return lax.all_to_all(array, axes, 0, 0, tiled=True)]
    all_to_all x0 -> x1, starting transfers between devices: none -> 22.2 us  [exchange(): return lax.all_to_all(array, axes, 0, 0, tiled=True)]
    unnamed x0 -> x1, blocking collectives: none -> 21.7 us
    ppermute x1, starting transfers between devices: 4.4 us -> 7.95 us  [shards(): left = lax.ppermute(second, 'frame', [(k, k + 1) for k in range(count - 1)])]
    unnamed x22 -> x25, local copies, waits for them, and re-layouts: 1.37 us -> 3.65 us
  transfers between devices with their start and end apart: 2 -> 3, of which waited for: 1 -> 1; matrix products, arithmetic and copies ran while one was open for 0% -> 1% of each run, Pallas kernels for 0% -> 0%
where the time goes in v4:
time: 154 us; the launch traced here: 151 us
  blocking collectives  91.1 us (59%)
  starting transfers between devices  32 us (21%)
  Pallas kernels  17.2 us (11%)
  waiting for transfers between devices  4.35 us (3%)
  local copies, waits for them, and re-layouts  3.65 us (2%)
  other arithmetic  2.07 us (1%)
    all_to_all x4, blocking collectives, exchange(): return lax.all_to_all(array, axes, 0, 0, tiled=True)  69.4 us
    all_to_all x1, starting transfers between devices, exchange(): return lax.all_to_all(array, axes, 0, 0, tiled=True)  22.2 us
    unnamed x1, blocking collectives  21.7 us
    pallas_call x6, Pallas kernels, call(): pl.pallas_call(kernel, out_shape=outs, in_specs=specs, out_specs=[VMEM] *...  17.2 us
    ppermute x1, starting transfers between devices, shards(): left = lax.ppermute(second, 'frame', [(k, k + 1) for k in range(count - 1)])  7.95 us
    ppermute x1, waiting for transfers between devices, shards(): right = lax.ppermute(first, 'frame', [(k + 1, k) for k in range(count - 1)])  4.35 us
    unnamed x25, local copies, waits for them, and re-layouts  3.65 us
  transfers between devices with their start and end apart: 3, of which 1 were waited for; matrix products, arithmetic and copies ran while one was open for 1% of the time, Pallas kernels for 0%

profile of v4, /device:TPU:1, one launch (start us, length us, event | category | flops | bytes accessed | tf_op | source)
XLA Modules:
  0.0 151.5 jit_solution(11911388532286412086)
XLA Ops:
  0.8 0.2 copy-done
  0.9 0.2 fusion
  1.1 0.6 fusion.6
  1.7 0.6 pad_maximum_fusion.scalars
  2.3 4.1 %shard_map.100 = bf16[2048,128]{1,0:T(8,128)(2,1)} custom-call(f32[3]{0:T(128)} %pad_maximum_fusion.scalars, f32[32,32,128]{2,1,0:T(8,128)} %bitcast.41, f32[32,32,128]{2,1,0:T(8,128)} %bitcast.27, f32[32,32,128]{2,1,0:T(8,128)} %bitcast.39, bf16[1152,128]{1,0:T(8,128)(2,1)} %space_weight.1, f32[1,128]{1,0:T(1,128)} %bitcast.35, ...), custom_call_target="tpu_custom_call" | custom-call | flops 301989888 | bytes 2393612 | tf_op jit(solution)/shard_map/pallas_call | solution.py:195
  6.4 0.0 copy-start.7
  6.4 0.0 copy-start.8
  6.4 22.2 %all-to-all-start = ((bf16[512,4,128]{2,1,0:T(4,128)(2,1)}), bf16[512,4,128]{2,1,0:T(4,128)(2,1)S(1)}, u32[]{:S(2)}, u32[]{:S(2)}) async-start(bf16[512,4,128]{2,1,0:T(4,128)(2,1)} %bitcast.40), calls=%async_computation | async-start | bytes 1048576 | tf_op jit(solution)/shard_map/all_to_all | solution.py:224
  28.6 1.3 dynamic-slice
  29.9 0.8 dynamic-update-slice
  30.7 21.7 %all-reduce.all_steps = s32[32]{0:T(128)S(1)} all-reduce(s32[32]{0:T(128)S(1)} %dynamic-update-slice), channel_id=1, replica_groups=mesh['tm_0'=4,'tm_1'=8,'frame'=16] {'tm_0','tm_1'}, use_global_device_ids=true, to_apply=%add | all-reduce | flops 32 | bytes 256
  52.4 0.0 all-to-all-done
  52.4 0.6 copy-done.9
  53.1 5.6 %shard_map.101 = bf16[1024,128]{1,0:T(8,128)(2,1)S(1)} custom-call(s32[32]{0:T(128)S(1)} %all-reduce.all_steps, bf16[2048,128]{1,0:T(8,128)(2,1)S(1)} %bitcast.33, f32[1,128]{1,0:T(1,128)S(1)} %bitcast.37, bf16[128,384]{1,0:T(8,128)(2,1)S(1)} %copy-done.7, bf16[128,128]{1,0:T(8,128)(2,1)S(1)} %copy-done.8), custom_call_target="tpu_custom_call" | custom-call | flops 268435456 | bytes 918144 | tf_op jit(solution)/shard_map/pallas_call | solution.py:195
  58.6 0.0 copy-start.2
  58.6 12.9 %all_to_all.25 = bf16[32,32,128]{2,1,0:T(8,128)(2,1)S(1)} all-to-all(bf16[32,32,128]{2,1,0:T(8,128)(2,1)S(1)} %bitcast.34), channel_id=1, replica_groups=mesh['tm_0'=4,'tm_1'=8,'frame'=16] {'tm_0','tm_1'}, dimensions={0} | all-to-all | bytes 524288 | tf_op jit(solution)/shard_map/all_to_all | solution.py:224
  71.5 0.7 copy-done.4
  72.2 0.2 shard_map.102
  72.4 0.0 copy-start.3
  72.4 7.9 %collective-permute-start = (bf16[32,16,128]{2,1,0:T(8,128)(2,1)S(1)}, bf16[32,16,128]{2,1,0:T(8,128)(2,1)S(1)}, u32[]{:S(2)}, u32[]{:S(2)}) collective-permute-start(bf16[32,16,128]{2,1,0:T(8,128)(2,1)S(1)} %get-tuple-element.7.second), channel_id=1, source_target_pairs={{0,1},{1,2},{2,3},{3,4},{4,5},{5,6},{6,7},{7,8},{8,9},{9,10},{10,1... | collective-permute-start | bytes 393224 | tf_op jit(solution)/shard_map/ppermute | solution.py:287
  80.4 1.9 %collective-permute-start.1 = (bf16[32,16,128]{2,1,0:T(8,128)(2,1)S(1)}, bf16[32,16,128]{2,1,0:T(8,128)(2,1)S(1)}, u32[]{:S(2)}, u32[]{:S(2)}) collective-permute-start(bf16[32,16,128]{2,1,0:T(8,128)(2,1)S(1)} %get-tuple-element.8.first), channel_id=1, source_target_pairs={{1,0},{2,1},{3,2},{4,3},{5,4},{6,5},{7,6},{8,7},{9,8},{10,9},{11,1... | collective-permute-start | bytes 393224 | tf_op jit(solution)/shard_map/ppermute | solution.py:288
  82.3 0.0 collective-permute-done.left
  82.3 4.3 %collective-permute-done.1.right = bf16[32,16,128]{2,1,0:T(8,128)(2,1)S(1)} collective-permute-done((bf16[32,16,128]{2,1,0:T(8,128)(2,1)S(1)}, bf16[32,16,128]{2,1,0:T(8,128)(2,1)S(1)}, u32[]{:S(2)}, u32[]{:S(2)}) %collective-permute-start.1) | collective-permute-done | bytes 131104 | tf_op jit(solution)/shard_map/ppermute | solution.py:288
  86.7 6.2 %shard_map.103 = bf16[16,64,128]{2,1,0:T(8,128)(2,1)S(1)} custom-call(f32[3]{0:T(128)S(1)} %copy-done.3, bf16[32,2,16,128]{3,2,1,0:T(8,128)(2,1)S(1)} %bitcast.31, bf16[32,16,128]{2,1,0:T(8,128)(2,1)S(1)} %collective-permute-done.left, bf16[32,16,128]{2,1,0:T(8,128)(2,1)S(1)} %get-tuple-element.8.first, bf16[32,16,128]{2,1,0:T(8,128)(2,1)S(1)} %get-tuple-element.7.second, ...), custom_call_target="tpu_custom_call" | custom-call | flops 570425344 | bytes 1475084 | tf_op jit(solution)/shard_map/pallas_call | solution.py:195
  92.9 0.0 copy-start.1
  92.9 21.2 %all_to_all.26.received = bf16[16,64,128]{2,1,0:T(8,128)(2,1)S(1)} all-to-all(bf16[16,64,128]{2,1,0:T(8,128)(2,1)S(1)} %shard_map.103), channel_id=1, replica_groups=mesh['tm_0'=4,'tm_1'=8,'frame'=16] {'frame'}, dimensions={0} | all-to-all | bytes 524288 | tf_op jit(solution)/shard_map/all_to_all | solution.py:224
  114.1 0.0 copy-done.1
  114.1 1.1 shard_map.104
  115.2 14.8 %all_to_all.27 = bf16[32,32,128]{2,1,0:T(8,128)(2,1)S(1)} all-to-all(bf16[32,32,128]{2,1,0:T(8,128)(2,1)S(1)} %bitcast.32), channel_id=1, replica_groups=mesh['tm_0'=4,'tm_1'=8,'frame'=16] {'tm_0','tm_1'}, dimensions={0} | all-to-all | bytes 524288 | tf_op jit(solution)/shard_map/all_to_all | solution.py:224
  130.0 0.0 copy-start.10
  130.0 20.6 %all_to_all.28 = f32[32,32,128]{2,1,0:T(8,128)S(1)} all-to-all(f32[32,32,128]{2,1,0:T(8,128)S(1)} %bitcast.26), channel_id=1, replica_groups=mesh['tm_0'=4,'tm_1'=8,'frame'=16] {'tm_0','tm_1'}, dimensions={0} | all-to-all | bytes 1048576 | tf_op jit(solution)/shard_map/all_to_all | solution.py:224
  150.6 0.9 add_bitcast_fusion
  (15 shorter events, 0.1 us)
Async XLA Ops:
  0.0 0.9 copy-start
  6.4 46.0 %copy-start.7 = (bf16[128,384]{1,0:T(8,128)(2,1)S(1)}, bf16[128,384]{1,0:T(8,128)(2,1)}, u32[]{:S(2)}) copy-start(bf16[128,384]{1,0:T(8,128)(2,1)} %attention_weight.3) | copy-start | bytes 294916
  6.4 46.0 %copy-start.8 = (bf16[128,128]{1,0:T(8,128)(2,1)S(1)}, bf16[128,128]{1,0:T(8,128)(2,1)}, u32[]{:S(2)}) copy-start(bf16[128,128]{1,0:T(8,128)(2,1)} %output_weight.3) | copy-start | bytes 98308
  6.4 46.0 %all-to-all-start = ((bf16[512,4,128]{2,1,0:T(4,128)(2,1)}), bf16[512,4,128]{2,1,0:T(4,128)(2,1)S(1)}, u32[]{:S(2)}, u32[]{:S(2)}) async-start(bf16[512,4,128]{2,1,0:T(4,128)(2,1)} %bitcast.40), calls=%async_computation | async-start | bytes 1048576 | tf_op jit(solution)/shard_map/all_to_all | solution.py:224
  52.4 0.7 copy-start.9
  58.6 28.1 %copy-start.2 = (bf16[1152,128]{1,0:T(8,128)(2,1)S(1)}, bf16[1152,128]{1,0:T(8,128)(2,1)}, u32[]{:S(2)}) copy-start(bf16[1152,128]{1,0:T(8,128)(2,1)} %space_weight.1) | copy-start | bytes 884740
  71.5 0.7 copy-start.4
  71.5 0.7 copy-start.5
  71.5 0.7 copy-start.6
  72.4 14.3 %copy-start.3 = (f32[3]{0:T(128)S(1)}, f32[3]{0:T(128)}, u32[]{:S(2)}) copy-start(f32[3]{0:T(128)} %pad_maximum_fusion.scalars) | copy-start | bytes 40
  72.4 9.9 %collective-permute-start = (bf16[32,16,128]{2,1,0:T(8,128)(2,1)S(1)}, bf16[32,16,128]{2,1,0:T(8,128)(2,1)S(1)}, u32[]{:S(2)}, u32[]{:S(2)}) collective-permute-start(bf16[32,16,128]{2,1,0:T(8,128)(2,1)S(1)} %get-tuple-element.7.second), channel_id=1, source_target_pairs={{0,1},{1,2},{2,3},{3,4},{4,5},{5,6},{6,7},{7,8},{8,9},{9,10},{10,1... | collective-permute-start | bytes 393224 | tf_op jit(solution)/shard_map/ppermute | solution.py:287
  80.4 6.3 %collective-permute-start.1 = (bf16[32,16,128]{2,1,0:T(8,128)(2,1)S(1)}, bf16[32,16,128]{2,1,0:T(8,128)(2,1)S(1)}, u32[]{:S(2)}, u32[]{:S(2)}) collective-permute-start(bf16[32,16,128]{2,1,0:T(8,128)(2,1)S(1)} %get-tuple-element.8.first), channel_id=1, source_target_pairs={{1,0},{2,1},{3,2},{4,3},{5,4},{6,5},{7,6},{8,7},{9,8},{10,9},{11,1... | collective-permute-start | bytes 393224 | tf_op jit(solution)/shard_map/ppermute | solution.py:288
  92.9 21.2 %copy-start.1 = (f32[1,1,32,32,128]{4,3,2,1,0:T(8,128)S(1)}, f32[1,1,32,32,128]{4,3,2,1,0:T(8,128)}, u32[]{:S(2)}) copy-start(f32[1,1,32,32,128]{4,3,2,1,0:T(8,128)} %param.12) | copy-start | bytes 1572868
  130.0 20.6 %copy-start.10 = (f32[1,32,32,128]{3,2,1,0:T(8,128)S(1)}, f32[1,32,32,128]{3,2,1,0:T(8,128)}, u32[]{:S(2)}) copy-start(f32[1,32,32,128]{3,2,1,0:T(8,128)} %param.10) | copy-start | bytes 1572868

commit v5 on v4

--- a/solution.py
+++ b/solution.py
@@ -57,14 +57,25 @@
     return dot(attended.astype(BF16), output_weight)
 
 
+def times(step):
+    value = step[0].astype(F32) / 1000.0
+    return value, (0.5 + value) / math.sqrt(STEPS)
+
+
 def first_kernel(
-    scalars, guess_far, noise_far, start_far, weight_far, gain, scaling, offset, out,
-    guess, noise, start, space_weight, padded, mixed, drawn, packed, sems,
+    step, guess_far, noise_far, start_far, weight_far, map_far, encoded, gain_s, gain_a, out, params,
+    guess, noise, start, space_weight, time_weight, padded, mixed, drawn, packed, sems,
 ):
     copies = [
         pltpu.make_async_copy(far, near, sems.at[i])
         for i, (far, near) in enumerate(
-            ((guess_far, guess), (weight_far, space_weight), (noise_far, noise), (start_far, start))
+            (
+                (guess_far, guess),
+                (weight_far, space_weight),
+                (noise_far, noise),
+                (start_far, start),
+                (map_far, time_weight),
+            )
         )
     ]
     for copy in copies:
@@ -72,11 +83,20 @@
     col = lax.broadcasted_iota(jnp.int32, (8, SIDE, C), 1)
     padded[0] = jnp.zeros((SIDE, 3 * C), BF16)
     padded[SIDE + 1] = jnp.zeros((SIDE, 3 * C), BF16)
+    copies[4].wait()
+    shifted = jnp.dot(
+        jnp.broadcast_to(encoded[...], (8, C)), time_weight[...],
+        precision=lax.Precision.HIGHEST, preferred_element_type=F32,
+    )[0:1]
+    scaling, offset = 1.0 + shifted[:, :C], shifted[:, C:]
+    gain = gain_s[...]
+    for i, row in enumerate((scaling, offset, gain, gain_a[...])):
+        params[pl.ds(i * 16, 16), :] = jnp.broadcast_to(row, (16, C))
     copies[0].wait()
     for block in range(4):
         rows = pl.ds(block * 8, 8)
         state = guess[rows]
-        normed = unit(state, gain[...]) * scaling[...] + offset[...]
+        normed = unit(state, gain) * scaling + offset
         left = jnp.where(col == 0, 0.0, pltpu.roll(normed, 1, 1))
         right = jnp.where(col == SIDE - 1, 0.0, pltpu.roll(normed, SIDE - 1, 1))
         at = pl.ds(block * 8 + 1, 8)
@@ -94,8 +114,9 @@
     mixed[...] = total
     copies[2].wait()
     copies[3].wait()
-    scale = scalars[0]
-    last = scalars[1] > 0.5
+    time_value, coefficient = times(step)
+    scale = time_value * coefficient
+    last = lax.axis_index("tm_0") * lax.axis_size("tm_1") + lax.axis_index("tm_1") == STEPS - 1
     for block in range(8):
         rows = pl.ds(block * 128, 128)
         band = pl.ds(block * 4, 4)
@@ -113,37 +134,40 @@
         out[rows, :] = packed[rows, :].astype(BF16)
 
 
-def owner_kernel(all_steps, received, gain, attention_weight, output_weight, states, wide, drifts):
+def owner_kernel(all_steps, received, params, attention_weight, output_weight, states, noise_before, wide, drifts):
     masks = attention_masks(True)
     wide[...] = received[...].astype(F32)
     for cell in range(2):
         for block in range(4):
             mixed = wide[pl.ds(block * 512 + cell, 128, 4), :]
             drifts[pl.ds(cell * 512 + block * 128, 128), :] = mixed + attend_block(
-                mixed, gain[...], attention_weight[...], output_weight[...], masks
+                mixed, params[48:49, :], attention_weight[...], output_weight[...], masks
             )
     for cell in range(2):
         tail = (STEPS - 1) * FRAMES * 4 + cell
         state = wide[pl.ds(tail + 2, FRAMES, 4), :] + wide[pl.ds(tail, FRAMES, 4), :]
+        noises = jnp.zeros((FRAMES, C), F32)
         for step in range(STEPS):
             states[pl.ds(step * 32 + cell * FRAMES, FRAMES), :] = state.astype(BF16)
+            noise_before[pl.ds(step * 32 + cell * FRAMES, FRAMES), :] = noises
             if step < STEPS - 1:
                 drawn = wide[pl.ds(step * FRAMES * 4 + 2 + cell, FRAMES, 4), :]
                 drift = drifts[pl.ds(cell * 512 + step * FRAMES, FRAMES), :]
                 coefficient = (0.5 + all_steps[step].astype(F32) / 1000.0) / math.sqrt(STEPS)
                 state = state + (coefficient * drift + drawn)
-
-
-def norm_kernel(state, gain, scaling, offset, first, second):
+                noises = noises + drawn
+
+
+def norm_kernel(state, params, first, second):
     for cell, out in ((0, first), (1, second)):
         for block in range(4):
             rows = state[pl.ds(block * 8, 8), cell].astype(F32)
-            normed = unit(rows, gain[...]) * scaling[...] + offset[...]
+            normed = unit(rows, params[32:33, :]) * params[0:1, :] + params[16:17, :]
             out[pl.ds(block * 8, 8)] = normed.astype(BF16)
 
 
 def second_kernel(
-    scalars, state, left, first, second, right, space_weight, gain, attention_weight, output_weight, out, padded, conv, block_out, turned
+    step, state, left, first, second, right, space_weight, params, attention_weight, output_weight, out, padded, conv
 ):
     for col, piece in enumerate((left, first, second, right)):
         padded[col, 0] = jnp.zeros((FRAMES, C), BF16)
@@ -157,36 +181,25 @@
         ]
         conv[cell] = dot(jnp.concatenate(taps, axis=-1), space_weight[...])
     masks = attention_masks(True)
-    coefficient = scalars[2]
+    coefficient = times(step)[1]
     for cell in range(2):
         for block in range(4):
             found = conv[cell, pl.ds(block * 128, 128), :]
             here = state[pl.ds(block * 8, 8), cell].reshape(128, C).astype(F32)
             mixed = here + found * jax.nn.sigmoid(found)
             drift = mixed + attend_block(
-                mixed, gain[...], attention_weight[...], output_weight[...], masks
+                mixed, params[48:49, :], attention_weight[...], output_weight[...], masks
             )
-            block_out[...] = coefficient * drift
-            for frame in range(FRAMES):
-                turned[frame, pl.ds(cell * SIDE + block * 8, 8), :] = block_out[pl.ds(frame, 8, FRAMES), :]
-    out[...] = turned[...].astype(BF16)
-
-
-def frame_kernel(scalars, received, noise, out, natural):
-    for holder in range(FRAMES):
-        for side in range(2):
-            piece = received[holder, pl.ds(side * SIDE, SIDE), :].astype(F32)
-            natural[pl.ds(2 * holder + side, SIDE, SIDE), :] = piece
-    out[...] = (natural[...] + scalars[0] * noise[...]).astype(BF16)
-
-
-def sum_kernel(received, out):
-    for half in range(2):
+            out[pl.ds(block * 8, 8), cell] = (coefficient * drift).reshape(8, FRAMES, C).astype(BF16)
+
+
+def sum_kernel(received, noise_before, out):
+    for cell in range(2):
         total = jnp.zeros((FRAMES, C), F32)
         for step in range(STEPS):
-            rows = pl.ds(step * 32 + half * FRAMES, FRAMES)
+            rows = pl.ds(step * 32 + cell * FRAMES, FRAMES)
             total = total + received[rows, :].astype(F32)
-            out[rows, :] = total
+            out[pl.ds(step * 32 + cell, FRAMES, 2), :] = total + noise_before[rows, :]
 
 
 def call(kernel, outs, operands, scratch, flops, spaces=(), grant=16):
@@ -209,15 +222,10 @@
 
 def embed_time(step_value):
     half_width = C // 2
-    frequency = jnp.exp(-math.log(10000.0) * jnp.arange(half_width, dtype=F32) / half_width)
+    lane = jnp.arange(C)
+    frequency = jnp.exp(-math.log(10000.0) * (lane % half_width).astype(F32) / half_width)
     angles = step_value.astype(F32) * frequency
-    return jnp.concatenate([jnp.cos(angles), jnp.sin(angles)])
-
-
-def modulation(step_value, time_weight):
-    encoded = embed_time(step_value)[None, :]
-    shifted = jnp.dot(encoded, time_weight, precision=lax.Precision.HIGHEST, preferred_element_type=F32)
-    return (1.0 + shifted[:, :C], shifted[:, C:])
+    return jnp.where(lane < half_width, jnp.cos(angles), jnp.sin(angles))[None, :]
 
 
 def exchange(array, axes):
@@ -236,41 +244,39 @@
     attention_weight,
     output_weight,
 ):
-    steps_total = lax.axis_size(TM)
-    step_value = timesteps[0]
-    time_value = step_value.astype(F32) / 1000.0
-    coefficient = (0.5 + time_value) / math.sqrt(steps_total)
-    scaling, offset = modulation(step_value, time_weight)
     guess, noise, start = initial_guess[0, 0], noise_draws[0, 0], start_state[0]
-    gain_s, gain_a = gain_space[None, :], gain_attention[None, :]
-    is_last = (lax.axis_index(TM) == steps_total - 1).astype(F32)
-    scalars = jnp.stack([coefficient * time_value, is_last, coefficient])
-
-    (sent,) = call(
+    time_value = timesteps[0].astype(F32) / 1000.0
+    own_scale = time_value * (0.5 + time_value) / math.sqrt(STEPS)
+    encoded, own_scale = lax.optimization_barrier((embed_time(timesteps[0]), own_scale))
+    sent, params = call(
         first_kernel,
-        [struct((2 * CELLS, C), BF16)],
-        (scalars, guess, noise, start, space_weight, gain_s, scaling, offset),
+        [struct((2 * CELLS, C), BF16), struct((64, C), F32)],
+        (
+            timesteps, guess, noise, start, space_weight, time_weight,
+            encoded, gain_space[None, :], gain_attention[None, :],
+        ),
         [
             pltpu.VMEM((SIDE, SIDE, C), F32),
             pltpu.VMEM((SIDE, SIDE, C), F32),
             pltpu.VMEM((SIDE, SIDE, C), F32),
             pltpu.VMEM((9 * C, C), BF16),
+            pltpu.VMEM((C, 2 * C), F32),
             pltpu.VMEM((SIDE + 2, SIDE, 3 * C), BF16),
             pltpu.VMEM((CELLS, C), F32),
             pltpu.VMEM((CELLS, C), F32),
             pltpu.VMEM((2 * CELLS, C), F32),
-            pltpu.SemaphoreType.DMA((4,)),
+            pltpu.SemaphoreType.DMA((5,)),
         ],
         2 * CELLS * 9 * C * C,
-        (SMEM, FAR, FAR, FAR, FAR),
+        (SMEM, FAR, FAR, FAR, FAR, FAR),
         62,
     )
     received = exchange(sent.reshape(512, 4, C), ALL).reshape(2 * CELLS, C)
     all_steps = lax.all_gather(timesteps, TM, tiled=True)
-    (states,) = call(
+    states, noise_before = call(
         owner_kernel,
-        [struct((CELLS, C), BF16)],
-        (all_steps, received, gain_a, attention_weight, output_weight),
+        [struct((CELLS, C), BF16), struct((CELLS, C), F32)],
+        (all_steps, received, params, attention_weight, output_weight),
         [pltpu.VMEM((2 * CELLS, C), F32), pltpu.VMEM((CELLS, C), F32)],
         2 * CELLS * 8 * C * C,
         (SMEM,),
@@ -279,38 +285,25 @@
     first, second = call(
         norm_kernel,
         [struct((SIDE, FRAMES, C), BF16)] * 2,
-        (state, gain_s, scaling, offset),
+        (state, params),
         [],
         10 * CELLS * C,
     )
     count = lax.axis_size("frame")
     left = lax.ppermute(second, "frame", [(k, k + 1) for k in range(count - 1)])
     right = lax.ppermute(first, "frame", [(k + 1, k) for k in range(count - 1)])
-    (terms,) = call(
+    (drifts,) = call(
         second_kernel,
-        [struct((FRAMES, 64, C), BF16)],
-        (scalars, state, left, first, second, right, space_weight, gain_a, attention_weight, output_weight),
-        [
-            pltpu.VMEM((4, SIDE + 2, FRAMES, C), BF16),
-            pltpu.VMEM((2, CELLS // 2, C), F32),
-            pltpu.VMEM((128, C), F32),
-            pltpu.VMEM((FRAMES, 64, C), F32),
-        ],
+        [struct((SIDE, 2, FRAMES, C), BF16)],
+        (timesteps, state, left, first, second, right, space_weight, params, attention_weight, output_weight),
+        [pltpu.VMEM((4, SIDE + 2, FRAMES, C), BF16), pltpu.VMEM((2, CELLS // 2, C), F32)],
         2 * CELLS * 17 * C * C,
         (SMEM,),
     )
-    (terms,) = call(
-        frame_kernel,
-        [struct((CELLS, C), BF16)],
-        (scalars, exchange(terms, "frame"), noise.reshape(CELLS, C)),
-        [pltpu.VMEM((CELLS, C), F32)],
-        2 * CELLS * C,
-        (SMEM,),
-    )
-    terms = exchange(terms.reshape(32, 32, C), TM).reshape(CELLS, C)
-    (sums,) = call(sum_kernel, [struct((CELLS, C), F32)], (terms,), [], 2 * CELLS * C)
-    sums = exchange(sums.reshape(32, 32, C), TM).reshape(SIDE, SIDE, C)
-    return (start + sums)[None, None]
+    drifts = exchange(drifts.reshape(32, 32, C), TM).reshape(CELLS, C)
+    (sums,) = call(sum_kernel, [struct((CELLS, C), F32)], (drifts, noise_before), [], 2 * CELLS * C)
+    sums = exchange(sums.reshape(512, 2, C), ALL).reshape(SIDE, SIDE, C)
+    return (start + (sums + own_scale * noise))[None, None]
 
 
 def solution(mesh):

time: 154 us -> 144 us (0.935); the launches traced: 151 us -> 143 us
  blocking collectives: 91.1 us -> 86.7 us
  local copies, waits for them, and re-layouts: 3.65 us -> 2.07 us
    all_to_all x4 -> x3, blocking collectives: 69.4 us -> 64.9 us  [exchange(): return lax.all_to_all(array, axes, 0, 0, tiled=True)]
    unnamed x25 -> x15, local copies, waits for them, and re-layouts: 3.65 us -> 2.07 us
    pallas_call x6 -> x5, Pallas kernels: 17.2 us -> 16.1 us  [call(): pl.pallas_call(kernel, out_shape=outs, in_specs=specs, out_specs=[VMEM] *...]
where the time goes in v5:
time: 144 us; the launch traced here: 143 us
  blocking collectives  86.7 us (60%)
  starting transfers between devices  31.8 us (22%)
  Pallas kernels  16.1 us (11%)
  waiting for transfers between devices  4.35 us (3%)
  local copies, waits for them, and re-layouts  2.07 us (1%)
  other arithmetic  1.54 us (1%)
    all_to_all x3, blocking collectives, exchange(): return lax.all_to_all(array, axes, 0, 0, tiled=True)  64.9 us
    all_to_all x1, starting transfers between devices, exchange(): return lax.all_to_all(array, axes, 0, 0, tiled=True)  22.2 us
    unnamed x1, blocking collectives  21.8 us
    pallas_call x5, Pallas kernels, call(): pl.pallas_call(kernel, out_shape=outs, in_specs=specs, out_specs=[VMEM] *...  16.1 us
    ppermute x1, starting transfers between devices, shards(): left = lax.ppermute(second, 'frame', [(k, k + 1) for k in range(count - 1)])  7.7 us
    ppermute x1, waiting for transfers between devices, shards(): right = lax.ppermute(first, 'frame', [(k + 1, k) for k in range(count - 1)])  4.35 us
  transfers between devices with their start and end apart: 3, of which 1 were waited for; matrix products, arithmetic and copies ran while one was open for 1% of the time, Pallas kernels for 0%

profile of v5, /device:TPU:1, one launch (start us, length us, event | category | flops | bytes accessed | tf_op | source)
XLA Modules:
  0.0 143.3 jit_solution(9147830810739983089)
XLA Ops:
  0.7 0.6 compare_select_fusion.encoded
  1.2 4.7 %shard_map.100 = (bf16[2048,128]{1,0:T(8,128)(2,1)}, f32[64,128]{1,0:T(8,128)}) custom-call(s32[1]{0:T(128)S(6)} %copy.12.step, f32[32,32,128]{2,1,0:T(8,128)} %bitcast.27, f32[32,32,128]{2,1,0:T(8,128)} %bitcast.25, f32[32,32,128]{2,1,0:T(8,128)} %bitcast.24, bf16[1152,128]{1,0:T(8,128)(2,1)} %space_weight.1, f32[128,256]{1,0:T(8,128)} %map_far.1, ...), custom_call_target="tpu_custom_call" | custom-call | flops 301989888 | bytes 2557444 | tf_op jit(solution)/shard_map/pallas_call | solution.py:208
  5.9 0.0 copy-start.1
  5.9 0.0 copy-start.2
  5.9 0.0 copy-start.3
  6.0 22.2 %all-to-all-start = ((bf16[512,4,128]{2,1,0:T(4,128)(2,1)}), bf16[512,4,128]{2,1,0:T(4,128)(2,1)S(1)}, u32[]{:S(2)}, u32[]{:S(2)}) async-start(bf16[512,4,128]{2,1,0:T(4,128)(2,1)} %bitcast.28), calls=%async_computation | async-start | bytes 1048576 | tf_op jit(solution)/shard_map/all_to_all | solution.py:232
  28.1 1.3 dynamic-slice
  29.4 0.7 dynamic-update-slice
  30.2 21.8 %all-reduce.all_steps = s32[32]{0:T(128)S(1)} all-reduce(s32[32]{0:T(128)S(1)} %dynamic-update-slice), channel_id=1, replica_groups=mesh['tm_0'=4,'tm_1'=8,'frame'=16] {'tm_0','tm_1'}, use_global_device_ids=true, to_apply=%add | all-reduce | flops 32 | bytes 256
  52.0 0.0 all-to-all-done
  52.0 0.0 copy-done.1
  52.0 0.0 copy-done.2
  52.0 0.0 copy-done.3
  52.0 5.6 %shard_map.101 = (bf16[1024,128]{1,0:T(8,128)(2,1)S(1)}, f32[1024,128]{1,0:T(8,128)S(1)}) custom-call(s32[32]{0:T(128)S(1)} %all-reduce.all_steps, bf16[2048,128]{1,0:T(8,128)(2,1)S(1)} %bitcast.21, f32[64,128]{1,0:T(8,128)S(1)} %copy-done.1, bf16[128,384]{1,0:T(8,128)(2,1)S(1)} %copy-done.2, bf16[128,128]{1,0:T(8,128)(2,1)S(1)} %copy-done.3), custom_call_target="tpu_custom_call" | custom-call | flops 268435456 | bytes 1474688 | tf_op jit(solution)/shard_map/pallas_call | solution.py:208
  57.5 0.0 copy-start
  57.6 12.9 %all_to_all.20 = bf16[32,32,128]{2,1,0:T(8,128)(2,1)S(1)} all-to-all(bf16[32,32,128]{2,1,0:T(8,128)(2,1)S(1)} %bitcast.23), channel_id=1, replica_groups=mesh['tm_0'=4,'tm_1'=8,'frame'=16] {'tm_0','tm_1'}, dimensions={0} | all-to-all | bytes 524288 | tf_op jit(solution)/shard_map/all_to_all | solution.py:232
  70.4 0.2 shard_map.102
  70.7 7.7 %collective-permute-start = (bf16[32,16,128]{2,1,0:T(8,128)(2,1)S(1)}, bf16[32,16,128]{2,1,0:T(8,128)(2,1)S(1)}, u32[]{:S(2)}, u32[]{:S(2)}) collective-permute-start(bf16[32,16,128]{2,1,0:T(8,128)(2,1)S(1)} %get-tuple-element.17.second), channel_id=1, source_target_pairs={{0,1},{1,2},{2,3},{3,4},{4,5},{5,6},{6,7},{7,8},{8,9},{9,10},{10,1... | collective-permute-start | bytes 393224 | tf_op jit(solution)/shard_map/ppermute | solution.py:293
  78.4 1.9 %collective-permute-start.1 = (bf16[32,16,128]{2,1,0:T(8,128)(2,1)S(1)}, bf16[32,16,128]{2,1,0:T(8,128)(2,1)S(1)}, u32[]{:S(2)}, u32[]{:S(2)}) collective-permute-start(bf16[32,16,128]{2,1,0:T(8,128)(2,1)S(1)} %get-tuple-element.18.first), channel_id=1, source_target_pairs={{1,0},{2,1},{3,2},{4,3},{5,4},{6,5},{7,6},{8,7},{9,8},{10,9},{11,1... | collective-permute-start | bytes 393224 | tf_op jit(solution)/shard_map/ppermute | solution.py:294
  80.3 0.0 collective-permute-done.left
  80.3 4.3 %collective-permute-done.1.right = bf16[32,16,128]{2,1,0:T(8,128)(2,1)S(1)} collective-permute-done((bf16[32,16,128]{2,1,0:T(8,128)(2,1)S(1)}, bf16[32,16,128]{2,1,0:T(8,128)(2,1)S(1)}, u32[]{:S(2)}, u32[]{:S(2)}) %collective-permute-start.1) | collective-permute-done | bytes 131104 | tf_op jit(solution)/shard_map/ppermute | solution.py:294
  84.7 0.0 copy-done
  84.7 5.6 %shard_map.103 = bf16[32,2,16,128]{3,2,1,0:T(8,128)(2,1)S(1)} custom-call(s32[1]{0:T(128)S(6)} %copy.12.step, bf16[32,2,16,128]{3,2,1,0:T(8,128)(2,1)S(1)} %bitcast.20, bf16[32,16,128]{2,1,0:T(8,128)(2,1)S(1)} %collective-permute-done.left, bf16[32,16,128]{2,1,0:T(8,128)(2,1)S(1)} %get-tuple-element.18.first, ...), custom_call_target="tpu_custom_call" | custom-call | flops 570425344 | bytes 1507332 | tf_op jit(solution)/shard_map/pallas_call | solution.py:208
  90.2 14.4 %all_to_all.21 = bf16[32,32,128]{2,1,0:T(8,128)(2,1)S(1)} all-to-all(bf16[32,32,128]{2,1,0:T(8,128)(2,1)S(1)} %bitcast.22), channel_id=1, replica_groups=mesh['tm_0'=4,'tm_1'=8,'frame'=16] {'tm_0','tm_1'}, dimensions={0} | all-to-all | bytes 524288 | tf_op jit(solution)/shard_map/all_to_all | solution.py:232
  104.6 0.1 shard_map.104
  104.7 0.0 copy-start.4
  104.7 0.0 copy-start.5
  104.7 37.7 %all_to_all.22 = f32[512,2,128]{2,1,0:T(2,128)S(1)} all-to-all(f32[512,2,128]{2,1,0:T(2,128)S(1)} %bitcast.17), channel_id=1, replica_groups=mesh['tm_0'=4,'tm_1'=8,'frame'=16] {'tm_0','tm_1','frame'}, dimensions={0} | all-to-all | bytes 1048576 | tf_op jit(solution)/shard_map/all_to_all | solution.py:232
  142.4 0.0 copy-done.4
  142.4 0.0 copy-done.5
  142.4 0.9 bitcast_add_fusion
  (1 shorter events, 0.0 us)
Async XLA Ops:
  5.9 46.0 %copy-start.1 = (f32[64,128]{1,0:T(8,128)S(1)}, f32[64,128]{1,0:T(8,128)}, u32[]{:S(2)}) copy-start(f32[64,128]{1,0:T(8,128)} %get-tuple-element.15.params) | copy-start | bytes 98308
  5.9 46.0 %copy-start.2 = (bf16[128,384]{1,0:T(8,128)(2,1)S(1)}, bf16[128,384]{1,0:T(8,128)(2,1)}, u32[]{:S(2)}) copy-start(bf16[128,384]{1,0:T(8,128)(2,1)} %attention_weight.3) | copy-start | bytes 294916
  5.9 46.0 %copy-start.3 = (bf16[128,128]{1,0:T(8,128)(2,1)S(1)}, bf16[128,128]{1,0:T(8,128)(2,1)}, u32[]{:S(2)}) copy-start(bf16[128,128]{1,0:T(8,128)(2,1)} %output_weight.3) | copy-start | bytes 98308
  6.0 46.0 %all-to-all-start = ((bf16[512,4,128]{2,1,0:T(4,128)(2,1)}), bf16[512,4,128]{2,1,0:T(4,128)(2,1)S(1)}, u32[]{:S(2)}, u32[]{:S(2)}) async-start(bf16[512,4,128]{2,1,0:T(4,128)(2,1)} %bitcast.28), calls=%async_computation | async-start | bytes 1048576 | tf_op jit(solution)/shard_map/all_to_all | solution.py:232
  57.5 27.1 %copy-start = (bf16[1152,128]{1,0:T(8,128)(2,1)S(1)}, bf16[1152,128]{1,0:T(8,128)(2,1)}, u32[]{:S(2)}) copy-start(bf16[1152,128]{1,0:T(8,128)(2,1)} %space_weight.1) | copy-start | bytes 884740
  70.7 9.6 %collective-permute-start = (bf16[32,16,128]{2,1,0:T(8,128)(2,1)S(1)}, bf16[32,16,128]{2,1,0:T(8,128)(2,1)S(1)}, u32[]{:S(2)}, u32[]{:S(2)}) collective-permute-start(bf16[32,16,128]{2,1,0:T(8,128)(2,1)S(1)} %get-tuple-element.17.second), channel_id=1, source_target_pairs={{0,1},{1,2},{2,3},{3,4},{4,5},{5,6},{6,7},{7,8},{8,9},{9,10},{10,1... | collective-permute-start | bytes 393224 | tf_op jit(solution)/shard_map/ppermute | solution.py:293
  78.4 6.3 %collective-permute-start.1 = (bf16[32,16,128]{2,1,0:T(8,128)(2,1)S(1)}, bf16[32,16,128]{2,1,0:T(8,128)(2,1)S(1)}, u32[]{:S(2)}, u32[]{:S(2)}) collective-permute-start(bf16[32,16,128]{2,1,0:T(8,128)(2,1)S(1)} %get-tuple-element.18.first), channel_id=1, source_target_pairs={{1,0},{2,1},{3,2},{4,3},{5,4},{6,5},{7,6},{8,7},{9,8},{10,9},{11,1... | collective-permute-start | bytes 393224 | tf_op jit(solution)/shard_map/ppermute | solution.py:294
  104.7 37.7 %copy-start.4 = (f32[1,32,32,128]{3,2,1,0:T(8,128)S(1)}, f32[1,32,32,128]{3,2,1,0:T(8,128)}, u32[]{:S(2)}) copy-start(f32[1,32,32,128]{3,2,1,0:T(8,128)} %param.10) | copy-start | bytes 1572868
  104.7 37.7 %copy-start.5 = (f32[1,1,32,32,128]{4,3,2,1,0:T(8,128)S(1)}, f32[1,1,32,32,128]{4,3,2,1,0:T(8,128)}, u32[]{:S(2)}) copy-start(f32[1,1,32,32,128]{4,3,2,1,0:T(8,128)} %param.12) | copy-start | bytes 1572868

commit v6 on v5

--- a/solution.py
+++ b/solution.py
@@ -31,30 +31,47 @@
     return field * lax.rsqrt(jnp.mean(field * field, axis=-1, keepdims=True) + 1e-06) * gain
 
 
-def attention_masks(cell_major):
+def attend(load, emit, gain, attention_weight, output_weight, normed, query_key, values_t, attended_t):
     row = lax.broadcasted_iota(jnp.int32, (128, 128), 0)
     lane = lax.broadcasted_iota(jnp.int32, (128, 128), 1)
-    same_cell = row // FRAMES == lane // FRAMES if cell_major else row % 8 == lane % 8
-    return same_cell, lane < HEAD_DIM
-
-
-def attend_block(mixed, gain, attention_weight, output_weight, masks):
-    same_cell, first_head = masks
-    projected = dot(unit(mixed, gain).astype(BF16), attention_weight).astype(BF16)
-    queries, keys, values = (projected[:, i * C : (i + 1) * C] for i in range(3))
+    first_head = lane < HEAD_DIM
+    same_cell = row // FRAMES == lane // FRAMES
     zero = jnp.zeros((), BF16)
-    attended = None
-    for head in range(2):
-        lanes = first_head if head == 0 else jnp.logical_not(first_head)
-        scores = lax.dot_general(
-            jnp.where(lanes, queries, zero), keys, (((1,), (1,)), ((), ())), preferred_element_type=F32
-        ) * (1.0 / math.sqrt(HEAD_DIM))
-        scores = jnp.where(same_cell, scores, -1e30)
-        grown = jnp.exp(scores - jnp.max(scores, axis=-1, keepdims=True))
-        weights = (grown * (1.0 / jnp.sum(grown, axis=-1, keepdims=True))).astype(BF16)
-        part = dot(weights, jnp.where(lanes, values, zero))
-        attended = part if attended is None else attended + part
-    return dot(attended.astype(BF16), output_weight)
+    for block in range(8):
+        normed[pl.ds(block * 128, 128), :] = unit(load(block), gain).astype(BF16)
+    query_key[...] = dot(normed[...], attention_weight[:, 0 : 2 * C]).astype(BF16)
+    values_t[...] = lax.dot_general(
+        attention_weight[:, 2 * C :].T, normed[...], (((1,), (1,)), ((), ())), preferred_element_type=F32
+    ).astype(BF16)
+    for block in range(8):
+        rows = pl.ds(block * 128, 128)
+        keys = query_key[rows, C : 2 * C]
+        keys = jnp.concatenate(
+            [jnp.where(first_head, keys, zero), jnp.where(first_head, zero, keys)], axis=0
+        )
+        scores_t = lax.dot_general(
+            keys, query_key[rows, 0:C], (((1,), (1,)), ((), ())), preferred_element_type=F32
+        )
+        parts = []
+        for head in range(2):
+            kept = jnp.where(same_cell, scores_t[head * 128 : (head + 1) * 128], 0.0)
+            scores = jnp.sum(kept.reshape(8, FRAMES, 128), axis=0) * (1.0 / math.sqrt(HEAD_DIM))
+            grown = jnp.exp(scores - jnp.max(scores, axis=0, keepdims=True))
+            weights = grown * (1.0 / jnp.sum(grown, axis=0, keepdims=True))
+            spread = jnp.where(same_cell, jnp.concatenate([weights] * 8, axis=0), 0.0)
+            held = values_t[head * HEAD_DIM : (head + 1) * HEAD_DIM, rows]
+            parts.append(dot(held, spread.astype(BF16)))
+        attended_t[:, rows] = jnp.concatenate(parts, axis=0).astype(BF16)
+    for block in range(8):
+        emit(
+            block,
+            lax.dot_general(
+                attended_t[:, pl.ds(block * 128, 128)],
+                output_weight[...],
+                (((0,), (0,)), ((), ())),
+                preferred_element_type=F32,
+            ),
+        )
 
 
 def times(step):
@@ -134,15 +151,19 @@
         out[rows, :] = packed[rows, :].astype(BF16)
 
 
-def owner_kernel(all_steps, received, params, attention_weight, output_weight, states, noise_before, wide, drifts):
-    masks = attention_masks(True)
+def owner_kernel(
+    all_steps, received, params, attention_weight, output_weight, states, noise_before,
+    wide, drifts, *room,
+):
     wide[...] = received[...].astype(F32)
-    for cell in range(2):
-        for block in range(4):
-            mixed = wide[pl.ds(block * 512 + cell, 128, 4), :]
-            drifts[pl.ds(cell * 512 + block * 128, 128), :] = mixed + attend_block(
-                mixed, params[48:49, :], attention_weight[...], output_weight[...], masks
-            )
+
+    def load(block):
+        return wide[pl.ds(block % 4 * 512 + block // 4, 128, 4), :]
+
+    def emit(block, found):
+        drifts[pl.ds(block * 128, 128), :] = load(block) + found
+
+    attend(load, emit, params[48:49, :], attention_weight, output_weight, *room)
     for cell in range(2):
         tail = (STEPS - 1) * FRAMES * 4 + cell
         state = wide[pl.ds(tail + 2, FRAMES, 4), :] + wide[pl.ds(tail, FRAMES, 4), :]
@@ -167,7 +188,8 @@
 
 
 def second_kernel(
-    step, state, left, first, second, right, space_weight, params, attention_weight, output_weight, out, padded, conv
+    step, state, left, first, second, right, space_weight, params, attention_weight, output_weight,
+    out, padded, mixed, *room,
 ):
     for col, piece in enumerate((left, first, second, right)):
         padded[col, 0] = jnp.zeros((FRAMES, C), BF16)
@@ -179,18 +201,22 @@
             for down in range(3)
             for across in range(3)
         ]
-        conv[cell] = dot(jnp.concatenate(taps, axis=-1), space_weight[...])
-    masks = attention_masks(True)
+        mixed[pl.ds(cell * 512, 512), :] = dot(jnp.concatenate(taps, axis=-1), space_weight[...])
     coefficient = times(step)[1]
-    for cell in range(2):
-        for block in range(4):
-            found = conv[cell, pl.ds(block * 128, 128), :]
-            here = state[pl.ds(block * 8, 8), cell].reshape(128, C).astype(F32)
-            mixed = here + found * jax.nn.sigmoid(found)
-            drift = mixed + attend_block(
-                mixed, params[48:49, :], attention_weight[...], output_weight[...], masks
-            )
-            out[pl.ds(block * 8, 8), cell] = (coefficient * drift).reshape(8, FRAMES, C).astype(BF16)
+    for block in range(8):
+        rows = pl.ds(block * 128, 128)
+        found = mixed[rows, :]
+        here = state[pl.ds(block % 4 * 8, 8), block // 4].reshape(128, C).astype(F32)
+        mixed[rows, :] = here + found * jax.nn.sigmoid(found)
+
+    def load(block):
+        return mixed[pl.ds(block * 128, 128), :]
+
+    def emit(block, found):
+        drift = coefficient * (load(block) + found)
+        out[pl.ds(block % 4 * 8, 8), block // 4] = drift.reshape(8, FRAMES, C).astype(BF16)
+
+    attend(load, emit, params[48:49, :], attention_weight, output_weight, *room)
 
 
 def sum_kernel(received, noise_before, out):
@@ -214,6 +240,15 @@
         compiler_params=pltpu.CompilerParams(vmem_limit_bytes=grant << 20),
         cost_estimate=pl.CostEstimate(flops=flops, bytes_accessed=moved, transcendentals=0),
     )(*operands)
+
+
+def attention_room():
+    return [
+        pltpu.VMEM((CELLS, C), BF16),
+        pltpu.VMEM((CELLS, 2 * C), BF16),
+        pltpu.VMEM((C, CELLS), BF16),
+        pltpu.VMEM((C, CELLS), BF16),
+    ]
 
 
 def struct(shape, dtype):
@@ -277,7 +312,7 @@
         owner_kernel,
         [struct((CELLS, C), BF16), struct((CELLS, C), F32)],
         (all_steps, received, params, attention_weight, output_weight),
-        [pltpu.VMEM((2 * CELLS, C), F32), pltpu.VMEM((CELLS, C), F32)],
+        [pltpu.VMEM((2 * CELLS, C), F32), pltpu.VMEM((CELLS, C), F32), *attention_room()],
         2 * CELLS * 8 * C * C,
         (SMEM,),
     )
@@ -295,8 +330,11 @@
     (drifts,) = call(
         second_kernel,
         [struct((SIDE, 2, FRAMES, C), BF16)],
-        (timesteps, state, left, first, second, right, space_weight, params, attention_weight, output_weight),
-        [pltpu.VMEM((4, SIDE + 2, FRAMES, C), BF16), pltpu.VMEM((2, CELLS // 2, C), F32)],
+        (
+            timesteps, state, left, first, second, right, space_weight, params,
+            attention_weight, output_weight,
+        ),
+        [pltpu.VMEM((4, SIDE + 2, FRAMES, C), BF16), pltpu.VMEM((CELLS, C), F32), *attention_room()],
         2 * CELLS * 17 * C * C,
         (SMEM,),
     )

time: 144 us -> 137 us (0.951)
  Pallas kernels: 16.1 us -> 9.2 us
    pallas_call x5, Pallas kernels: 16.1 us -> 9.2 us  [call(): pl.pallas_call(kernel, out_shape=outs, in_specs=specs, out_specs=[VMEM] *...]
where the time goes in v6:
time: 137 us; the launch traced here: 136 us
  blocking collectives  86.7 us (63%)
  starting transfers between devices  31.8 us (23%)
  Pallas kernels  9.2 us (7%)
  waiting for transfers between devices  4.35 us (3%)
  local copies, waits for them, and re-layouts  2.07 us (2%)
  other arithmetic  1.54 us (1%)
    all_to_all x3, blocking collectives, exchange(): return lax.all_to_all(array, axes, 0, 0, tiled=True)  64.9 us
    all_to_all x1, starting transfers between devices, exchange(): return lax.all_to_all(array, axes, 0, 0, tiled=True)  22.2 us
    unnamed x1, blocking collectives  21.8 us
    pallas_call x5, Pallas kernels, call(): pl.pallas_call(kernel, out_shape=outs, in_specs=specs, out_specs=[VMEM] *...  9.2 us
    ppermute x1, starting transfers between devices, shards(): left = lax.ppermute(second, 'frame', [(k, k + 1) for k in range(count - 1)])  7.7 us
    ppermute x1, waiting for transfers between devices, shards(): right = lax.ppermute(first, 'frame', [(k + 1, k) for k in range(count - 1)])  4.35 us
  transfers between devices with their start and end apart: 3, of which 1 were waited for; matrix products, arithmetic and copies ran while one was open for 1% of the time, Pallas kernels for 0%

profile of v6, /device:TPU:1, one launch (start us, length us, event | category | flops | bytes accessed | tf_op | source)
XLA Modules:
  0.0 136.5 jit_solution(2927177399477311326)
XLA Ops:
  0.7 0.6 compare_select_fusion.encoded
  1.2 4.7 %shard_map.100 = (bf16[2048,128]{1,0:T(8,128)(2,1)}, f32[64,128]{1,0:T(8,128)}) custom-call(s32[1]{0:T(128)S(6)} %copy.12.step, f32[32,32,128]{2,1,0:T(8,128)} %bitcast.27, f32[32,32,128]{2,1,0:T(8,128)} %bitcast.25, f32[32,32,128]{2,1,0:T(8,128)} %bitcast.24, bf16[1152,128]{1,0:T(8,128)(2,1)} %space_weight.1, f32[128,256]{1,0:T(8,128)} %map_far.1, ...), custom_call_target="tpu_custom_call" | custom-call | flops 301989888 | bytes 2557444 | tf_op jit(solution)/shard_map/pallas_call | solution.py:234
  5.9 0.0 copy-start.1
  5.9 0.0 copy-start.2
  5.9 0.0 copy-start.3
  6.0 22.2 %all-to-all-start = ((bf16[512,4,128]{2,1,0:T(4,128)(2,1)}), bf16[512,4,128]{2,1,0:T(4,128)(2,1)S(1)}, u32[]{:S(2)}, u32[]{:S(2)}) async-start(bf16[512,4,128]{2,1,0:T(4,128)(2,1)} %bitcast.28), calls=%async_computation | async-start | bytes 1048576 | tf_op jit(solution)/shard_map/all_to_all | solution.py:267
  28.1 1.3 dynamic-slice
  29.4 0.7 dynamic-update-slice
  30.2 21.8 %all-reduce.all_steps = s32[32]{0:T(128)S(1)} all-reduce(s32[32]{0:T(128)S(1)} %dynamic-update-slice), channel_id=1, replica_groups=mesh['tm_0'=4,'tm_1'=8,'frame'=16] {'tm_0','tm_1'}, use_global_device_ids=true, to_apply=%add | all-reduce | flops 32 | bytes 256
  52.0 0.0 all-to-all-done
  52.0 0.0 copy-done.1
  52.0 0.0 copy-done.2
  52.0 0.0 copy-done.3
  52.0 2.1 %shard_map.101 = (bf16[1024,128]{1,0:T(8,128)(2,1)S(1)}, f32[1024,128]{1,0:T(8,128)S(1)}) custom-call(s32[32]{0:T(128)S(1)} %all-reduce.all_steps, bf16[2048,128]{1,0:T(8,128)(2,1)S(1)} %bitcast.21, f32[64,128]{1,0:T(8,128)S(1)} %copy-done.1, bf16[128,384]{1,0:T(8,128)(2,1)S(1)} %copy-done.2, bf16[128,128]{1,0:T(8,128)(2,1)S(1)} %copy-done.3), custom_call_target="tpu_custom_call" | custom-call | flops 268435456 | bytes 1474688 | tf_op jit(solution)/shard_map/pallas_call | solution.py:234
  54.1 0.0 copy-start
  54.1 12.9 %all_to_all.20 = bf16[32,32,128]{2,1,0:T(8,128)(2,1)S(1)} all-to-all(bf16[32,32,128]{2,1,0:T(8,128)(2,1)S(1)} %bitcast.23), channel_id=1, replica_groups=mesh['tm_0'=4,'tm_1'=8,'frame'=16] {'tm_0','tm_1'}, dimensions={0} | all-to-all | bytes 524288 | tf_op jit(solution)/shard_map/all_to_all | solution.py:267
  67.0 0.2 shard_map.102
  67.2 7.7 %collective-permute-start = (bf16[32,16,128]{2,1,0:T(8,128)(2,1)S(1)}, bf16[32,16,128]{2,1,0:T(8,128)(2,1)S(1)}, u32[]{:S(2)}, u32[]{:S(2)}) collective-permute-start(bf16[32,16,128]{2,1,0:T(8,128)(2,1)S(1)} %get-tuple-element.17.second), channel_id=1, source_target_pairs={{0,1},{1,2},{2,3},{3,4},{4,5},{5,6},{6,7},{7,8},{8,9},{9,10},{10,1... | collective-permute-start | bytes 393224 | tf_op jit(solution)/shard_map/ppermute | solution.py:328
  74.9 1.9 %collective-permute-start.1 = (bf16[32,16,128]{2,1,0:T(8,128)(2,1)S(1)}, bf16[32,16,128]{2,1,0:T(8,128)(2,1)S(1)}, u32[]{:S(2)}, u32[]{:S(2)}) collective-permute-start(bf16[32,16,128]{2,1,0:T(8,128)(2,1)S(1)} %get-tuple-element.18.first), channel_id=1, source_target_pairs={{1,0},{2,1},{3,2},{4,3},{5,4},{6,5},{7,6},{8,7},{9,8},{10,9},{11,1... | collective-permute-start | bytes 393224 | tf_op jit(solution)/shard_map/ppermute | solution.py:329
  76.8 0.0 collective-permute-done.left
  76.8 4.3 %collective-permute-done.1.right = bf16[32,16,128]{2,1,0:T(8,128)(2,1)S(1)} collective-permute-done((bf16[32,16,128]{2,1,0:T(8,128)(2,1)S(1)}, bf16[32,16,128]{2,1,0:T(8,128)(2,1)S(1)}, u32[]{:S(2)}, u32[]{:S(2)}) %collective-permute-start.1) | collective-permute-done | bytes 131104 | tf_op jit(solution)/shard_map/ppermute | solution.py:329
  81.2 0.0 copy-done
  81.2 2.2 %shard_map.103 = bf16[32,2,16,128]{3,2,1,0:T(8,128)(2,1)S(1)} custom-call(s32[1]{0:T(128)S(6)} %copy.12.step, bf16[32,2,16,128]{3,2,1,0:T(8,128)(2,1)S(1)} %bitcast.20, bf16[32,16,128]{2,1,0:T(8,128)(2,1)S(1)} %collective-permute-done.left, bf16[32,16,128]{2,1,0:T(8,128)(2,1)S(1)} %get-tuple-element.18.first, ...), custom_call_target="tpu_custom_call" | custom-call | flops 570425344 | bytes 1507332 | tf_op jit(solution)/shard_map/pallas_call | solution.py:234
  83.4 14.4 %all_to_all.21 = bf16[32,32,128]{2,1,0:T(8,128)(2,1)S(1)} all-to-all(bf16[32,32,128]{2,1,0:T(8,128)(2,1)S(1)} %bitcast.22), channel_id=1, replica_groups=mesh['tm_0'=4,'tm_1'=8,'frame'=16] {'tm_0','tm_1'}, dimensions={0} | all-to-all | bytes 524288 | tf_op jit(solution)/shard_map/all_to_all | solution.py:267
  97.8 0.1 shard_map.104
  97.8 0.0 copy-start.4
  97.8 0.0 copy-start.5
  97.8 37.7 %all_to_all.22 = f32[512,2,128]{2,1,0:T(2,128)S(1)} all-to-all(f32[512,2,128]{2,1,0:T(2,128)S(1)} %bitcast.17), channel_id=1, replica_groups=mesh['tm_0'=4,'tm_1'=8,'frame'=16] {'tm_0','tm_1','frame'}, dimensions={0} | all-to-all | bytes 1048576 | tf_op jit(solution)/shard_map/all_to_all | solution.py:267
  135.5 0.0 copy-done.4
  135.5 0.0 copy-done.5
  135.5 0.9 bitcast_add_fusion
  (1 shorter events, 0.0 us)
Async XLA Ops:
  5.9 46.0 %copy-start.1 = (f32[64,128]{1,0:T(8,128)S(1)}, f32[64,128]{1,0:T(8,128)}, u32[]{:S(2)}) copy-start(f32[64,128]{1,0:T(8,128)} %get-tuple-element.15.params) | copy-start | bytes 98308
  5.9 46.0 %copy-start.2 = (bf16[128,384]{1,0:T(8,128)(2,1)S(1)}, bf16[128,384]{1,0:T(8,128)(2,1)}, u32[]{:S(2)}) copy-start(bf16[128,384]{1,0:T(8,128)(2,1)} %attention_weight.3) | copy-start | bytes 294916
  5.9 46.0 %copy-start.3 = (bf16[128,128]{1,0:T(8,128)(2,1)S(1)}, bf16[128,128]{1,0:T(8,128)(2,1)}, u32[]{:S(2)}) copy-start(bf16[128,128]{1,0:T(8,128)(2,1)} %output_weight.3) | copy-start | bytes 98308
  6.0 46.0 %all-to-all-start = ((bf16[512,4,128]{2,1,0:T(4,128)(2,1)}), bf16[512,4,128]{2,1,0:T(4,128)(2,1)S(1)}, u32[]{:S(2)}, u32[]{:S(2)}) async-start(bf16[512,4,128]{2,1,0:T(4,128)(2,1)} %bitcast.28), calls=%async_computation | async-start | bytes 1048576 | tf_op jit(solution)/shard_map/all_to_all | solution.py:267
  54.1 27.1 %copy-start = (bf16[1152,128]{1,0:T(8,128)(2,1)S(1)}, bf16[1152,128]{1,0:T(8,128)(2,1)}, u32[]{:S(2)}) copy-start(bf16[1152,128]{1,0:T(8,128)(2,1)} %space_weight.1) | copy-start | bytes 884740
  67.2 9.6 %collective-permute-start = (bf16[32,16,128]{2,1,0:T(8,128)(2,1)S(1)}, bf16[32,16,128]{2,1,0:T(8,128)(2,1)S(1)}, u32[]{:S(2)}, u32[]{:S(2)}) collective-permute-start(bf16[32,16,128]{2,1,0:T(8,128)(2,1)S(1)} %get-tuple-element.17.second), channel_id=1, source_target_pairs={{0,1},{1,2},{2,3},{3,4},{4,5},{5,6},{6,7},{7,8},{8,9},{9,10},{10,1... | collective-permute-start | bytes 393224 | tf_op jit(solution)/shard_map/ppermute | solution.py:328
  74.9 6.3 %collective-permute-start.1 = (bf16[32,16,128]{2,1,0:T(8,128)(2,1)S(1)}, bf16[32,16,128]{2,1,0:T(8,128)(2,1)S(1)}, u32[]{:S(2)}, u32[]{:S(2)}) collective-permute-start(bf16[32,16,128]{2,1,0:T(8,128)(2,1)S(1)} %get-tuple-element.18.first), channel_id=1, source_target_pairs={{1,0},{2,1},{3,2},{4,3},{5,4},{6,5},{7,6},{8,7},{9,8},{10,9},{11,1... | collective-permute-start | bytes 393224 | tf_op jit(solution)/shard_map/ppermute | solution.py:329
  97.8 37.7 %copy-start.4 = (f32[1,32,32,128]{3,2,1,0:T(8,128)S(1)}, f32[1,32,32,128]{3,2,1,0:T(8,128)}, u32[]{:S(2)}) copy-start(f32[1,32,32,128]{3,2,1,0:T(8,128)} %param.10) | copy-start | bytes 1572868
  97.8 37.7 %copy-start.5 = (f32[1,1,32,32,128]{4,3,2,1,0:T(8,128)S(1)}, f32[1,1,32,32,128]{4,3,2,1,0:T(8,128)}, u32[]{:S(2)}) copy-start(f32[1,1,32,32,128]{4,3,2,1,0:T(8,128)} %param.12) | copy-start | bytes 1572868

commit v7 on v6

--- a/solution.py
+++ b/solution.py
@@ -80,18 +80,18 @@
 
 
 def first_kernel(
-    step, guess_far, noise_far, start_far, weight_far, map_far, encoded, gain_s, gain_a, out, params,
+    step, guess_far, noise_far, start_far, weight_far, map_far, gain_s, gain_a, out, params,
     guess, noise, start, space_weight, time_weight, padded, mixed, drawn, packed, sems,
 ):
     copies = [
         pltpu.make_async_copy(far, near, sems.at[i])
         for i, (far, near) in enumerate(
             (
+                (map_far, time_weight),
                 (guess_far, guess),
                 (weight_far, space_weight),
                 (noise_far, noise),
                 (start_far, start),
-                (map_far, time_weight),
             )
         )
     ]
@@ -100,16 +100,19 @@
     col = lax.broadcasted_iota(jnp.int32, (8, SIDE, C), 1)
     padded[0] = jnp.zeros((SIDE, 3 * C), BF16)
     padded[SIDE + 1] = jnp.zeros((SIDE, 3 * C), BF16)
-    copies[4].wait()
+    copies[0].wait()
+    lane = lax.broadcasted_iota(jnp.int32, (8, C), 1)
+    frequency = jnp.exp((lane % HEAD_DIM).astype(F32) * (-math.log(10000.0) / HEAD_DIM))
+    angles = step[0].astype(F32) * frequency
     shifted = jnp.dot(
-        jnp.broadcast_to(encoded[...], (8, C)), time_weight[...],
+        jnp.where(lane < HEAD_DIM, jnp.cos(angles), jnp.sin(angles)), time_weight[...],
         precision=lax.Precision.HIGHEST, preferred_element_type=F32,
     )[0:1]
     scaling, offset = 1.0 + shifted[:, :C], shifted[:, C:]
     gain = gain_s[...]
     for i, row in enumerate((scaling, offset, gain, gain_a[...])):
         params[pl.ds(i * 16, 16), :] = jnp.broadcast_to(row, (16, C))
-    copies[0].wait()
+    copies[1].wait()
     for block in range(4):
         rows = pl.ds(block * 8, 8)
         state = guess[rows]
@@ -120,7 +123,8 @@
         padded[at, :, 0:C] = left.astype(BF16)
         padded[at, :, C : 2 * C] = normed.astype(BF16)
         padded[at, :, 2 * C : 3 * C] = right.astype(BF16)
-    copies[1].wait()
+    for copy in copies[2:]:
+        copy.wait()
     total = None
     for shift in range(3):
         part = dot(
@@ -129,8 +133,6 @@
         )
         total = part if total is None else total + part
     mixed[...] = total
-    copies[2].wait()
-    copies[3].wait()
     time_value, coefficient = times(step)
     scale = time_value * coefficient
     last = lax.axis_index("tm_0") * lax.axis_size("tm_1") + lax.axis_index("tm_1") == STEPS - 1
@@ -179,22 +181,36 @@
                 noises = noises + drawn
 
 
-def norm_kernel(state, params, first, second):
-    for cell, out in ((0, first), (1, second)):
-        for block in range(4):
-            rows = state[pl.ds(block * 8, 8), cell].astype(F32)
-            normed = unit(rows, params[32:33, :]) * params[0:1, :] + params[16:17, :]
-            out[pl.ds(block * 8, 8)] = normed.astype(BF16)
+def norm_kernel(state, params, inner, outer):
+    odd = lax.axis_index("frame") % 2 == 1
+    for block in range(4):
+        rows = pl.ds(block * 8, 8)
+        pair = [
+            unit(state[rows, cell].astype(F32), params[32:33, :]) * params[0:1, :] + params[16:17, :]
+            for cell in range(2)
+        ]
+        inner[rows] = jnp.where(odd, pair[0], pair[1]).astype(BF16)
+        outer[rows] = jnp.where(odd, pair[1], pair[0]).astype(BF16)
 
 
 def second_kernel(
-    step, state, left, first, second, right, space_weight, params, attention_weight, output_weight,
+    step, state, inner, outer, from_core, from_chip, space_weight, params, attention_weight, output_weight,
     out, padded, mixed, *room,
 ):
-    for col, piece in enumerate((left, first, second, right)):
+    odd = lax.axis_index("frame") % 2 == 1
+    columns = ((from_chip, from_core), (outer, inner), (inner, outer), (from_core, from_chip))
+    for col, (when_even, when_odd) in enumerate(columns):
         padded[col, 0] = jnp.zeros((FRAMES, C), BF16)
         padded[col, SIDE + 1] = jnp.zeros((FRAMES, C), BF16)
-        padded[col, 1 : SIDE + 1] = piece[...]
+
+        @pl.when(odd)
+        def _(col=col, piece=when_odd):
+            padded[col, 1 : SIDE + 1] = piece[...]
+
+        @pl.when(jnp.logical_not(odd))
+        def _(col=col, piece=when_even):
+            padded[col, 1 : SIDE + 1] = piece[...]
+
     for cell in range(2):
         taps = [
             padded[cell + across, down : down + SIDE].reshape(SIDE * FRAMES, C)
@@ -253,14 +269,6 @@
 
 def struct(shape, dtype):
     return jax.ShapeDtypeStruct(shape, dtype)
-
-
-def embed_time(step_value):
-    half_width = C // 2
-    lane = jnp.arange(C)
-    frequency = jnp.exp(-math.log(10000.0) * (lane % half_width).astype(F32) / half_width)
-    angles = step_value.astype(F32) * frequency
-    return jnp.where(lane < half_width, jnp.cos(angles), jnp.sin(angles))[None, :]
 
 
 def exchange(array, axes):
@@ -282,13 +290,13 @@
     guess, noise, start = initial_guess[0, 0], noise_draws[0, 0], start_state[0]
     time_value = timesteps[0].astype(F32) / 1000.0
     own_scale = time_value * (0.5 + time_value) / math.sqrt(STEPS)
-    encoded, own_scale = lax.optimization_barrier((embed_time(timesteps[0]), own_scale))
+    gain_space, own_scale = lax.optimization_barrier((gain_space, own_scale))
     sent, params = call(
         first_kernel,
         [struct((2 * CELLS, C), BF16), struct((64, C), F32)],
         (
             timesteps, guess, noise, start, space_weight, time_weight,
-            encoded, gain_space[None, :], gain_attention[None, :],
+            gain_space[None, :], gain_attention[None, :],
         ),
         [
             pltpu.VMEM((SIDE, SIDE, C), F32),
@@ -317,7 +325,7 @@
         (SMEM,),
     )
     state = exchange(states.reshape(32, 32, C), TM).reshape(SIDE, 2, FRAMES, C)
-    first, second = call(
+    inner, outer = call(
         norm_kernel,
         [struct((SIDE, FRAMES, C), BF16)] * 2,
         (state, params),
@@ -325,13 +333,15 @@
         10 * CELLS * C,
     )
     count = lax.axis_size("frame")
-    left = lax.ppermute(second, "frame", [(k, k + 1) for k in range(count - 1)])
-    right = lax.ppermute(first, "frame", [(k + 1, k) for k in range(count - 1)])
+    chips = [(k + i, k + 1 - i) for k in range(1, count - 1, 2) for i in range(2)]
+    cores = [(k, k ^ 1) for k in range(count)]
+    from_chip = lax.ppermute(outer, "frame", chips)
+    from_core = lax.ppermute(inner, "frame", cores)
     (drifts,) = call(
         second_kernel,
         [struct((SIDE, 2, FRAMES, C), BF16)],
         (
-            timesteps, state, left, first, second, right, space_weight, params,
+            timesteps, state, inner, outer, from_core, from_chip, space_weight, params,
             attention_weight, output_weight,
         ),
         [pltpu.VMEM((4, SIDE + 2, FRAMES, C), BF16), pltpu.VMEM((CELLS, C), F32), *attention_room()],

time: 137 us -> 136 us (level)
  no operation moved by 1% of the time
where the time goes in v7:
time: 136 us
  blocking collectives  87.6 us (64%)
  starting transfers between devices  31.8 us (23%)
  Pallas kernels  8.6 us (6%)
  waiting for transfers between devices  4.19 us (3%)
  local copies, waits for them, and re-layouts  2.07 us (2%)
    all_to_all x3, blocking collectives, exchange(): return lax.all_to_all(array, axes, 0, 0, tiled=True)  65.8 us
    all_to_all x1, starting transfers between devices, exchange(): return lax.all_to_all(array, axes, 0, 0, tiled=True)  22.2 us
    unnamed x1, blocking collectives  21.8 us
    pallas_call x5, Pallas kernels, call(): pl.pallas_call(kernel, out_shape=outs, in_specs=specs, out_specs=[VMEM] *...  8.6 us
    ppermute x1, starting transfers between devices, shards(): from_core = lax.ppermute(inner, 'frame', cores)  7.54 us
    ppermute x1, waiting for transfers between devices, shards(): from_chip = lax.ppermute(outer, 'frame', chips)  4.19 us
  transfers between devices with their start and end apart: 3, of which 1 were waited for; matrix products, arithmetic and copies ran while one was open for 1% of the time, Pallas kernels for 0%

profile of v7, /device:TPU:1, one launch (start us, length us, event | category | flops | bytes accessed | tf_op | source)
XLA Modules:
  0.0 135.9 jit_solution(14277940481165094735)
XLA Ops:
  0.7 4.0 %shard_map.100 = (bf16[2048,128]{1,0:T(8,128)(2,1)}, f32[64,128]{1,0:T(8,128)}) custom-call(s32[1]{0:T(128)S(6)} %copy.12.step, f32[32,32,128]{2,1,0:T(8,128)} %bitcast.28, f32[32,32,128]{2,1,0:T(8,128)} %bitcast.26, f32[32,32,128]{2,1,0:T(8,128)} %bitcast.25, bf16[1152,128]{1,0:T(8,128)(2,1)} %space_weight.1, f32[128,256]{1,0:T(8,128)} %map_far.1, ...), custom_call_target="tpu_custom_call" | custom-call | flops 301989888 | bytes 2556932 | tf_op jit(solution)/shard_map/pallas_call | solution.py:250
  4.7 0.0 copy-start.1
  4.7 0.0 copy-start.2
  4.7 0.0 copy-start.3
  4.7 22.2 %all-to-all-start = ((bf16[512,4,128]{2,1,0:T(4,128)(2,1)}), bf16[512,4,128]{2,1,0:T(4,128)(2,1)S(1)}, u32[]{:S(2)}, u32[]{:S(2)}) async-start(bf16[512,4,128]{2,1,0:T(4,128)(2,1)} %bitcast.27), calls=%async_computation | async-start | bytes 1048576 | tf_op jit(solution)/shard_map/all_to_all | solution.py:275
  26.9 1.3 dynamic-slice
  28.2 0.7 dynamic-update-slice
  28.9 21.8 %all-reduce.all_steps = s32[32]{0:T(128)S(1)} all-reduce(s32[32]{0:T(128)S(1)} %dynamic-update-slice), channel_id=1, replica_groups=mesh['tm_0'=4,'tm_1'=8,'frame'=16] {'tm_0','tm_1'}, use_global_device_ids=true, to_apply=%add | all-reduce | flops 32 | bytes 256
  50.7 0.0 all-to-all-done
  50.7 0.0 copy-done.1
  50.7 0.0 copy-done.2
  50.7 0.0 copy-done.3
  50.7 2.1 %shard_map.101 = (bf16[1024,128]{1,0:T(8,128)(2,1)S(1)}, f32[1024,128]{1,0:T(8,128)S(1)}) custom-call(s32[32]{0:T(128)S(1)} %all-reduce.all_steps, bf16[2048,128]{1,0:T(8,128)(2,1)S(1)} %bitcast.21, f32[64,128]{1,0:T(8,128)S(1)} %copy-done.1, bf16[128,384]{1,0:T(8,128)(2,1)S(1)} %copy-done.2, bf16[128,128]{1,0:T(8,128)(2,1)S(1)} %copy-done.3), custom_call_target="tpu_custom_call" | custom-call | flops 268435456 | bytes 1474688 | tf_op jit(solution)/shard_map/pallas_call | solution.py:250
  52.8 0.0 copy-start
  52.8 12.9 %all_to_all.20 = bf16[32,32,128]{2,1,0:T(8,128)(2,1)S(1)} all-to-all(bf16[32,32,128]{2,1,0:T(8,128)(2,1)S(1)} %bitcast.23), channel_id=1, replica_groups=mesh['tm_0'=4,'tm_1'=8,'frame'=16] {'tm_0','tm_1'}, dimensions={0} | all-to-all | bytes 524288 | tf_op jit(solution)/shard_map/all_to_all | solution.py:275
  65.7 0.2 shard_map.102
  65.9 7.5 %collective-permute-start = (bf16[32,16,128]{2,1,0:T(8,128)(2,1)S(1)}, bf16[32,16,128]{2,1,0:T(8,128)(2,1)S(1)}, u32[]{:S(2)}, u32[]{:S(2)}) collective-permute-start(bf16[32,16,128]{2,1,0:T(8,128)(2,1)S(1)} %get-tuple-element.17.inner), channel_id=1, source_target_pairs={{0,1},{1,0},{2,3},{3,2},{4,5},{5,4},{6,7},{7,6},{8,9},{9,8},{10,11... | collective-permute-start | bytes 393224 | tf_op jit(solution)/shard_map/ppermute | solution.py:339
  73.5 2.1 %collective-permute-start.1 = (bf16[32,16,128]{2,1,0:T(8,128)(2,1)S(1)}, bf16[32,16,128]{2,1,0:T(8,128)(2,1)S(1)}, u32[]{:S(2)}, u32[]{:S(2)}) collective-permute-start(bf16[32,16,128]{2,1,0:T(8,128)(2,1)S(1)} %get-tuple-element.18.outer), channel_id=1, source_target_pairs={{1,2},{2,1},{3,4},{4,3},{5,6},{6,5},{7,8},{8,7},{9,10},{10,9},{11,... | collective-permute-start | bytes 393224 | tf_op jit(solution)/shard_map/ppermute | solution.py:338
  75.6 0.0 collective-permute-done.from_core
  75.6 4.2 %collective-permute-done.1.from_chip = bf16[32,16,128]{2,1,0:T(8,128)(2,1)S(1)} collective-permute-done((bf16[32,16,128]{2,1,0:T(8,128)(2,1)S(1)}, bf16[32,16,128]{2,1,0:T(8,128)(2,1)S(1)}, u32[]{:S(2)}, u32[]{:S(2)}) %collective-permute-start.1) | collective-permute-done | bytes 131104 | tf_op jit(solution)/shard_map/ppermute | solution.py:338
  79.8 0.0 copy-done
  79.8 2.2 %shard_map.103 = bf16[32,2,16,128]{3,2,1,0:T(8,128)(2,1)S(1)} custom-call(s32[1]{0:T(128)S(6)} %copy.12.step, bf16[32,2,16,128]{3,2,1,0:T(8,128)(2,1)S(1)} %bitcast.20, bf16[32,16,128]{2,1,0:T(8,128)(2,1)S(1)} %get-tuple-element.17.inner, bf16[32,16,128]{2,1,0:T(8,128)(2,1)S(1)} %get-tuple-element.18.outer, ...), custom_call_target="tpu_custom_call" | custom-call | flops 570425344 | bytes 1507332 | tf_op jit(solution)/shard_map/pallas_call | solution.py:250
  82.0 13.9 %all_to_all.21 = bf16[32,32,128]{2,1,0:T(8,128)(2,1)S(1)} all-to-all(bf16[32,32,128]{2,1,0:T(8,128)(2,1)S(1)} %bitcast.22), channel_id=1, replica_groups=mesh['tm_0'=4,'tm_1'=8,'frame'=16] {'tm_0','tm_1'}, dimensions={0} | all-to-all | bytes 524288 | tf_op jit(solution)/shard_map/all_to_all | solution.py:275
  95.9 0.1 shard_map.104
  96.0 0.0 copy-start.4
  96.0 0.0 copy-start.5
  96.0 39.0 %all_to_all.22 = f32[512,2,128]{2,1,0:T(2,128)S(1)} all-to-all(f32[512,2,128]{2,1,0:T(2,128)S(1)} %bitcast.17), channel_id=1, replica_groups=mesh['tm_0'=4,'tm_1'=8,'frame'=16] {'tm_0','tm_1','frame'}, dimensions={0} | all-to-all | bytes 1048576 | tf_op jit(solution)/shard_map/all_to_all | solution.py:275
  135.0 0.0 copy-done.4
  135.0 0.0 copy-done.5
  135.0 0.9 bitcast_add_fusion
  (1 shorter events, 0.0 us)
Async XLA Ops:
  4.7 46.0 %copy-start.1 = (f32[64,128]{1,0:T(8,128)S(1)}, f32[64,128]{1,0:T(8,128)}, u32[]{:S(2)}) copy-start(f32[64,128]{1,0:T(8,128)} %get-tuple-element.15.params) | copy-start | bytes 98308
  4.7 46.0 %copy-start.2 = (bf16[128,384]{1,0:T(8,128)(2,1)S(1)}, bf16[128,384]{1,0:T(8,128)(2,1)}, u32[]{:S(2)}) copy-start(bf16[128,384]{1,0:T(8,128)(2,1)} %attention_weight.3) | copy-start | bytes 294916
  4.7 46.0 %copy-start.3 = (bf16[128,128]{1,0:T(8,128)(2,1)S(1)}, bf16[128,128]{1,0:T(8,128)(2,1)}, u32[]{:S(2)}) copy-start(bf16[128,128]{1,0:T(8,128)(2,1)} %output_weight.3) | copy-start | bytes 98308
  4.7 46.0 %all-to-all-start = ((bf16[512,4,128]{2,1,0:T(4,128)(2,1)}), bf16[512,4,128]{2,1,0:T(4,128)(2,1)S(1)}, u32[]{:S(2)}, u32[]{:S(2)}) async-start(bf16[512,4,128]{2,1,0:T(4,128)(2,1)} %bitcast.27), calls=%async_computation | async-start | bytes 1048576 | tf_op jit(solution)/shard_map/all_to_all | solution.py:275
  52.8 27.0 %copy-start = (bf16[1152,128]{1,0:T(8,128)(2,1)S(1)}, bf16[1152,128]{1,0:T(8,128)(2,1)}, u32[]{:S(2)}) copy-start(bf16[1152,128]{1,0:T(8,128)(2,1)} %space_weight.1) | copy-start | bytes 884740
  65.9 9.6 %collective-permute-start = (bf16[32,16,128]{2,1,0:T(8,128)(2,1)S(1)}, bf16[32,16,128]{2,1,0:T(8,128)(2,1)S(1)}, u32[]{:S(2)}, u32[]{:S(2)}) collective-permute-start(bf16[32,16,128]{2,1,0:T(8,128)(2,1)S(1)} %get-tuple-element.17.inner), channel_id=1, source_target_pairs={{0,1},{1,0},{2,3},{3,2},{4,5},{5,4},{6,7},{7,6},{8,9},{9,8},{10,11... | collective-permute-start | bytes 393224 | tf_op jit(solution)/shard_map/ppermute | solution.py:339
  73.5 6.3 %collective-permute-start.1 = (bf16[32,16,128]{2,1,0:T(8,128)(2,1)S(1)}, bf16[32,16,128]{2,1,0:T(8,128)(2,1)S(1)}, u32[]{:S(2)}, u32[]{:S(2)}) collective-permute-start(bf16[32,16,128]{2,1,0:T(8,128)(2,1)S(1)} %get-tuple-element.18.outer), channel_id=1, source_target_pairs={{1,2},{2,1},{3,4},{4,3},{5,6},{6,5},{7,8},{8,7},{9,10},{10,9},{11,... | collective-permute-start | bytes 393224 | tf_op jit(solution)/shard_map/ppermute | solution.py:338
  96.0 39.0 %copy-start.4 = (f32[1,32,32,128]{3,2,1,0:T(8,128)S(1)}, f32[1,32,32,128]{3,2,1,0:T(8,128)}, u32[]{:S(2)}) copy-start(f32[1,32,32,128]{3,2,1,0:T(8,128)} %param.10) | copy-start | bytes 1572868
  96.0 39.0 %copy-start.5 = (f32[1,1,32,32,128]{4,3,2,1,0:T(8,128)S(1)}, f32[1,1,32,32,128]{4,3,2,1,0:T(8,128)}, u32[]{:S(2)}) copy-start(f32[1,1,32,32,128]{4,3,2,1,0:T(8,128)} %param.12) | copy-start | bytes 1572868

commit v8 on v7

--- a/solution.py
+++ b/solution.py
@@ -154,7 +154,7 @@
 
 
 def owner_kernel(
-    all_steps, received, params, attention_weight, output_weight, states, noise_before,
+    all_steps, received, params, attention_weight, output_weight, states, rest_before, own_share,
     wide, drifts, *room,
 ):
     wide[...] = received[...].astype(F32)
@@ -166,18 +166,25 @@
         drifts[pl.ds(block * 128, 128), :] = load(block) + found
 
     attend(load, emit, params[48:49, :], attention_weight, output_weight, *room)
+    coefficients = [(0.5 + all_steps[step].astype(F32) / 1000.0) / math.sqrt(STEPS) for step in range(STEPS)]
+    here = lax.axis_index("tm_0") * lax.axis_size("tm_1") + lax.axis_index("tm_1")
+    shares, own = [], jnp.float32(0.0)
+    for step, coefficient in enumerate(coefficients):
+        shares.append(coefficient if step == 0 else shares[-1] + coefficient)
+        own = jnp.where(here == step, shares[-1], own)
+    own_share[...] = jnp.full((1, C), own, F32)
     for cell in range(2):
         tail = (STEPS - 1) * FRAMES * 4 + cell
-        state = wide[pl.ds(tail + 2, FRAMES, 4), :] + wide[pl.ds(tail, FRAMES, 4), :]
-        noises = jnp.zeros((FRAMES, C), F32)
+        begun = wide[pl.ds(tail + 2, FRAMES, 4), :] + wide[pl.ds(tail, FRAMES, 4), :]
+        state, noises = begun, jnp.zeros((FRAMES, C), F32)
         for step in range(STEPS):
-            states[pl.ds(step * 32 + cell * FRAMES, FRAMES), :] = state.astype(BF16)
-            noise_before[pl.ds(step * 32 + cell * FRAMES, FRAMES), :] = noises
+            rows = pl.ds(step * 32 + cell * FRAMES, FRAMES)
+            states[rows, :] = state.astype(BF16)
+            rest_before[rows, :] = noises - shares[step] * begun
             if step < STEPS - 1:
                 drawn = wide[pl.ds(step * FRAMES * 4 + 2 + cell, FRAMES, 4), :]
                 drift = drifts[pl.ds(cell * 512 + step * FRAMES, FRAMES), :]
-                coefficient = (0.5 + all_steps[step].astype(F32) / 1000.0) / math.sqrt(STEPS)
-                state = state + (coefficient * drift + drawn)
+                state = state + (coefficients[step] * drift + drawn)
                 noises = noises + drawn
 
 
@@ -235,13 +242,14 @@
     attend(load, emit, params[48:49, :], attention_weight, output_weight, *room)
 
 
-def sum_kernel(received, noise_before, out):
+def sum_kernel(received, rest_before, out, turned):
     for cell in range(2):
         total = jnp.zeros((FRAMES, C), F32)
         for step in range(STEPS):
             rows = pl.ds(step * 32 + cell * FRAMES, FRAMES)
             total = total + received[rows, :].astype(F32)
-            out[pl.ds(step * 32 + cell, FRAMES, 2), :] = total + noise_before[rows, :]
+            turned[pl.ds(step * 32 + cell, FRAMES, 2), :] = total + rest_before[rows, :]
+    out[...] = turned[...].astype(BF16)
 
 
 def call(kernel, outs, operands, scratch, flops, spaces=(), grant=16):
@@ -316,9 +324,9 @@
     )
     received = exchange(sent.reshape(512, 4, C), ALL).reshape(2 * CELLS, C)
     all_steps = lax.all_gather(timesteps, TM, tiled=True)
-    states, noise_before = call(
+    states, rest_before, own_share = call(
         owner_kernel,
-        [struct((CELLS, C), BF16), struct((CELLS, C), F32)],
+        [struct((CELLS, C), BF16), struct((CELLS, C), F32), struct((1, C), F32)],
         (all_steps, received, params, attention_weight, output_weight),
         [pltpu.VMEM((2 * CELLS, C), F32), pltpu.VMEM((CELLS, C), F32), *attention_room()],
         2 * CELLS * 8 * C * C,
@@ -349,9 +357,16 @@
         (SMEM,),
     )
     drifts = exchange(drifts.reshape(32, 32, C), TM).reshape(CELLS, C)
-    (sums,) = call(sum_kernel, [struct((CELLS, C), F32)], (drifts, noise_before), [], 2 * CELLS * C)
-    sums = exchange(sums.reshape(512, 2, C), ALL).reshape(SIDE, SIDE, C)
-    return (start + (sums + own_scale * noise))[None, None]
+    (rest,) = call(
+        sum_kernel,
+        [struct((CELLS, C), BF16)],
+        (drifts, rest_before),
+        [pltpu.VMEM((CELLS, C), F32)],
+        2 * CELLS * C,
+    )
+    rest = exchange(rest.reshape(512, 2, C), ALL).reshape(SIDE, SIDE, C).astype(F32)
+    advanced = start + ((own_share * start + rest) + own_scale * noise)
+    return advanced[None, None]
 
 
 def solution(mesh):

time: 136 us -> 131 us (0.963)
  blocking collectives: 87.6 us -> 82.5 us
    all_to_all x3, blocking collectives: 65.8 us -> 60.7 us  [exchange(): return lax.all_to_all(array, axes, 0, 0, tiled=True)]
  transfers between devices with their start and end apart: 3 -> 3, of which waited for: 1 -> 1; matrix products, arithmetic and copies ran while one was open for 1% -> 2% of each run, Pallas kernels for 0% -> 0%
where the time goes in v8:
time: 131 us
  blocking collectives  82.5 us (63%)
  starting transfers between devices  31.8 us (24%)
  Pallas kernels  8.62 us (7%)
  waiting for transfers between devices  4.19 us (3%)
  local copies, waits for them, and re-layouts  2.07 us (2%)
    all_to_all x3, blocking collectives, exchange(): return lax.all_to_all(array, axes, 0, 0, tiled=True)  60.7 us
    all_to_all x1, starting transfers between devices, exchange(): return lax.all_to_all(array, axes, 0, 0, tiled=True)  22.2 us
    unnamed x1, blocking collectives  21.8 us
    pallas_call x5, Pallas kernels, call(): pl.pallas_call(kernel, out_shape=outs, in_specs=specs, out_specs=[VMEM] *...  8.62 us
    ppermute x1, starting transfers between devices, shards(): from_core = lax.ppermute(inner, 'frame', cores)  7.54 us
    ppermute x1, waiting for transfers between devices, shards(): from_chip = lax.ppermute(outer, 'frame', chips)  4.19 us
  transfers between devices with their start and end apart: 3, of which 1 were waited for; matrix products, arithmetic and copies ran while one was open for 2% of the time, Pallas kernels for 0%

profile of v8, /device:TPU:1, one launch (start us, length us, event | category | flops | bytes accessed | tf_op | source)
XLA Modules:
  0.0 130.9 jit_solution(3115566705966255357)
XLA Ops:
  0.7 4.0 %shard_map.100 = (bf16[2048,128]{1,0:T(8,128)(2,1)}, f32[64,128]{1,0:T(8,128)}) custom-call(s32[1]{0:T(128)S(6)} %copy.12.step, f32[32,32,128]{2,1,0:T(8,128)} %bitcast.34, f32[32,32,128]{2,1,0:T(8,128)} %bitcast.30, f32[32,32,128]{2,1,0:T(8,128)} %bitcast.31, bf16[1152,128]{1,0:T(8,128)(2,1)} %space_weight.1, f32[128,256]{1,0:T(8,128)} %map_far.1, ...), custom_call_target="tpu_custom_call" | custom-call | flops 301989888 | bytes 2556932 | tf_op jit(solution)/shard_map/pallas_call | solution.py:258
  4.7 0.0 copy-start.1
  4.7 0.0 copy-start.2
  4.7 0.0 copy-start.3
  4.7 22.2 %all-to-all-start = ((bf16[512,4,128]{2,1,0:T(4,128)(2,1)}), bf16[512,4,128]{2,1,0:T(4,128)(2,1)S(1)}, u32[]{:S(2)}, u32[]{:S(2)}) async-start(bf16[512,4,128]{2,1,0:T(4,128)(2,1)} %bitcast.33), calls=%async_computation | async-start | bytes 1048576 | tf_op jit(solution)/shard_map/all_to_all | solution.py:283
  26.9 1.3 dynamic-slice
  28.2 0.7 dynamic-update-slice
  28.9 21.8 %all-reduce.all_steps = s32[32]{0:T(128)S(1)} all-reduce(s32[32]{0:T(128)S(1)} %dynamic-update-slice), channel_id=1, replica_groups=mesh['tm_0'=4,'tm_1'=8,'frame'=16] {'tm_0','tm_1'}, use_global_device_ids=true, to_apply=%add | all-reduce | flops 32 | bytes 256
  50.7 0.0 all-to-all-done
  50.7 0.0 copy-done.1
  50.7 0.0 copy-done.2
  50.7 0.0 copy-done.3
  50.7 2.1 %shard_map.101 = (bf16[1024,128]{1,0:T(8,128)(2,1)S(1)}, f32[1024,128]{1,0:T(8,128)S(1)}, f32[1,128]{1,0:T(1,128)S(1)}) custom-call(s32[32]{0:T(128)S(1)} %all-reduce.all_steps, bf16[2048,128]{1,0:T(8,128)(2,1)S(1)} %bitcast.26, f32[64,128]{1,0:T(8,128)S(1)} %copy-done.1, bf16[128,384]{1,0:T(8,128)(2,1)S(1)} %copy-done.2, bf16[128,128]{1,0:T(8,128)(2,1)S(1)} %copy-done.3), custom_call_target="tpu_custom_call" | custom-call | flops 268435456 | bytes 1475200 | tf_op jit(solution)/shard_map/pallas_call | solution.py:258
  52.8 0.0 copy-start
  52.8 12.9 %all_to_all.20 = bf16[32,32,128]{2,1,0:T(8,128)(2,1)S(1)} all-to-all(bf16[32,32,128]{2,1,0:T(8,128)(2,1)S(1)} %bitcast.28), channel_id=1, replica_groups=mesh['tm_0'=4,'tm_1'=8,'frame'=16] {'tm_0','tm_1'}, dimensions={0} | all-to-all | bytes 524288 | tf_op jit(solution)/shard_map/all_to_all | solution.py:283
  65.7 0.2 shard_map.102
  65.9 7.5 %collective-permute-start = (bf16[32,16,128]{2,1,0:T(8,128)(2,1)S(1)}, bf16[32,16,128]{2,1,0:T(8,128)(2,1)S(1)}, u32[]{:S(2)}, u32[]{:S(2)}) collective-permute-start(bf16[32,16,128]{2,1,0:T(8,128)(2,1)S(1)} %get-tuple-element.19.inner), channel_id=1, source_target_pairs={{0,1},{1,0},{2,3},{3,2},{4,5},{5,4},{6,7},{7,6},{8,9},{9,8},{10,11... | collective-permute-start | bytes 393224 | tf_op jit(solution)/shard_map/ppermute | solution.py:347
  73.5 2.1 %collective-permute-start.1 = (bf16[32,16,128]{2,1,0:T(8,128)(2,1)S(1)}, bf16[32,16,128]{2,1,0:T(8,128)(2,1)S(1)}, u32[]{:S(2)}, u32[]{:S(2)}) collective-permute-start(bf16[32,16,128]{2,1,0:T(8,128)(2,1)S(1)} %get-tuple-element.20.outer), channel_id=1, source_target_pairs={{1,2},{2,1},{3,4},{4,3},{5,6},{6,5},{7,8},{8,7},{9,10},{10,9},{11,... | collective-permute-start | bytes 393224 | tf_op jit(solution)/shard_map/ppermute | solution.py:346
  75.6 0.0 collective-permute-done.from_core
  75.6 4.2 %collective-permute-done.1.from_chip = bf16[32,16,128]{2,1,0:T(8,128)(2,1)S(1)} collective-permute-done((bf16[32,16,128]{2,1,0:T(8,128)(2,1)S(1)}, bf16[32,16,128]{2,1,0:T(8,128)(2,1)S(1)}, u32[]{:S(2)}, u32[]{:S(2)}) %collective-permute-start.1) | collective-permute-done | bytes 131104 | tf_op jit(solution)/shard_map/ppermute | solution.py:346
  79.8 0.0 copy-done
  79.8 2.2 %shard_map.103 = bf16[32,2,16,128]{3,2,1,0:T(8,128)(2,1)S(1)} custom-call(s32[1]{0:T(128)S(6)} %copy.12.step, bf16[32,2,16,128]{3,2,1,0:T(8,128)(2,1)S(1)} %bitcast.23, bf16[32,16,128]{2,1,0:T(8,128)(2,1)S(1)} %get-tuple-element.19.inner, bf16[32,16,128]{2,1,0:T(8,128)(2,1)S(1)} %get-tuple-element.20.outer, ...), custom_call_target="tpu_custom_call" | custom-call | flops 570425344 | bytes 1507332 | tf_op jit(solution)/shard_map/pallas_call | solution.py:258
  82.0 13.9 %all_to_all.21 = bf16[32,32,128]{2,1,0:T(8,128)(2,1)S(1)} all-to-all(bf16[32,32,128]{2,1,0:T(8,128)(2,1)S(1)} %bitcast.27), channel_id=1, replica_groups=mesh['tm_0'=4,'tm_1'=8,'frame'=16] {'tm_0','tm_1'}, dimensions={0} | all-to-all | bytes 524288 | tf_op jit(solution)/shard_map/all_to_all | solution.py:283
  95.9 0.0 copy-start.5
  95.9 0.1 shard_map.104
  96.0 0.0 copy-start.4
  96.0 34.0 %all_to_all.22 = bf16[512,2,128]{2,1,0:T(2,128)(2,1)S(1)} all-to-all(bf16[512,2,128]{2,1,0:T(2,128)(2,1)S(1)} %bitcast.25), channel_id=1, replica_groups=mesh['tm_0'=4,'tm_1'=8,'frame'=16] {'tm_0','tm_1','frame'}, dimensions={0} | all-to-all | bytes 524288 | tf_op jit(solution)/shard_map/all_to_all | solution.py:283
  130.0 0.0 copy-done.5
  130.0 0.0 copy-done.4
  130.0 0.9 fusion.1
  (1 shorter events, 0.0 us)
Async XLA Ops:
  4.7 46.0 %copy-start.1 = (f32[64,128]{1,0:T(8,128)S(1)}, f32[64,128]{1,0:T(8,128)}, u32[]{:S(2)}) copy-start(f32[64,128]{1,0:T(8,128)} %get-tuple-element.16.params) | copy-start | bytes 98308
  4.7 46.0 %copy-start.2 = (bf16[128,384]{1,0:T(8,128)(2,1)S(1)}, bf16[128,384]{1,0:T(8,128)(2,1)}, u32[]{:S(2)}) copy-start(bf16[128,384]{1,0:T(8,128)(2,1)} %attention_weight.3) | copy-start | bytes 294916
  4.7 46.0 %copy-start.3 = (bf16[128,128]{1,0:T(8,128)(2,1)S(1)}, bf16[128,128]{1,0:T(8,128)(2,1)}, u32[]{:S(2)}) copy-start(bf16[128,128]{1,0:T(8,128)(2,1)} %output_weight.3) | copy-start | bytes 98308
  4.7 46.0 %all-to-all-start = ((bf16[512,4,128]{2,1,0:T(4,128)(2,1)}), bf16[512,4,128]{2,1,0:T(4,128)(2,1)S(1)}, u32[]{:S(2)}, u32[]{:S(2)}) async-start(bf16[512,4,128]{2,1,0:T(4,128)(2,1)} %bitcast.33), calls=%async_computation | async-start | bytes 1048576 | tf_op jit(solution)/shard_map/all_to_all | solution.py:283
  52.8 27.0 %copy-start = (bf16[1152,128]{1,0:T(8,128)(2,1)S(1)}, bf16[1152,128]{1,0:T(8,128)(2,1)}, u32[]{:S(2)}) copy-start(bf16[1152,128]{1,0:T(8,128)(2,1)} %space_weight.1) | copy-start | bytes 884740
  65.9 9.6 %collective-permute-start = (bf16[32,16,128]{2,1,0:T(8,128)(2,1)S(1)}, bf16[32,16,128]{2,1,0:T(8,128)(2,1)S(1)}, u32[]{:S(2)}, u32[]{:S(2)}) collective-permute-start(bf16[32,16,128]{2,1,0:T(8,128)(2,1)S(1)} %get-tuple-element.19.inner), channel_id=1, source_target_pairs={{0,1},{1,0},{2,3},{3,2},{4,5},{5,4},{6,7},{7,6},{8,9},{9,8},{10,11... | collective-permute-start | bytes 393224 | tf_op jit(solution)/shard_map/ppermute | solution.py:347
  73.5 6.3 %collective-permute-start.1 = (bf16[32,16,128]{2,1,0:T(8,128)(2,1)S(1)}, bf16[32,16,128]{2,1,0:T(8,128)(2,1)S(1)}, u32[]{:S(2)}, u32[]{:S(2)}) collective-permute-start(bf16[32,16,128]{2,1,0:T(8,128)(2,1)S(1)} %get-tuple-element.20.outer), channel_id=1, source_target_pairs={{1,2},{2,1},{3,4},{4,3},{5,6},{6,5},{7,8},{8,7},{9,10},{10,9},{11,... | collective-permute-start | bytes 393224 | tf_op jit(solution)/shard_map/ppermute | solution.py:346
  95.9 34.1 %copy-start.5 = (f32[1,32,32,128]{3,2,1,0:T(8,128)S(1)}, f32[1,32,32,128]{3,2,1,0:T(8,128)}, u32[]{:S(2)}) copy-start(f32[1,32,32,128]{3,2,1,0:T(8,128)} %param.10) | copy-start | bytes 1572868
  96.0 34.0 %copy-start.4 = (f32[1,1,32,32,128]{4,3,2,1,0:T(8,128)S(1)}, f32[1,1,32,32,128]{4,3,2,1,0:T(8,128)}, u32[]{:S(2)}) copy-start(f32[1,1,32,32,128]{4,3,2,1,0:T(8,128)} %param.12) | copy-start | bytes 1572868

commit v9 on v8

--- a/solution.py
+++ b/solution.py
@@ -80,7 +80,7 @@
 
 
 def first_kernel(
-    step, guess_far, noise_far, start_far, weight_far, map_far, gain_s, gain_a, out, params,
+    step, guess_far, noise_far, start_far, weight_far, map_far, gain_s, gain_a, out, params, steps_row,
     guess, noise, start, space_weight, time_weight, padded, mixed, drawn, packed, sems,
 ):
     copies = [
@@ -88,7 +88,7 @@
         for i, (far, near) in enumerate(
             (
                 (map_far, time_weight),
-                (guess_far, guess),
+                *((guess_far.at[pl.ds(i * 8, 8)], guess.at[pl.ds(i * 8, 8)]) for i in range(4)),
                 (weight_far, space_weight),
                 (noise_far, noise),
                 (start_far, start),
@@ -112,8 +112,8 @@
     gain = gain_s[...]
     for i, row in enumerate((scaling, offset, gain, gain_a[...])):
         params[pl.ds(i * 16, 16), :] = jnp.broadcast_to(row, (16, C))
-    copies[1].wait()
     for block in range(4):
+        copies[1 + block].wait()
         rows = pl.ds(block * 8, 8)
         state = guess[rows]
         normed = unit(state, gain) * scaling + offset
@@ -123,7 +123,7 @@
         padded[at, :, 0:C] = left.astype(BF16)
         padded[at, :, C : 2 * C] = normed.astype(BF16)
         padded[at, :, 2 * C : 3 * C] = right.astype(BF16)
-    for copy in copies[2:]:
+    for copy in copies[5:]:
         copy.wait()
     total = None
     for shift in range(3):
@@ -135,7 +135,9 @@
     mixed[...] = total
     time_value, coefficient = times(step)
     scale = time_value * coefficient
-    last = lax.axis_index("tm_0") * lax.axis_size("tm_1") + lax.axis_index("tm_1") == STEPS - 1
+    place = lax.axis_index("tm_0") * lax.axis_size("tm_1") + lax.axis_index("tm_1")
+    last = place == STEPS - 1
+    steps_row[...] = jnp.where(lax.broadcasted_iota(jnp.int32, (1, C), 1) == place, step[0], 0)
     for block in range(8):
         rows = pl.ds(block * 128, 128)
         band = pl.ds(block * 4, 4)
@@ -166,7 +168,7 @@
         drifts[pl.ds(block * 128, 128), :] = load(block) + found
 
     attend(load, emit, params[48:49, :], attention_weight, output_weight, *room)
-    coefficients = [(0.5 + all_steps[step].astype(F32) / 1000.0) / math.sqrt(STEPS) for step in range(STEPS)]
+    coefficients = [(0.5 + all_steps[0, step].astype(F32) / 1000.0) / math.sqrt(STEPS) for step in range(STEPS)]
     here = lax.axis_index("tm_0") * lax.axis_size("tm_1") + lax.axis_index("tm_1")
     shares, own = [], jnp.float32(0.0)
     for step, coefficient in enumerate(coefficients):
@@ -299,9 +301,9 @@
     time_value = timesteps[0].astype(F32) / 1000.0
     own_scale = time_value * (0.5 + time_value) / math.sqrt(STEPS)
     gain_space, own_scale = lax.optimization_barrier((gain_space, own_scale))
-    sent, params = call(
+    sent, params, steps_row = call(
         first_kernel,
-        [struct((2 * CELLS, C), BF16), struct((64, C), F32)],
+        [struct((2 * CELLS, C), BF16), struct((64, C), F32), struct((1, C), jnp.int32)],
         (
             timesteps, guess, noise, start, space_weight, time_weight,
             gain_space[None, :], gain_attention[None, :],
@@ -316,14 +318,14 @@
             pltpu.VMEM((CELLS, C), F32),
             pltpu.VMEM((CELLS, C), F32),
             pltpu.VMEM((2 * CELLS, C), F32),
-            pltpu.SemaphoreType.DMA((5,)),
+            pltpu.SemaphoreType.DMA((8,)),
         ],
         2 * CELLS * 9 * C * C,
         (SMEM, FAR, FAR, FAR, FAR, FAR),
         62,
     )
     received = exchange(sent.reshape(512, 4, C), ALL).reshape(2 * CELLS, C)
-    all_steps = lax.all_gather(timesteps, TM, tiled=True)
+    all_steps = lax.psum(steps_row, TM)
     states, rest_before, own_share = call(
         owner_kernel,
         [struct((CELLS, C), BF16), struct((CELLS, C), F32), struct((1, C), F32)],
@@ -343,8 +345,8 @@
     count = lax.axis_size("frame")
     chips = [(k + i, k + 1 - i) for k in range(1, count - 1, 2) for i in range(2)]
     cores = [(k, k ^ 1) for k in range(count)]
+    from_core = lax.ppermute(inner, "frame", cores)
     from_chip = lax.ppermute(outer, "frame", chips)
-    from_core = lax.ppermute(inner, "frame", cores)
     (drifts,) = call(
         second_kernel,
         [struct((SIDE, 2, FRAMES, C), BF16)],

time: 131 us -> 132 us (level)
  blocking collectives: 82.5 us -> 84.9 us
  local copies, waits for them, and re-layouts: 2.07 us -> 0.63 us
    psum x0 -> x1, blocking collectives: none -> 21.8 us  [shards(): all_steps = lax.psum(steps_row, TM)]
    unnamed x1 -> x0, blocking collectives: 21.8 us -> none
    all_to_all x3, blocking collectives: 60.7 us -> 63 us  [exchange(): return lax.all_to_all(array, axes, 0, 0, tiled=True)]
    unnamed x15 -> x14, local copies, waits for them, and re-layouts: 2.07 us -> 0.63 us
  transfers between devices with their start and end apart: 3 -> 3, of which waited for: 1 -> 1; matrix products, arithmetic and copies ran while one was open for 2% -> 0% of each run, Pallas kernels for 0% -> 0%
where the time goes in v9:
time: 132 us; the launch traced here: 131 us
  blocking collectives  84.9 us (64%)
  starting transfers between devices  30.9 us (23%)
  Pallas kernels  8.92 us (7%)
  waiting for transfers between devices  4.12 us (3%)
    all_to_all x3, blocking collectives, exchange(): return lax.all_to_all(array, axes, 0, 0, tiled=True)  63 us
    all_to_all x1, starting transfers between devices, exchange(): return lax.all_to_all(array, axes, 0, 0, tiled=True)  22.2 us
    psum x1, blocking collectives, shards(): all_steps = lax.psum(steps_row, TM)  21.8 us
    pallas_call x5, Pallas kernels, call(): pl.pallas_call(kernel, out_shape=outs, in_specs=specs, out_specs=[VMEM] *...  8.92 us
    ppermute x1, starting transfers between devices, shards(): from_core = lax.ppermute(inner, 'frame', cores)  6.61 us
    ppermute x1, waiting for transfers between devices, shards(): from_chip = lax.ppermute(outer, 'frame', chips)  4.11 us
  transfers between devices with their start and end apart: 3, of which 1 were waited for; matrix products, arithmetic and copies ran while one was open for 0% of the time, Pallas kernels for 0%

profile of v9, /device:TPU:1, one launch (start us, length us, event | category | flops | bytes accessed | tf_op | source)
XLA Modules:
  0.0 131.2 jit_solution(4496088758626751489)
XLA Ops:
  0.7 4.3 %shard_map.100 = (bf16[2048,128]{1,0:T(8,128)(2,1)}, f32[64,128]{1,0:T(8,128)}, s32[1,128]{1,0:T(1,128)}) custom-call(s32[1]{0:T(128)S(6)} %copy.11.step, f32[32,32,128]{2,1,0:T(8,128)} %bitcast.33, f32[32,32,128]{2,1,0:T(8,128)} %bitcast.29, f32[32,32,128]{2,1,0:T(8,128)} %bitcast.30, bf16[1152,128]{1,0:T(8,128)(2,1)} %space_weight.1, f32[128,256]{1,0:T(8,128)} %map_far.1, ...), custom_call_target="tpu_custom_call" | custom-call | flops 301989888 | bytes 2557444 | tf_op jit(solution)/shard_map/pallas_call | solution.py:260
  5.0 0.0 copy-start.1
  5.0 0.0 copy-start.2
  5.0 0.0 copy-start.3
  5.0 22.2 %all-to-all-start = ((bf16[512,4,128]{2,1,0:T(4,128)(2,1)}), bf16[512,4,128]{2,1,0:T(4,128)(2,1)S(1)}, u32[]{:S(2)}, u32[]{:S(2)}) async-start(bf16[512,4,128]{2,1,0:T(4,128)(2,1)} %bitcast.32), calls=%async_computation | async-start | bytes 1048576 | tf_op jit(solution)/shard_map/all_to_all | solution.py:285
  27.2 0.0 copy-start.6
  27.2 0.6 copy-done.6
  27.8 21.8 %psum.7.all_steps = s32[1,128]{1,0:T(1,128)S(1)} all-reduce(s32[1,128]{1,0:T(1,128)S(1)} %copy-done.6), channel_id=1, replica_groups=mesh['tm_0'=4,'tm_1'=8,'frame'=16] {'tm_0','tm_1'}, use_global_device_ids=true, to_apply=%region_0.0 | all-reduce | flops 128 | bytes 1024 | tf_op jit(solution)/shard_map/psum | solution.py:328
  49.6 0.0 all-to-all-done
  49.6 0.0 copy-done.1
  49.6 0.0 copy-done.2
  49.6 0.0 copy-done.3
  49.6 2.1 %shard_map.101 = (bf16[1024,128]{1,0:T(8,128)(2,1)S(1)}, f32[1024,128]{1,0:T(8,128)S(1)}, f32[1,128]{1,0:T(1,128)S(1)}) custom-call(s32[1,128]{1,0:T(1,128)S(1)} %psum.7.all_steps, bf16[2048,128]{1,0:T(8,128)(2,1)S(1)} %bitcast.25, f32[64,128]{1,0:T(8,128)S(1)} %copy-done.1, bf16[128,384]{1,0:T(8,128)(2,1)S(1)} %copy-done.2, bf16[128,128]{1,0:T(8,128)(2,1)S(1)} %copy-done.3), custom_call_target="tpu_custom_call" | custom-call | flops 268435456 | bytes 1475584 | tf_op jit(solution)/shard_map/pallas_call | solution.py:260
  51.7 0.0 copy-start
  51.7 14.3 %all_to_all.20 = bf16[32,32,128]{2,1,0:T(8,128)(2,1)S(1)} all-to-all(bf16[32,32,128]{2,1,0:T(8,128)(2,1)S(1)} %bitcast.27), channel_id=1, replica_groups=mesh['tm_0'=4,'tm_1'=8,'frame'=16] {'tm_0','tm_1'}, dimensions={0} | all-to-all | bytes 524288 | tf_op jit(solution)/shard_map/all_to_all | solution.py:285
  66.0 0.2 shard_map.102
  66.2 6.6 %collective-permute-start = (bf16[32,16,128]{2,1,0:T(8,128)(2,1)S(1)}, bf16[32,16,128]{2,1,0:T(8,128)(2,1)S(1)}, u32[]{:S(2)}, u32[]{:S(2)}) collective-permute-start(bf16[32,16,128]{2,1,0:T(8,128)(2,1)S(1)} %get-tuple-element.21.inner), channel_id=1, source_target_pairs={{0,1},{1,0},{2,3},{3,2},{4,5},{5,4},{6,7},{7,6},{8,9},{9,8},{10,11... | collective-permute-start | bytes 393224 | tf_op jit(solution)/shard_map/ppermute | solution.py:348
  72.8 2.2 %collective-permute-start.1 = (bf16[32,16,128]{2,1,0:T(8,128)(2,1)S(1)}, bf16[32,16,128]{2,1,0:T(8,128)(2,1)S(1)}, u32[]{:S(2)}, u32[]{:S(2)}) collective-permute-start(bf16[32,16,128]{2,1,0:T(8,128)(2,1)S(1)} %get-tuple-element.22.outer), channel_id=1, source_target_pairs={{1,2},{2,1},{3,4},{4,3},{5,6},{6,5},{7,8},{8,7},{9,10},{10,9},{11,... | collective-permute-start | bytes 393224 | tf_op jit(solution)/shard_map/ppermute | solution.py:349
  75.0 0.0 collective-permute-done.from_core
  75.0 4.1 %collective-permute-done.1.from_chip = bf16[32,16,128]{2,1,0:T(8,128)(2,1)S(1)} collective-permute-done((bf16[32,16,128]{2,1,0:T(8,128)(2,1)S(1)}, bf16[32,16,128]{2,1,0:T(8,128)(2,1)S(1)}, u32[]{:S(2)}, u32[]{:S(2)}) %collective-permute-start.1) | collective-permute-done | bytes 131104 | tf_op jit(solution)/shard_map/ppermute | solution.py:349
  79.1 0.0 copy-done
  79.1 2.2 %shard_map.103 = bf16[32,2,16,128]{3,2,1,0:T(8,128)(2,1)S(1)} custom-call(s32[1]{0:T(128)S(6)} %copy.11.step, bf16[32,2,16,128]{3,2,1,0:T(8,128)(2,1)S(1)} %bitcast.22, bf16[32,16,128]{2,1,0:T(8,128)(2,1)S(1)} %get-tuple-element.21.inner, bf16[32,16,128]{2,1,0:T(8,128)(2,1)S(1)} %get-tuple-element.22.outer, ...), custom_call_target="tpu_custom_call" | custom-call | flops 570425344 | bytes 1507332 | tf_op jit(solution)/shard_map/pallas_call | solution.py:260
  81.4 13.8 %all_to_all.21 = bf16[32,32,128]{2,1,0:T(8,128)(2,1)S(1)} all-to-all(bf16[32,32,128]{2,1,0:T(8,128)(2,1)S(1)} %bitcast.26), channel_id=1, replica_groups=mesh['tm_0'=4,'tm_1'=8,'frame'=16] {'tm_0','tm_1'}, dimensions={0} | all-to-all | bytes 524288 | tf_op jit(solution)/shard_map/all_to_all | solution.py:285
  95.2 0.0 copy-start.5
  95.2 0.1 shard_map.104
  95.3 0.0 copy-start.4
  95.3 35.0 %all_to_all.22 = bf16[512,2,128]{2,1,0:T(2,128)(2,1)S(1)} all-to-all(bf16[512,2,128]{2,1,0:T(2,128)(2,1)S(1)} %bitcast.24), channel_id=1, replica_groups=mesh['tm_0'=4,'tm_1'=8,'frame'=16] {'tm_0','tm_1','frame'}, dimensions={0} | all-to-all | bytes 524288 | tf_op jit(solution)/shard_map/all_to_all | solution.py:285
  130.3 0.0 copy-done.5
  130.3 0.0 copy-done.4
  130.3 0.9 fusion.1
Async XLA Ops:
  5.0 44.7 %copy-start.1 = (f32[64,128]{1,0:T(8,128)S(1)}, f32[64,128]{1,0:T(8,128)}, u32[]{:S(2)}) copy-start(f32[64,128]{1,0:T(8,128)} %get-tuple-element.18.params) | copy-start | bytes 98308
  5.0 44.6 %copy-start.2 = (bf16[128,384]{1,0:T(8,128)(2,1)S(1)}, bf16[128,384]{1,0:T(8,128)(2,1)}, u32[]{:S(2)}) copy-start(bf16[128,384]{1,0:T(8,128)(2,1)} %attention_weight.3) | copy-start | bytes 294916
  5.0 44.6 %copy-start.3 = (bf16[128,128]{1,0:T(8,128)(2,1)S(1)}, bf16[128,128]{1,0:T(8,128)(2,1)}, u32[]{:S(2)}) copy-start(bf16[128,128]{1,0:T(8,128)(2,1)} %output_weight.3) | copy-start | bytes 98308
  5.0 44.6 %all-to-all-start = ((bf16[512,4,128]{2,1,0:T(4,128)(2,1)}), bf16[512,4,128]{2,1,0:T(4,128)(2,1)S(1)}, u32[]{:S(2)}, u32[]{:S(2)}) async-start(bf16[512,4,128]{2,1,0:T(4,128)(2,1)} %bitcast.32), calls=%async_computation | async-start | bytes 1048576 | tf_op jit(solution)/shard_map/all_to_all | solution.py:285
  27.2 0.6 copy-start.6
  51.7 27.4 %copy-start = (bf16[1152,128]{1,0:T(8,128)(2,1)S(1)}, bf16[1152,128]{1,0:T(8,128)(2,1)}, u32[]{:S(2)}) copy-start(bf16[1152,128]{1,0:T(8,128)(2,1)} %space_weight.1) | copy-start | bytes 884740
  66.2 8.8 %collective-permute-start = (bf16[32,16,128]{2,1,0:T(8,128)(2,1)S(1)}, bf16[32,16,128]{2,1,0:T(8,128)(2,1)S(1)}, u32[]{:S(2)}, u32[]{:S(2)}) collective-permute-start(bf16[32,16,128]{2,1,0:T(8,128)(2,1)S(1)} %get-tuple-element.21.inner), channel_id=1, source_target_pairs={{0,1},{1,0},{2,3},{3,2},{4,5},{5,4},{6,7},{7,6},{8,9},{9,8},{10,11... | collective-permute-start | bytes 393224 | tf_op jit(solution)/shard_map/ppermute | solution.py:348
  72.8 6.3 %collective-permute-start.1 = (bf16[32,16,128]{2,1,0:T(8,128)(2,1)S(1)}, bf16[32,16,128]{2,1,0:T(8,128)(2,1)S(1)}, u32[]{:S(2)}, u32[]{:S(2)}) collective-permute-start(bf16[32,16,128]{2,1,0:T(8,128)(2,1)S(1)} %get-tuple-element.22.outer), channel_id=1, source_target_pairs={{1,2},{2,1},{3,4},{4,3},{5,6},{6,5},{7,8},{8,7},{9,10},{10,9},{11,... | collective-permute-start | bytes 393224 | tf_op jit(solution)/shard_map/ppermute | solution.py:349
  95.2 35.1 %copy-start.5 = (f32[1,32,32,128]{3,2,1,0:T(8,128)S(1)}, f32[1,32,32,128]{3,2,1,0:T(8,128)}, u32[]{:S(2)}) copy-start(f32[1,32,32,128]{3,2,1,0:T(8,128)} %param.10) | copy-start | bytes 1572868
  95.3 35.0 %copy-start.4 = (f32[1,1,32,32,128]{4,3,2,1,0:T(8,128)S(1)}, f32[1,1,32,32,128]{4,3,2,1,0:T(8,128)}, u32[]{:S(2)}) copy-start(f32[1,1,32,32,128]{4,3,2,1,0:T(8,128)} %param.12) | copy-start | bytes 1572868
